TPU v7x, 512 devices: a whole 4x8x8 slice. The times are simulated.
512 devices in a mesh: row: 64 (over y, z), col: 8 (over x, core).
Axes of the slice: x: 4, y: 8, z: 8, core: 2. Of those that a mesh axis runs over, the one named last changes fastest.
Arguments:
- object_field: float32 [2, 16384, 2048], P(None, 'row', 'col'), may hold values from -6 to 6
- probe_field: float32 [2, 256, 256], replicated, may hold values from -6 to 6
- amplitudes: float32 [128, 2048, 256], P('row', 'col'), may hold values from 0 to 4
- offsets: int32 [64, 8, 2, 2], P('row', 'col'), may hold values from 0 to 128, as said below
- counts: int32 [64, 8], P('row', 'col'), may hold values from 1 to 2
Outputs:
- object_out: float32 [2, 16384, 2048], P(None, 'row', 'col')
- probe_out: float32 [2, 256, 256], replicated
Inputs may be any that keep to these rules, and one draw needn't show every extreme that they name: `offsets`: slots from counts[r, c] on are padding and hold no window.
All inputs are finite; a program needn't handle non-finite values.
Results may differ from a plain program's by a relative error of at most 0.0003.
Values sent between devices are 32-bit elements; how exact they have to be, the bound alone decides.
No kernel may reach another device: no remote copies, remote signals or barrier semaphores. Data moves between devices by JAX's collectives and lax.ppermute only.
A program may use at most 64 MiB of HBM per device.

v0:
```python
import math

import jax
import jax.numpy as jnp
from jax import lax
from jax.sharding import PartitionSpec as P

HALO = 128
OUTER = 2


smooth_floor = 0.5
object_step = 0.5
tiny_value = 1e-06


def shifted(value, axis, by):
    length = lax.axis_size(axis)
    pairs = [(i, i + by) for i in range(length) if 0 <= i + by < length]
    return lax.ppermute(value, axis, pairs)


def make_tables(length):
    indices = jnp.arange(length, dtype=jnp.int32)
    product = indices[:, None] * indices[None, :] % length
    angles = product.astype(jnp.float32) * (2.0 * math.pi / length)
    norming = 1.0 / math.sqrt(length)
    cosine_table = jnp.cos(angles) * norming
    sine_table = jnp.sin(angles) * norming
    forward = (cosine_table, -sine_table - cosine_table, cosine_table - sine_table)
    inverse = (cosine_table, sine_table - cosine_table, cosine_table + sine_table)
    return (forward, inverse)


def complex_product(real_part, imag_part, matrices, pattern):
    first_term = jnp.einsum(
        pattern, real_part + imag_part, matrices[0], precision=lax.Precision.HIGHEST
    )
    second_term = jnp.einsum(pattern, real_part, matrices[1], precision=lax.Precision.HIGHEST)
    third_term = jnp.einsum(pattern, imag_part, matrices[2], precision=lax.Precision.HIGHEST)
    return (first_term - third_term, first_term + second_term)


def transform(real_part, imag_part, matrices):
    rows_real, rows_imag = complex_product(real_part, imag_part, matrices, "bjk,kw->bjw")
    return complex_product(rows_real, rows_imag, matrices, "bkw,jk->bjw")


def window_terms(win_real, win_imag, measured, probe_real, probe_imag, forward, inverse):
    psi_real = probe_real * win_real - probe_imag * win_imag
    psi_imag = probe_real * win_imag + probe_imag * win_real
    hat_real, hat_imag = transform(psi_real, psi_imag, forward)
    ratio_term = measured / jnp.sqrt(hat_real * hat_real + hat_imag * hat_imag + smooth_floor) - 1.0
    return transform(hat_real * ratio_term, hat_imag * ratio_term, inverse)


def add_window(grid_now, terms, first_row, first_col):
    zero_index = jnp.zeros((), jnp.int32)
    present = lax.dynamic_slice(grid_now, (zero_index, first_row, first_col), terms.shape)
    return lax.dynamic_update_slice(grid_now, present + terms, (zero_index, first_row, first_col))


def shards(object_field, probe_field, amplitudes, offsets, counts):
    tile_rows = object_field.shape[1]
    tile_cols = object_field.shape[2]
    window = probe_field.shape[1]
    slot_count = amplitudes.shape[0]
    margin = HALO
    forward, inverse = make_tables(window)
    count_here = counts[0, 0]
    current = object_field
    probe_now = probe_field
    for outer_step in range(OUTER):
        probe_real = probe_now[0]
        probe_imag = probe_now[1]
        probe_mean = jnp.sum(probe_now * probe_now) / (window * window)
        lower_rows = shifted(current[:, :margin, :], "row", -1)
        taller = jnp.concatenate([current, lower_rows], axis=1)
        right_cols = shifted(taller[:, :, :margin], "col", -1)
        extended = jnp.concatenate([taller, right_cols], axis=2)
        grad_ext = jnp.zeros_like(extended)
        zero_index = jnp.zeros((), jnp.int32)
        window_list = [
            lax.dynamic_slice(
                extended,
                (zero_index, offsets[0, 0, slot_index, 0], offsets[0, 0, slot_index, 1]),
                (2, window, window),
            )
            for slot_index in range(slot_count)
        ]
        stacked = jnp.stack(window_list, axis=1)
        win_real = stacked[0]
        win_imag = stacked[1]
        diff_real, diff_imag = window_terms(
            win_real, win_imag, amplitudes, probe_real, probe_imag, forward, inverse
        )
        live_mask = (jnp.arange(slot_count, dtype=jnp.int32) < count_here).astype(jnp.float32)[
            :, None, None
        ]
        diff_real = diff_real * live_mask
        diff_imag = diff_imag * live_mask
        object_real = probe_real * diff_real + probe_imag * diff_imag
        object_imag = probe_real * diff_imag - probe_imag * diff_real
        probe_grad = jnp.stack(
            [
                jnp.sum(win_real * diff_real + win_imag * diff_imag, axis=0),
                jnp.sum(win_real * diff_imag - win_imag * diff_real, axis=0),
            ]
        )
        power_sum = jnp.sum(live_mask * (win_real * win_real + win_imag * win_imag))
        for slot_index in range(slot_count):
            terms = jnp.stack([object_real[slot_index], object_imag[slot_index]])
            grad_ext = add_window(
                grad_ext, terms, offsets[0, 0, slot_index, 0], offsets[0, 0, slot_index, 1]
            )
        rim_right = shifted(grad_ext[:, :, tile_cols:], "col", 1)
        narrowed = grad_ext[:, :, :tile_cols]
        narrowed = jnp.concatenate(
            [narrowed[:, :, :margin] + rim_right, narrowed[:, :, margin:]], axis=2
        )
        rim_lower = shifted(narrowed[:, tile_rows:, :], "row", 1)
        tile_grad = jnp.concatenate(
            [narrowed[:, :margin, :] + rim_lower, narrowed[:, margin:tile_rows, :]], axis=1
        )
        current = current + object_step * tile_grad / (probe_mean + tiny_value)
        power_old = jnp.sum(probe_now * probe_now)
        summed_grad, summed_power = lax.psum((probe_grad, power_sum), ("row", "col"))
        moved_probe = probe_now + summed_grad / (summed_power / (window * window) + tiny_value)
        power_new = jnp.sum(moved_probe * moved_probe)
        probe_now = moved_probe * jnp.sqrt(power_old / (power_new + tiny_value))
    return (current, probe_now)


def solution(mesh):
    return jax.shard_map(
        shards,
        mesh=mesh,
        in_specs=(
            P(None, "row", "col"),
            P(),
            P("row", "col", None),
            P("row", "col", None, None),
            P("row", "col"),
        ),
        out_specs=(P(None, "row", "col"), P()),
        check_vma=False,
    )
```

profile of v0, /device:TPU:17, one launch (start us, length us, event | category | flops | bytes accessed | tf_op | source)
XLA Modules:
  0.0 694.1 jit_solution(13178830681612049637)
XLA Ops:
  8.2 10.7 %collective-permute-start = (f32[2,128,256]{2,1,0:T(8,128)S(1)}, f32[2,128,256]{2,1,0:T(8,128)S(1)}, u32[]{:S(2)}, u32[]{:S(2)}) collective-permute-start(f32[2,128,256]{2,1,0:T(8,128)S(1)} %slice.127), channel_id=1, source_target_pairs={{8,0},{16,8},{24,16},{32,24},{40,32},{48,40},{56,48},{64,56},{72,6... | collective-permute-start | bytes 786440 | tf_op jit(solution)/shard_map/ppermute | solution.py:20
  20.0 3.9 collective-permute-done
  23.9 3.4 collective-permute-start.1
  47.3 2.0 fusion.42
  49.3 1.8 convolution_add_fusion.5
  51.1 1.8 convolution_subtract_fusion.5
  54.5 1.7 fusion.9
  56.3 2.4 add_reduce_fusion.1
  59.6 4.8 dynamic_update_slice.12
  65.5 7.9 %dynamic_update_slice.13 = f32[2,384,384]{2,1,0:T(8,128)S(1)} dynamic-update-slice(f32[2,384,384]{2,1,0:T(8,128)S(1)} %dynamic_update_slice.12, f32[2,256,256]{2,1,0:T(8,128)S(1)} %maximum_add_fusion, s32[]{:T(128)} %constant.29.clone.1, s32[]{:T(128)S(6)} %select_n.84, s32[]{:T(128)S(6)} %select_n.85) | dynamic-update-slice | bytes 1048580 | tf_op jit(solution)/shard_map/dynamic_update_slice | solution.py:60
  73.5 5.8 collective-permute-start.2
  80.2 3.8 collective-permute-done.2
  85.1 1.9 collective-permute-start.3
  87.0 101.5 %psum.29 = f32[]{:T(128)} all-reduce(f32[]{:T(128)} %get-tuple-element.7), channel_id=1, replica_groups=mesh['row'=64,'col'=8] {'row','col'}, use_global_device_ids=true, to_apply=%region_5.6 | all-reduce | flops 1 | bytes 8 | tf_op jit(solution)/shard_map/psum | solution.py:127
  189.2 164.0 %all-reduce.3.cloned.1.call-done = f32[2,256,256]{2,1,0:T(8,128)} async-done(((f32[2,256,256]{2,1,0:T(8,128)}), f32[2,256,256]{2,1,0:T(8,128)}) %all-reduce.3.cloned.1.call-update) | async-done | bytes 524304 | tf_op jit(solution)/shard_map/psum | solution.py:127
  353.2 1.8 multiply_reduce_fusion.3
  355.8 2.1 collective-permute-start.4
  359.2 6.5 collective-permute-done.4
  365.7 2.5 collective-permute-start.5
  368.4 6.5 collective-permute-done.5
  385.5 1.9 fusion.32
  387.4 1.8 convolution_add_fusion.1
  389.2 1.8 convolution_subtract_fusion.1
  394.3 2.4 add_reduce_fusion
  397.8 4.8 dynamic_update_slice.14
  402.8 7.9 %dynamic_update_slice.15 = f32[2,384,384]{2,1,0:T(8,128)S(1)} dynamic-update-slice(f32[2,384,384]{2,1,0:T(8,128)S(1)} %dynamic_update_slice.14, f32[2,256,256]{2,1,0:T(8,128)S(1)} %maximum_add_fusion.1, s32[]{:T(128)} %constant.29.clone.1, s32[]{:T(128)S(6)} %select_n.84, s32[]{:T(128)S(6)} %select_n.85) | dynamic-update-slice | bytes 1048580 | tf_op jit(solution)/shard_map/dynamic_update_slice | solution.py:60
  410.7 4.6 collective-permute-start.6
  415.3 99.1 %psum.31 = f32[]{:T(128)} all-reduce(f32[]{:T(128)} %get-tuple-element.6), channel_id=1, replica_groups=mesh['row'=64,'col'=8] {'row','col'}, use_global_device_ids=true, to_apply=%region_12.13 | all-reduce | flops 1 | bytes 8 | tf_op jit(solution)/shard_map/psum | solution.py:127
  515.0 154.1 %all-reduce.5.cloned.1.call-done = f32[2,256,256]{2,1,0:T(8,128)} async-done(((f32[2,256,256]{2,1,0:T(8,128)}), f32[2,256,256]{2,1,0:T(8,128)}) %all-reduce.5.cloned.1.call-update) | async-done | bytes 524304 | tf_op jit(solution)/shard_map/psum | solution.py:127
  669.2 1.8 multiply_reduce_fusion
  674.1 1.9 collective-permute-start.7
  676.9 9.1 %collective-permute-done.7 = f32[2,128,256]{2,1,0:T(8,128)S(1)} collective-permute-done((f32[2,128,256]{2,1,0:T(8,128)S(1)}, f32[2,128,256]{2,1,0:T(8,128)S(1)}, u32[]{:S(2)}, u32[]{:S(2)}) %collective-permute-start.7) | collective-permute-done | bytes 262176 | tf_op jit(solution)/shard_map/ppermute | solution.py:20
  (72 shorter events, 37.8 us)
Async XLA Ops:
  7.2 346.0 %all-reduce.3.cloned.1.call-start = ((), (), s32[]{:S(2)}) async-start(), calls=%async_computation | async-start | bytes 1048576 | tf_op jit(solution)/shard_map/psum | solution.py:127
  8.2 19.2 %copy-start.5 = (s32[1,1,2,2]{3,2,1,0:T(2,128)S(1)}, s32[1,1,2,2]{3,2,1,0:T(2,128)}, u32[]{:S(2)}) copy-start(s32[1,1,2,2]{3,2,1,0:T(2,128)} %param.8) | copy-start | bytes 52
  8.2 28.2 %copy-start.1 = (f32[2,256,256]{2,1,0:T(8,128)S(1)}, f32[2,256,256]{2,1,0:T(8,128)}, u32[]{:S(2)}) copy-start(f32[2,256,256]{2,1,0:T(8,128)} %param.6) | copy-start | bytes 1572868
  8.2 15.7 %collective-permute-start = (f32[2,128,256]{2,1,0:T(8,128)S(1)}, f32[2,128,256]{2,1,0:T(8,128)S(1)}, u32[]{:S(2)}, u32[]{:S(2)}) collective-permute-start(f32[2,128,256]{2,1,0:T(8,128)S(1)} %slice.127), channel_id=1, source_target_pairs={{8,0},{16,8},{24,16},{32,24},{40,32},{48,40},{56,48},{64,56},{72,6... | collective-permute-start | bytes 786440 | tf_op jit(solution)/shard_map/ppermute | solution.py:20
  23.9 12.5 %collective-permute-start.1 = (f32[2,384,128]{2,1,0:T(8,128)S(1)}, f32[2,384,128]{2,1,0:T(8,128)S(1)}, u32[]{:S(2)}, u32[]{:S(2)}) collective-permute-start(f32[2,384,128]{2,1,0:T(8,128)S(1)} %slice.162), channel_id=1, source_target_pairs={{1,0},{2,1},{3,2},{4,3},{5,4},{6,5},{7,6},{9,8},{10,9},{11,10},{12... | collective-permute-start | bytes 1179656 | tf_op jit(solution)/shard_map/ppermute | solution.py:20
  45.5 1.7 copy-start
  73.5 10.5 %collective-permute-start.2 = (f32[2,384,128]{2,1,0:T(8,128)S(1)}, f32[2,384,128]{2,1,0:T(8,128)}, u32[]{:S(2)}, u32[]{:S(2)}) collective-permute-start(f32[2,384,128]{2,1,0:T(8,128)S(1)} %slice.170), channel_id=1, source_target_pairs={{0,1},{1,2},{2,3},{3,4},{4,5},{5,6},{6,7},{8,9},{9,10},{10,11},{11... | collective-permute-start | bytes 1179656 | tf_op jit(solution)/shard_map/ppermute | solution.py:20
  80.2 589.0 %all-reduce.5.cloned.1.call-start = ((), (), s32[]{:S(2)}) async-start(), calls=%async_computation.1 | async-start | bytes 1048576 | tf_op jit(solution)/shard_map/psum | solution.py:127
  85.1 270.5 %collective-permute-start.3 = (f32[2,128,256]{2,1,0:T(8,128)S(1)}, f32[2,128,256]{2,1,0:T(8,128)S(1)}, u32[]{:S(2)}, u32[]{:S(2)}) collective-permute-start(f32[2,128,256]{2,1,0:T(8,128)S(1)} %fusion.56), channel_id=1, source_target_pairs={{0,8},{8,16},{16,24},{24,32},{32,40},{40,48},{48,56},{56,64},{64,7... | collective-permute-start | bytes 786440 | tf_op jit(solution)/shard_map/ppermute | solution.py:20
  189.2 166.5 %copy-start.2 = (f32[2,256,256]{2,1,0:T(8,128)S(1)}, f32[2,256,256]{2,1,0:T(8,128)}, u32[]{:S(2)}) copy-start(f32[2,256,256]{2,1,0:T(8,128)} %param.5) | copy-start | bytes 1572868
  355.7 12.5 %copy-start.4 = (f32[2,256,256]{2,1,0:T(8,128)S(1)}, f32[2,256,256]{2,1,0:T(8,128)}, u32[]{:S(2)}) copy-start(f32[2,256,256]{2,1,0:T(8,128)} %all-reduce.3.cloned.1.call-done) | copy-start | bytes 1572868
  355.8 9.9 %collective-permute-start.4 = (f32[2,128,256]{2,1,0:T(8,128)S(1)}, f32[2,128,256]{2,1,0:T(8,128)S(1)}, u32[]{:S(2)}, u32[]{:S(2)}) collective-permute-start(f32[2,128,256]{2,1,0:T(8,128)S(1)} %slice.177), channel_id=1, source_target_pairs={{8,0},{16,8},{24,16},{32,24},{40,32},{48,40},{56,48},{64,56},{72,6... | collective-permute-start | bytes 786440 | tf_op jit(solution)/shard_map/ppermute | solution.py:20
  365.7 9.1 %collective-permute-start.5 = (f32[2,384,128]{2,1,0:T(8,128)S(1)}, f32[2,384,128]{2,1,0:T(8,128)S(1)}, u32[]{:S(2)}, u32[]{:S(2)}) collective-permute-start(f32[2,384,128]{2,1,0:T(8,128)S(1)} %pad_maximum_fusion.7), channel_id=1, source_target_pairs={{1,0},{2,1},{3,2},{4,3},{5,4},{6,5},{7,6},{9,8},{10,9},{11,10},{12... | collective-permute-start | bytes 1179656 | tf_op jit(solution)/shard_map/ppermute | solution.py:20
  410.7 262.2 %collective-permute-start.6 = (f32[2,384,128]{2,1,0:T(8,128)S(1)}, f32[2,384,128]{2,1,0:T(8,128)}, u32[]{:S(2)}, u32[]{:S(2)}) collective-permute-start(f32[2,384,128]{2,1,0:T(8,128)S(1)} %slice.186), channel_id=1, source_target_pairs={{0,1},{1,2},{2,3},{3,4},{4,5},{5,6},{6,7},{8,9},{9,10},{10,11},{11... | collective-permute-start | bytes 1179656 | tf_op jit(solution)/shard_map/ppermute | solution.py:20
  672.9 3.1 copy-start.3
  674.1 11.9 %collective-permute-start.7 = (f32[2,128,256]{2,1,0:T(8,128)S(1)}, f32[2,128,256]{2,1,0:T(8,128)S(1)}, u32[]{:S(2)}, u32[]{:S(2)}) collective-permute-start(f32[2,128,256]{2,1,0:T(8,128)S(1)} %fusion.53), channel_id=1, source_target_pairs={{0,8},{8,16},{16,24},{24,32},{32,40},{40,48},{48,56},{56,64},{64,7... | collective-permute-start | bytes 786440 | tf_op jit(solution)/shard_map/ppermute | solution.py:20
Sparse Core Ops, SparseCore 0:
  80.3 272.8 all-reduce.2
  397.7 271.3 all-reduce.4
where the time goes:
time: 704 us; the launch traced here: 694 us
  waiting for transfers between devices  348 us (49%)
  blocking collectives  201 us (29%)
  matrix products  42.7 us (6%)
  starting transfers between devices  33 us (5%)
  local copies, waits for them, and re-layouts  29.6 us (4%)
  between operations  28.6 us (4%)
  other arithmetic  11.7 us (2%)
    psum x2, waiting for transfers between devices, shards(): lax.psum((probe_grad, power_sum), ('row', 'col'))  318 us
    psum x2, blocking collectives, shards(): lax.psum((probe_grad, power_sum), ('row', 'col'))  201 us
    ppermute x8, starting transfers between devices, shifted(): return lax.ppermute(value, axis, pairs)  32.9 us
    ppermute x8, waiting for transfers between devices, shifted(): return lax.ppermute(value, axis, pairs)  29.8 us
    dynamic_update_slice x4, local copies, waits for them, and re-layouts, add_window(): lax.dynamic_update_slice(grid_now, present + terms, (zero_index, first_ro...  25.3 us
    dot_general x8, matrix products, complex_product(): jnp.einsum(pattern, real_part, matrices[1], precision=lax.Precision.HIGHEST)  15.1 us
  transfers between devices with their start and end apart: 10, of which 7 were waited for; matrix products, arithmetic and copies ran while one was open for 3% of the time, Pallas kernels for 0%

commit v1 on v0

v1 whole, which is shorter than its diff:
```python
import functools

import jax
import jax.numpy as jnp
import numpy as np
from jax import lax
from jax.experimental import pallas as pl
from jax.experimental.pallas import tpu as pltpu
from jax.sharding import PartitionSpec as P

HALO = 128
SUB, LANE = 8, 128
OUTER = 2
NEAR = 8

smooth_floor = 0.5
object_step = 0.5
tiny_value = 1e-06

VMEM = pl.BlockSpec(memory_space=pltpu.VMEM)
SMEM = pl.BlockSpec(memory_space=pltpu.SMEM)


def shifted(value, down_by, across_by):
    down = lax.axis_size("row")
    across = lax.axis_size("col")
    pairs = [
        (r * across + c, (r + down_by) * across + c + across_by)
        for r in range(down)
        for c in range(across)
        if 0 <= r + down_by < down and 0 <= c + across_by < across
    ]
    return lax.ppermute(value, ("row", "col"), pairs)


def device_groups(down, across):
    far = down // NEAR
    near_groups = [
        [(y * NEAR + z) * across + c for z in range(NEAR) for c in range(across)]
        for y in range(far)
    ]
    far_groups = [
        [(y * NEAR + z) * across + c for y in range(far)]
        for z in range(NEAR)
        for c in range(across)
    ]
    return near_groups, far_groups


def exchange(rows, groups):
    count, lanes = rows.shape
    paired = rows.reshape(count // 2, 2, lanes)
    moved = lax.all_to_all(
        paired, ("row", "col"), 0, 0, tiled=True, axis_index_groups=groups
    )
    return moved.reshape(count, lanes)


def make_tables(length):
    half = length // 2
    out = []
    for start in (0, 1):
        first = np.arange(half)[:, None]
        second = np.arange(start, length, 2)[None, :]
        angle = -2.0 * np.pi * ((first * second) % length) / length
        real = np.cos(angle) / np.sqrt(length)
        imag = np.sin(angle) / np.sqrt(length)
        block = np.block([[real, imag], [-imag, real]])
        for table in (block, block.T):
            high = table.astype(np.float32).astype(jnp.bfloat16)
            low = (table - high.astype(np.float64)).astype(np.float32)
            out += [high, low.astype(jnp.bfloat16)]
    return np.stack(out)


def split(value):
    high = value.astype(jnp.bfloat16)
    low = (value - high.astype(jnp.float32)).astype(jnp.bfloat16)
    return high, low


def mul(left, right):
    return jnp.dot(left, right, preferred_element_type=jnp.float32)


def mul3(left, right):
    return mul(left[0], right[0]) + (mul(left[0], right[1]) + mul(left[1], right[0]))


def edges_kernel(tile, low, right, corner):
    low[...] = tile[:, :HALO, :]
    right[...] = tile[:, :, :HALO]
    corner[...] = tile[:, :HALO, :HALO]


def order_kernel(amplitudes, pick, out, held):
    slots, size, _ = amplitudes.shape
    half = size // 2
    for slot in range(slots):
        rest = amplitudes[slot]
        total = jnp.zeros((size, size), jnp.float32)
        for _ in range(3):
            piece = rest.astype(jnp.bfloat16)
            total = total + mul(piece, pick[...])
            rest = rest - piece.astype(jnp.float32)
        for side in range(2):
            held[2 * slot + side] = total[:, side * half : (side + 1) * half]
            for part in range(2):
                out[slot, part * half : (part + 1) * half, side * half : (side + 1) * half] = held[
                    2 * slot + side, pl.ds(part, half, 2), :
                ]


def halves(row, col):
    rest = jnp.bitwise_and(row, SUB - 1)
    base = pl.multiple_of(row - rest, SUB)
    at_row = lax.broadcasted_iota(jnp.int32, (1, SUB, LANE), 1)
    at_col = lax.broadcasted_iota(jnp.int32, (1, SUB, LANE), 2)
    return rest, base, at_row, at_col


def take_window(ext, part, row, col, size):
    rest, base, at_row, at_col = halves(row, col)
    wide = ext[part, pl.ds(base, size + SUB), :]
    wide = wide.reshape(size // SUB + 1, SUB, wide.shape[1])
    turn_col = jnp.bitwise_and(LANE - col, LANE - 1)
    turn_row = jnp.bitwise_and(SUB - rest, SUB - 1)
    turned = []
    for t in range(wide.shape[2] // LANE):
        block = pltpu.roll(wide[:, :, t * LANE : (t + 1) * LANE], turn_col, 2)
        turned.append(pltpu.roll(block, turn_row, 1))
    out = []
    for t in range(len(turned) - 1):
        block = jnp.where(at_col < LANE - col, turned[t], turned[t + 1])
        block = jnp.where(at_row < SUB - rest, block[:-1], block[1:])
        out.append(block.reshape(size, LANE))
    return jnp.concatenate(out, axis=1)


def add_window(ext, part, row, col, value):
    size = value.shape[0]
    rest, base, at_row, at_col = halves(row, col)
    turn_col = jnp.bitwise_and(col, LANE - 1)
    blocks = []
    for t in range(size // LANE):
        block = value[:, t * LANE : (t + 1) * LANE].reshape(size // SUB, SUB, LANE)
        block = pltpu.roll(pltpu.roll(block, turn_col, 2), rest, 1)
        edge = jnp.zeros((1, SUB, LANE), jnp.float32)
        blocks.append(
            jnp.where(
                at_row < rest,
                jnp.concatenate([edge, block], axis=0),
                jnp.concatenate([block, edge], axis=0),
            )
        )
    none = jnp.zeros_like(blocks[0])
    blocks = [none] + blocks + [none]
    for t in range(len(blocks) - 1):
        placed = jnp.where(at_col < col, blocks[t], blocks[t + 1])
        at = (part, pl.ds(base, size + SUB), slice(t * LANE, (t + 1) * LANE))
        ext[at] = ext[at] + placed.reshape(size + SUB, LANE)


def solve_kernel(first, members, *refs):
    if first:
        (offsets, counts, tile, low, right, corner, probe, amp, tables) = refs[:9]
        message, terms, ext = refs[9:]
    else:
        (offsets, counts, tile, low, right, corner, probe, grad, power, amp, tables) = refs[:11]
        message, terms, new_probe, ext = refs[11:]
    size = tile.shape[1]
    half = size // 2
    slots = amp.shape[0]
    ext[:, :size, :size] = tile[...]
    ext[:, size : size + HALO, :size] = low[...]
    ext[:, :size, size:] = right[...]
    ext[:, size : size + HALO, size:] = corner[...]
    ext[:, size + HALO :, :] = jnp.zeros((2, SUB, size + HALO), jnp.float32)

    if first:
        p_real = probe[0]
        p_imag = probe[1]
    else:
        p_real, p_imag = moved_probe(probe, grad, power)
        new_probe[0] = p_real
        new_probe[1] = p_imag
    mean = jnp.sum(p_real * p_real + p_imag * p_imag) / (size * size)
    scale = object_step / (mean + tiny_value)

    even, even_t, odd, odd_t = (
        (tables[2 * n], tables[2 * n + 1]) for n in range(4)
    )
    pg_real = jnp.zeros((size, size), jnp.float32)
    pg_imag = jnp.zeros((size, size), jnp.float32)
    power_sum = jnp.zeros((), jnp.float32)
    for slot in range(slots):
        row = jnp.clip(offsets[slot, 0], 0, HALO)
        col = jnp.clip(offsets[slot, 1], 0, HALO)
        live = slot < counts[0]
        z_real = take_window(ext, 0, row, col, size)
        z_imag = take_window(ext, 1, row, col, size)
        psi_real = p_real * z_real - p_imag * z_imag
        psi_imag = p_real * z_imag + p_imag * z_real
        plus = jnp.concatenate(
            [psi_real[:, :half] + psi_real[:, half:], psi_imag[:, :half] + psi_imag[:, half:]], axis=1
        )
        minus = jnp.concatenate(
            [psi_real[:, :half] - psi_real[:, half:], psi_imag[:, :half] - psi_imag[:, half:]], axis=1
        )
        a_even = mul3(split(plus), even)
        a_odd = mul3(split(minus), odd)
        y_real = jnp.concatenate([a_even[:, :half], a_odd[:, :half]], axis=1)
        y_imag = jnp.concatenate([a_even[:, half:], a_odd[:, half:]], axis=1)
        plus = jnp.concatenate([y_real[:half] + y_real[half:], y_imag[:half] + y_imag[half:]], axis=0)
        minus = jnp.concatenate([y_real[:half] - y_real[half:], y_imag[:half] - y_imag[half:]], axis=0)
        sums = []
        for part, (data, table, back) in enumerate(((plus, even_t, even), (minus, odd_t, odd))):
            hat = mul3(table, split(data))
            h_real = hat[:half]
            h_imag = hat[half:]
            magnitude = h_real * h_real + h_imag * h_imag
            measured = amp[slot, part * half : (part + 1) * half, :]
            ratio = measured * lax.rsqrt(magnitude + smooth_floor) - 1.0
            scaled = jnp.concatenate([h_real * ratio, h_imag * ratio], axis=0)
            sums.append(mul3(back, split(scaled)))
        top = sums[0] + sums[1]
        bottom = sums[0] - sums[1]
        z_even = jnp.concatenate(
            [
                jnp.concatenate([top[:half, :half], top[half:, :half]], axis=1),
                jnp.concatenate([bottom[:half, :half], bottom[half:, :half]], axis=1),
            ],
            axis=0,
        )
        z_odd = jnp.concatenate(
            [
                jnp.concatenate([top[:half, half:], top[half:, half:]], axis=1),
                jnp.concatenate([bottom[:half, half:], bottom[half:, half:]], axis=1),
            ],
            axis=0,
        )
        u = mul3(split(z_even), even_t)
        v = mul3(split(z_odd), odd_t)
        plus = u + v
        minus = u - v
        d_real = jnp.concatenate([plus[:, :half], minus[:, :half]], axis=1)
        d_imag = jnp.concatenate([plus[:, half:], minus[:, half:]], axis=1)
        d_real = jnp.where(live, d_real, 0.0)
        d_imag = jnp.where(live, d_imag, 0.0)
        pg_real = pg_real + (z_real * d_real + z_imag * d_imag)
        pg_imag = pg_imag + (z_real * d_imag - z_imag * d_real)
        terms[slot, 0] = (p_real * d_real + p_imag * d_imag) * scale
        terms[slot, 1] = (p_real * d_imag - p_imag * d_real) * scale
        window_power = jnp.sum(z_real * z_real + z_imag * z_imag)
        power_sum = power_sum + jnp.where(live, window_power, 0.0)

    pieces = [pg_real[:, :half], pg_real[:, half:], pg_imag[:, :half], pg_imag[:, half:]]
    per = 4 * size // members
    for m in range(members):
        source = pieces[m * per // size]
        at = m * per % size
        message[m * (per + 2) : m * (per + 2) + per, :] = source[at : at + per, :]
        message[m * (per + 2) + per : (m + 1) * (per + 2), :] = jnp.full((2, half), power_sum)


def moved_probe(probe, grad, power):
    size = probe.shape[1]
    half = size // 2
    factor = 1.0 / (power[0:1, 0:1] / (size * size) + tiny_value)
    p_real = probe[0]
    p_imag = probe[1]
    g_real = jnp.concatenate([grad[:size, :], grad[size : 2 * size, :]], axis=1)
    g_imag = jnp.concatenate([grad[2 * size : 3 * size, :], grad[3 * size :, :]], axis=1)
    m_real = p_real + g_real * factor
    m_imag = p_imag + g_imag * factor
    old = jnp.sum(p_real * p_real + p_imag * p_imag)
    new = jnp.sum(m_real * m_real + m_imag * m_imag)
    gain = jnp.sqrt(jnp.full((1, 1), old) / (jnp.full((1, 1), new) + tiny_value))
    return m_real * gain, m_imag * gain


def probe_kernel(probe, grad, power, out):
    real, imag = moved_probe(probe, grad, power)
    out[0] = real
    out[1] = imag


def place_kernel(offsets, tile, terms, partial, rim_right, rim_low, rim_corner, ext):
    size = tile.shape[1]
    slots = terms.shape[0]
    ext[...] = jnp.zeros_like(ext)
    for slot in range(slots):
        row = jnp.clip(offsets[slot, 0], 0, HALO)
        col = jnp.clip(offsets[slot, 1], 0, HALO)
        for part in range(2):
            add_window(ext, part, row, col, terms[slot, part])
    partial[...] = tile[...] + ext[:, :size, :size]
    rim_right[...] = ext[:, :size, size:]
    rim_low[...] = ext[:, size : size + HALO, :size]
    rim_corner[...] = ext[:, size : size + HALO, size:]


def update_kernel(with_edges, partial, from_left, from_above, from_corner, out, *edges):
    size = partial.shape[1]
    out[...] = partial[...]
    out[:, :, :HALO] += from_left[...]
    out[:, :HALO, :] += from_above[...]
    out[:, :HALO, :HALO] += from_corner[...]
    if with_edges:
        edges_kernel(out, *edges)


def fold_kernel(members, copies, keep, source, out, *power):
    count = source.shape[0]
    n = count // members
    step = 4 * n
    groups = count // step
    total = source[0:step, :]
    for g in range(1, groups):
        total = total + source[g * step : (g + 1) * step, :]
    summed = total[0:n] + total[n : 2 * n] + (total[2 * n : 3 * n] + total[3 * n :])
    for c in range(copies):
        out[c * keep : (c + 1) * keep, :] = summed[:keep]
    if power:
        power[0][...] = jnp.broadcast_to(summed[n - 1 : n], power[0].shape)


def call(kernel, outs, specs, *args, scratch=()):
    return pl.pallas_call(
        kernel,
        out_shape=[jax.ShapeDtypeStruct(shape, jnp.float32) for shape in outs],
        in_specs=specs,
        out_specs=[VMEM] * len(outs),
        scratch_shapes=[pltpu.VMEM(shape, jnp.float32) for shape in scratch],
    )(*args)


def shards(object_field, probe_field, amplitudes, offsets, counts):
    _, size, _ = object_field.shape
    half = size // 2
    slots = amplitudes.shape[0]
    margin = HALO
    edge_shapes = [(2, margin, size), (2, size, margin), (2, margin, margin)]
    near_groups, far_groups = device_groups(lax.axis_size("row"), lax.axis_size("col"))
    near, far = len(near_groups[0]), len(far_groups[0])
    per = 4 * size // near
    tables = jnp.asarray(make_tables(size))
    order = np.concatenate([np.arange(0, size, 2), np.arange(1, size, 2)])
    pick = jnp.asarray(np.eye(size)[:, order].astype(jnp.bfloat16))
    spots = offsets.reshape(slots, 2)
    live = counts.reshape(1)

    current = object_field
    probe_now = probe_field
    edges = call(edges_kernel, edge_shapes, [VMEM], current)
    (amp,) = call(
        order_kernel,
        [amplitudes.shape],
        [VMEM, VMEM],
        amplitudes,
        pick,
        scratch=[(2 * slots, size, half)],
    )
    grad = power = None
    for outer_step in range(OUTER):
        low = shifted(edges[0], -1, 0)
        right = shifted(edges[1], 0, -1)
        corner = shifted(edges[2], -1, -1)
        first = outer_step == 0
        outs = [(near * (per + 2), half), (slots, 2, size, size)]
        args = [spots, live, current, low, right, corner, probe_now]
        if not first:
            outs.append((2, size, size))
            args += [grad, power]
        args += [amp, tables]
        done = call(
            functools.partial(solve_kernel, first, near),
            outs,
            [SMEM, SMEM] + [VMEM] * (len(args) - 2),
            *args,
            scratch=[(2, size + margin + SUB, size + margin)],
        )
        message, terms = done[:2]
        if not first:
            probe_now = done[2]
        arrived = exchange(message, near_groups)
        partial, rim_right, rim_low, rim_corner = call(
            place_kernel,
            [current.shape, edge_shapes[1], edge_shapes[0], edge_shapes[2]],
            [SMEM, VMEM, VMEM],
            spots,
            current,
            terms,
            scratch=[(2, size + margin + SUB, size + margin)],
        )
        from_left = shifted(rim_right, 0, 1)
        from_above = shifted(rim_low, 1, 0)
        from_corner = shifted(rim_corner, 1, 1)
        (copies,) = call(
            functools.partial(fold_kernel, near, far, per + 2),
            [(far * (per + 2), half)],
            [VMEM],
            arrived,
        )
        arrived = exchange(copies, far_groups)
        copies, power = call(
            functools.partial(fold_kernel, far, near, per),
            [(near * per, half), (8, half)],
            [VMEM],
            arrived,
        )
        grad = exchange(copies, near_groups)
        last = outer_step == OUTER - 1
        current, *edges = call(
            functools.partial(update_kernel, not last),
            [current.shape] + ([] if last else edge_shapes),
            [VMEM] * 4,
            partial,
            from_left,
            from_above,
            from_corner,
        )
    (probe_now,) = call(
        probe_kernel, [probe_field.shape], [VMEM] * 3, probe_now, grad, power
    )
    return (current, probe_now)


def solution(mesh):
    return jax.shard_map(
        shards,
        mesh=mesh,
        in_specs=(
            P(None, "row", "col"),
            P(),
            P("row", "col", None),
            P("row", "col", None, None),
            P("row", "col"),
        ),
        out_specs=(P(None, "row", "col"), P()),
        check_vma=False,
    )
```

time: 704 us -> 210 us (0.30)
  the two profiles are of different devices: /device:TPU:17 before, /device:TPU:14 now
where the time goes in v1:
time: 210 us; the launch traced here: 208 us
  blocking collectives  82.3 us (39%)
  starting transfers between devices  51.6 us (25%)
  Pallas kernels  37.1 us (18%)
  waiting for transfers between devices  31.6 us (15%)
  local copies, waits for them, and re-layouts  4.23 us (2%)
    all_to_all x4, blocking collectives, exchange(): lax.all_to_all(paired, ('row', 'col'), 0, 0, tiled=True, axis_index_group...  82.3 us
    ppermute x12, starting transfers between devices, shifted(): return lax.ppermute(value, ('row', 'col'), pairs)  40 us
    pallas_call x13, Pallas kernels, call(): pl.pallas_call(kernel, out_shape=[jax.ShapeDtypeStruct(shape, jnp.float32...  37.1 us
    ppermute x12, waiting for transfers between devices, shifted(): return lax.ppermute(value, ('row', 'col'), pairs)  31.6 us
    all_to_all x2, starting transfers between devices, exchange(): lax.all_to_all(paired, ('row', 'col'), 0, 0, tiled=True, axis_index_group...  11.6 us
    unnamed x28, local copies, waits for them, and re-layouts  4.23 us
  transfers between devices with their start and end apart: 14, of which 4 were waited for; matrix products, arithmetic and copies ran while one was open for 0% of the time, Pallas kernels for 6%

profile of v1, /device:TPU:14, one launch (start us, length us, event | category | flops | bytes accessed | tf_op | source)
XLA Modules:
  0.0 208.4 jit_solution(5932072009253065555)
XLA Ops:
  0.6 1.9 shard_map.86
  2.5 10.8 %collective-permute-start = (f32[2,128,256]{2,1,0:T(8,128)}, f32[2,128,256]{2,1,0:T(8,128)S(1)}, u32[]{:S(2)}, u32[]{:S(2)}) collective-permute-start(f32[2,128,256]{2,1,0:T(8,128)} %get-tuple-element.26), channel_id=1, source_target_pairs={{8,0},{9,1},{10,2},{11,3},{12,4},{13,5},{14,6},{15,7},{16,8},{17,9... | collective-permute-start | bytes 786440 | tf_op jit(solution)/shard_map/ppermute | solution.py:33
  13.4 1.9 collective-permute-start.1
  15.3 2.8 %collective-permute-start.2 = (f32[2,128,128]{2,1,0:T(8,128)}, f32[2,128,128]{2,1,0:T(8,128)S(1)}, u32[]{:S(2)}, u32[]{:S(2)}) collective-permute-start(f32[2,128,128]{2,1,0:T(8,128)} %get-tuple-element.28), channel_id=1, source_target_pairs={{9,0},{10,1},{11,2},{12,3},{13,4},{14,5},{15,6},{17,8},{18,9},{19,... | collective-permute-start | bytes 393224 | tf_op jit(solution)/shard_map/ppermute | solution.py:33
  18.8 2.3 %shard_map.87.refs_7_.refs_9_ = f32[2,256,256]{2,1,0:T(8,128)} custom-call(f32[2,256,256]{2,1,0:T(8,128)} %amplitudes.1, bf16[256,256]{1,0:T(8,128)(2,1)} %constant.5.clone.pick), custom_call_target="tpu_custom_call" | custom-call | tf_op jit(solution)/shard_map/pallas_call | solution.py:329
  23.1 6.6 %shard_map.88 = (f32[1152,128]{1,0:T(8,128)}, f32[2,2,256,256]{3,2,1,0:T(8,128)}) custom-call(s32[2,2]{1,0:T(2,128)} %bitcast.28, s32[1]{0:T(128)} %bitcast.14.refs_1_, f32[2,256,256]{2,1,0:T(8,128)} %tile.3, f32[2,128,256]{2,1,0:T(8,128)} %copy-done.2, f32[2,256,128]{2,1,0:T(8,128)} %copy-done.3, f32[2,128,128]{2,1,0:T(8,128)} %copy-done.11, ...), custom_call_target="tpu_custom_call" | custom-call | tf_op jit(solution)/shard_map/pallas_call | solution.py:329
  29.7 28.3 %all_to_all.30 = f32[576,2,128]{2,1,0:T(2,128)} all-to-all(f32[576,2,128]{2,1,0:T(2,128)} %bitcast.21), channel_id=1, replica_groups={{0,1,2,3,4,5,6,7,8,9,10,11,12,13,14,15,16,17,18,19,20,21,22,23,24,25,26..., dimensions={0} | all-to-all | bytes 1179648 | tf_op jit(solution)/shard_map/all_to_all | solution.py:53
  58.0 1.7 shard_map.91
  59.8 14.6 %all_to_all.31 = f32[72,2,128]{2,1,0:T(2,128)} all-to-all(f32[72,2,128]{2,1,0:T(2,128)} %bitcast.26), channel_id=1, replica_groups={{0,64,128,192,256,320,384,448},{1,65,129,193,257,321,385,449},{2,66,130..., dimensions={0} | all-to-all | bytes 147456 | tf_op jit(solution)/shard_map/all_to_all | solution.py:53
  76.1 5.8 %all-to-all-start.2 = ((f32[512,2,128]{2,1,0:T(2,128)}), f32[512,2,128]{2,1,0:T(2,128)S(1)}, u32[]{:S(2)}, u32[]{:S(2)}) async-start(f32[512,2,128]{2,1,0:T(2,128)} %bitcast.22), calls=%async_computation.2 | async-start | bytes 1048576 | tf_op jit(solution)/shard_map/all_to_all | solution.py:53
  81.9 2.8 %shard_map.89 = (f32[2,256,256]{2,1,0:T(8,128)}, f32[2,256,128]{2,1,0:T(8,128)}, f32[2,128,256]{2,1,0:T(8,128)}, f32[2,128,128]{2,1,0:T(8,128)}) custom-call(s32[2,2]{1,0:T(2,128)} %bitcast.29, f32[2,256,256]{2,1,0:T(8,128)} %tile.3, f32[2,2,256,256]{3,2,1,0:T(8,128)} %get-tuple-element.29.terms), custom_call_target="tpu_custom_call" | custom-call | tf_op jit(solution)/shard_map/pallas_call | solution.py:329
  84.7 2.0 collective-permute-start.3
  86.7 3.4 %collective-permute-start.4 = (f32[2,128,256]{2,1,0:T(8,128)}, f32[2,128,256]{2,1,0:T(8,128)S(1)}, u32[]{:S(2)}, u32[]{:S(2)}) collective-permute-start(f32[2,128,256]{2,1,0:T(8,128)} %get-tuple-element.32), channel_id=1, source_target_pairs={{0,8},{1,9},{2,10},{3,11},{4,12},{5,13},{6,14},{7,15},{8,16},{9,17... | collective-permute-start | bytes 786440 | tf_op jit(solution)/shard_map/ppermute | solution.py:33
  90.1 2.1 %collective-permute-start.5 = (f32[2,128,128]{2,1,0:T(8,128)}, f32[2,128,128]{2,1,0:T(8,128)S(1)}, u32[]{:S(2)}, u32[]{:S(2)}) collective-permute-start(f32[2,128,128]{2,1,0:T(8,128)} %get-tuple-element.33), channel_id=1, source_target_pairs={{0,9},{1,10},{2,11},{3,12},{4,13},{5,14},{6,15},{8,17},{9,18},{10,... | collective-permute-start | bytes 393224 | tf_op jit(solution)/shard_map/ppermute | solution.py:33
  92.2 13.1 %collective-permute-done.5.from_corner = f32[2,128,128]{2,1,0:T(8,128)S(1)} collective-permute-done((f32[2,128,128]{2,1,0:T(8,128)}, f32[2,128,128]{2,1,0:T(8,128)S(1)}, u32[]{:S(2)}, u32[]{:S(2)}) %collective-permute-start.5) | collective-permute-done | bytes 131104 | tf_op jit(solution)/shard_map/ppermute | solution.py:33
  106.2 2.3 %shard_map.90 = (f32[2,256,256]{2,1,0:T(8,128)}, f32[2,128,256]{2,1,0:T(8,128)}, f32[2,256,128]{2,1,0:T(8,128)}, f32[2,128,128]{2,1,0:T(8,128)}) custom-call(f32[2,256,256]{2,1,0:T(8,128)} %get-tuple-element.30.partial, f32[2,256,128]{2,1,0:T(8,128)} %copy-done.4, f32[2,128,256]{2,1,0:T(8,128)} %copy-done.5, f32[2,128,128]{2,1,0:T(8,128)} %copy-done.10), custom_call_target="tpu_custom_call" | custom-call | tf_op jit(solution)/shard_map/pallas_call | solution.py:329
  108.5 3.9 %collective-permute-start.6 = (f32[2,128,256]{2,1,0:T(8,128)}, f32[2,128,256]{2,1,0:T(8,128)S(1)}, u32[]{:S(2)}, u32[]{:S(2)}) collective-permute-start(f32[2,128,256]{2,1,0:T(8,128)} %get-tuple-element.35), channel_id=1, source_target_pairs={{8,0},{9,1},{10,2},{11,3},{12,4},{13,5},{14,6},{15,7},{16,8},{17,9... | collective-permute-start | bytes 786440 | tf_op jit(solution)/shard_map/ppermute | solution.py:33
  112.4 2.2 %collective-permute-start.7 = (f32[2,256,128]{2,1,0:T(8,128)}, f32[2,256,128]{2,1,0:T(8,128)S(1)}, u32[]{:S(2)}, u32[]{:S(2)}) collective-permute-start(f32[2,256,128]{2,1,0:T(8,128)} %get-tuple-element.36), channel_id=1, source_target_pairs={{1,0},{2,1},{3,2},{4,3},{5,4},{6,5},{7,6},{9,8},{10,9},{11,10},{12... | collective-permute-start | bytes 786440 | tf_op jit(solution)/shard_map/ppermute | solution.py:33
  114.6 3.3 %collective-permute-start.8 = (f32[2,128,128]{2,1,0:T(8,128)}, f32[2,128,128]{2,1,0:T(8,128)S(1)}, u32[]{:S(2)}, u32[]{:S(2)}) collective-permute-start(f32[2,128,128]{2,1,0:T(8,128)} %get-tuple-element.37), channel_id=1, source_target_pairs={{9,0},{10,1},{11,2},{12,3},{13,4},{14,5},{15,6},{17,8},{18,9},{19,... | collective-permute-start | bytes 393224 | tf_op jit(solution)/shard_map/ppermute | solution.py:33
  118.0 4.2 %collective-permute-done.8.refs_5_ = f32[2,128,128]{2,1,0:T(8,128)S(1)} collective-permute-done((f32[2,128,128]{2,1,0:T(8,128)}, f32[2,128,128]{2,1,0:T(8,128)S(1)}, u32[]{:S(2)}, u32[]{:S(2)}) %collective-permute-start.8) | collective-permute-done | bytes 131104 | tf_op jit(solution)/shard_map/ppermute | solution.py:33
  123.1 7.1 %shard_map.93 = (f32[1152,128]{1,0:T(8,128)}, f32[2,2,256,256]{3,2,1,0:T(8,128)}, f32[2,256,256]{2,1,0:T(8,128)}) custom-call(s32[2,2]{1,0:T(2,128)} %bitcast.30, s32[1]{0:T(128)} %bitcast.15.refs_1_, f32[2,256,256]{2,1,0:T(8,128)} %get-tuple-element.34.refs_2_.tile, f32[2,128,256]{2,1,0:T(8,128)} %copy-done.8, f32[2,256,128]{2,1,0:T(8,128)} %copy-done.9, ...), custom_call_target="tpu_custom_call" | custom-call | tf_op jit(solution)/shard_map/pallas_call | solution.py:329
  130.3 26.9 %all_to_all.32 = f32[576,2,128]{2,1,0:T(2,128)} all-to-all(f32[576,2,128]{2,1,0:T(2,128)} %bitcast.20), channel_id=1, replica_groups={{0,1,2,3,4,5,6,7,8,9,10,11,12,13,14,15,16,17,18,19,20,21,22,23,24,25,26..., dimensions={0} | all-to-all | bytes 1179648 | tf_op jit(solution)/shard_map/all_to_all | solution.py:53
  157.2 1.7 shard_map.96
  159.0 12.4 %all_to_all.33 = f32[72,2,128]{2,1,0:T(2,128)} all-to-all(f32[72,2,128]{2,1,0:T(2,128)} %bitcast.27), channel_id=1, replica_groups={{0,64,128,192,256,320,384,448},{1,65,129,193,257,321,385,449},{2,66,130..., dimensions={0} | all-to-all | bytes 147456 | tf_op jit(solution)/shard_map/all_to_all | solution.py:53
  173.1 5.8 %all-to-all-start.5 = ((f32[512,2,128]{2,1,0:T(2,128)}), f32[512,2,128]{2,1,0:T(2,128)S(1)}, u32[]{:S(2)}, u32[]{:S(2)}) async-start(f32[512,2,128]{2,1,0:T(2,128)} %bitcast.23), calls=%async_computation.5 | async-start | bytes 1048576 | tf_op jit(solution)/shard_map/all_to_all | solution.py:53
  178.9 2.8 %shard_map.94 = (f32[2,256,256]{2,1,0:T(8,128)}, f32[2,256,128]{2,1,0:T(8,128)}, f32[2,128,256]{2,1,0:T(8,128)}, f32[2,128,128]{2,1,0:T(8,128)}) custom-call(s32[2,2]{1,0:T(2,128)} %bitcast.31, f32[2,256,256]{2,1,0:T(8,128)} %get-tuple-element.34.refs_2_.tile, f32[2,2,256,256]{3,2,1,0:T(8,128)} %get-tuple-element.41.terms), custom_call_target="tpu_custom_call" | custom-call | tf_op jit(solution)/shard_map/pallas_call | solution.py:329
  181.7 2.0 collective-permute-start.9
  183.7 3.4 %collective-permute-start.10 = (f32[2,128,256]{2,1,0:T(8,128)}, f32[2,128,256]{2,1,0:T(8,128)S(1)}, u32[]{:S(2)}, u32[]{:S(2)}) collective-permute-start(f32[2,128,256]{2,1,0:T(8,128)} %get-tuple-element.44), channel_id=1, source_target_pairs={{0,8},{1,9},{2,10},{3,11},{4,12},{5,13},{6,14},{7,15},{8,16},{9,17... | collective-permute-start | bytes 786440 | tf_op jit(solution)/shard_map/ppermute | solution.py:33
  187.1 2.1 %collective-permute-start.11 = (f32[2,128,128]{2,1,0:T(8,128)}, f32[2,128,128]{2,1,0:T(8,128)S(1)}, u32[]{:S(2)}, u32[]{:S(2)}) collective-permute-start(f32[2,128,128]{2,1,0:T(8,128)} %get-tuple-element.45), channel_id=1, source_target_pairs={{0,9},{1,10},{2,11},{3,12},{4,13},{5,14},{6,15},{8,17},{9,18},{10,... | collective-permute-start | bytes 393224 | tf_op jit(solution)/shard_map/ppermute | solution.py:33
  189.2 13.1 %collective-permute-done.11.from_corner = f32[2,128,128]{2,1,0:T(8,128)S(1)} collective-permute-done((f32[2,128,128]{2,1,0:T(8,128)}, f32[2,128,128]{2,1,0:T(8,128)S(1)}, u32[]{:S(2)}, u32[]{:S(2)}) %collective-permute-start.11) | collective-permute-done | bytes 131104 | tf_op jit(solution)/shard_map/ppermute | solution.py:33
  203.2 2.1 shard_map.95
  206.1 2.3 %shard_map.98 = f32[2,256,256]{2,1,0:T(8,128)} custom-call(f32[2,256,256]{2,1,0:T(8,128)} %get-tuple-element.46.probe, f32[1024,128]{1,0:T(8,128)} %bitcast.18, f32[8,128]{1,0:T(8,128)} %get-tuple-element.49.power), custom_call_target="tpu_custom_call" | custom-call | tf_op jit(solution)/shard_map/pallas_call | solution.py:329
  (41 shorter events, 8.9 us)
Async XLA Ops:
  2.5 19.7 %collective-permute-start = (f32[2,128,256]{2,1,0:T(8,128)}, f32[2,128,256]{2,1,0:T(8,128)S(1)}, u32[]{:S(2)}, u32[]{:S(2)}) collective-permute-start(f32[2,128,256]{2,1,0:T(8,128)} %get-tuple-element.26), channel_id=1, source_target_pairs={{8,0},{9,1},{10,2},{11,3},{12,4},{13,5},{14,6},{15,7},{16,8},{17,9... | collective-permute-start | bytes 786440 | tf_op jit(solution)/shard_map/ppermute | solution.py:33
  13.4 8.9 %collective-permute-start.1 = (f32[2,256,128]{2,1,0:T(8,128)}, f32[2,256,128]{2,1,0:T(8,128)S(1)}, u32[]{:S(2)}, u32[]{:S(2)}) collective-permute-start(f32[2,256,128]{2,1,0:T(8,128)} %get-tuple-element.27), channel_id=1, source_target_pairs={{1,0},{2,1},{3,2},{4,3},{5,4},{6,5},{7,6},{9,8},{10,9},{11,10},{12... | collective-permute-start | bytes 786440 | tf_op jit(solution)/shard_map/ppermute | solution.py:33
  15.3 7.0 %collective-permute-start.2 = (f32[2,128,128]{2,1,0:T(8,128)}, f32[2,128,128]{2,1,0:T(8,128)S(1)}, u32[]{:S(2)}, u32[]{:S(2)}) collective-permute-start(f32[2,128,128]{2,1,0:T(8,128)} %get-tuple-element.28), channel_id=1, source_target_pairs={{9,0},{10,1},{11,2},{12,3},{13,4},{14,5},{15,6},{17,8},{18,9},{19,... | collective-permute-start | bytes 393224 | tf_op jit(solution)/shard_map/ppermute | solution.py:33
  22.3 0.7 copy-start.11
  22.3 0.7 copy-start.2
  22.3 0.8 copy-start.3
  76.1 46.0 %all-to-all-start.2 = ((f32[512,2,128]{2,1,0:T(2,128)}), f32[512,2,128]{2,1,0:T(2,128)S(1)}, u32[]{:S(2)}, u32[]{:S(2)}) async-start(f32[512,2,128]{2,1,0:T(2,128)} %bitcast.22), calls=%async_computation.2 | async-start | bytes 1048576 | tf_op jit(solution)/shard_map/all_to_all | solution.py:53
  84.7 20.6 %collective-permute-start.3 = (f32[2,256,128]{2,1,0:T(8,128)}, f32[2,256,128]{2,1,0:T(8,128)S(1)}, u32[]{:S(2)}, u32[]{:S(2)}) collective-permute-start(f32[2,256,128]{2,1,0:T(8,128)} %get-tuple-element.31), channel_id=1, source_target_pairs={{0,1},{1,2},{2,3},{3,4},{4,5},{5,6},{6,7},{8,9},{9,10},{10,11},{11... | collective-permute-start | bytes 786440 | tf_op jit(solution)/shard_map/ppermute | solution.py:33
  86.7 18.6 %collective-permute-start.4 = (f32[2,128,256]{2,1,0:T(8,128)}, f32[2,128,256]{2,1,0:T(8,128)S(1)}, u32[]{:S(2)}, u32[]{:S(2)}) collective-permute-start(f32[2,128,256]{2,1,0:T(8,128)} %get-tuple-element.32), channel_id=1, source_target_pairs={{0,8},{1,9},{2,10},{3,11},{4,12},{5,13},{6,14},{7,15},{8,16},{9,17... | collective-permute-start | bytes 786440 | tf_op jit(solution)/shard_map/ppermute | solution.py:33
  90.1 15.2 %collective-permute-start.5 = (f32[2,128,128]{2,1,0:T(8,128)}, f32[2,128,128]{2,1,0:T(8,128)S(1)}, u32[]{:S(2)}, u32[]{:S(2)}) collective-permute-start(f32[2,128,128]{2,1,0:T(8,128)} %get-tuple-element.33), channel_id=1, source_target_pairs={{0,9},{1,10},{2,11},{3,12},{4,13},{5,14},{6,15},{8,17},{9,18},{10,... | collective-permute-start | bytes 393224 | tf_op jit(solution)/shard_map/ppermute | solution.py:33
  105.3 0.6 copy-start.10
  105.3 0.7 copy-start.4
  105.4 0.8 copy-start.5
  108.5 13.7 %collective-permute-start.6 = (f32[2,128,256]{2,1,0:T(8,128)}, f32[2,128,256]{2,1,0:T(8,128)S(1)}, u32[]{:S(2)}, u32[]{:S(2)}) collective-permute-start(f32[2,128,256]{2,1,0:T(8,128)} %get-tuple-element.35), channel_id=1, source_target_pairs={{8,0},{9,1},{10,2},{11,3},{12,4},{13,5},{14,6},{15,7},{16,8},{17,9... | collective-permute-start | bytes 786440 | tf_op jit(solution)/shard_map/ppermute | solution.py:33
  112.4 9.7 %collective-permute-start.7 = (f32[2,256,128]{2,1,0:T(8,128)}, f32[2,256,128]{2,1,0:T(8,128)S(1)}, u32[]{:S(2)}, u32[]{:S(2)}) collective-permute-start(f32[2,256,128]{2,1,0:T(8,128)} %get-tuple-element.36), channel_id=1, source_target_pairs={{1,0},{2,1},{3,2},{4,3},{5,4},{6,5},{7,6},{9,8},{10,9},{11,10},{12... | collective-permute-start | bytes 786440 | tf_op jit(solution)/shard_map/ppermute | solution.py:33
  114.6 7.5 %collective-permute-start.8 = (f32[2,128,128]{2,1,0:T(8,128)}, f32[2,128,128]{2,1,0:T(8,128)S(1)}, u32[]{:S(2)}, u32[]{:S(2)}) collective-permute-start(f32[2,128,128]{2,1,0:T(8,128)} %get-tuple-element.37), channel_id=1, source_target_pairs={{9,0},{10,1},{11,2},{12,3},{13,4},{14,5},{15,6},{17,8},{18,9},{19,... | collective-permute-start | bytes 393224 | tf_op jit(solution)/shard_map/ppermute | solution.py:33
  122.1 0.6 copy-start.13
  122.1 0.7 copy-start.8
  122.1 0.8 copy-start.9
  122.2 1.0 copy-start.1
  173.1 32.2 %all-to-all-start.5 = ((f32[512,2,128]{2,1,0:T(2,128)}), f32[512,2,128]{2,1,0:T(2,128)S(1)}, u32[]{:S(2)}, u32[]{:S(2)}) async-start(f32[512,2,128]{2,1,0:T(2,128)} %bitcast.23), calls=%async_computation.5 | async-start | bytes 1048576 | tf_op jit(solution)/shard_map/all_to_all | solution.py:53
  181.7 20.6 %collective-permute-start.9 = (f32[2,256,128]{2,1,0:T(8,128)}, f32[2,256,128]{2,1,0:T(8,128)S(1)}, u32[]{:S(2)}, u32[]{:S(2)}) collective-permute-start(f32[2,256,128]{2,1,0:T(8,128)} %get-tuple-element.43), channel_id=1, source_target_pairs={{0,1},{1,2},{2,3},{3,4},{4,5},{5,6},{6,7},{8,9},{9,10},{10,11},{11... | collective-permute-start | bytes 786440 | tf_op jit(solution)/shard_map/ppermute | solution.py:33
  183.7 18.6 %collective-permute-start.10 = (f32[2,128,256]{2,1,0:T(8,128)}, f32[2,128,256]{2,1,0:T(8,128)S(1)}, u32[]{:S(2)}, u32[]{:S(2)}) collective-permute-start(f32[2,128,256]{2,1,0:T(8,128)} %get-tuple-element.44), channel_id=1, source_target_pairs={{0,8},{1,9},{2,10},{3,11},{4,12},{5,13},{6,14},{7,15},{8,16},{9,17... | collective-permute-start | bytes 786440 | tf_op jit(solution)/shard_map/ppermute | solution.py:33
  187.1 15.2 %collective-permute-start.11 = (f32[2,128,128]{2,1,0:T(8,128)}, f32[2,128,128]{2,1,0:T(8,128)S(1)}, u32[]{:S(2)}, u32[]{:S(2)}) collective-permute-start(f32[2,128,128]{2,1,0:T(8,128)} %get-tuple-element.45), channel_id=1, source_target_pairs={{0,9},{1,10},{2,11},{3,12},{4,13},{5,14},{6,15},{8,17},{9,18},{10,... | collective-permute-start | bytes 393224 | tf_op jit(solution)/shard_map/ppermute | solution.py:33
  202.3 0.6 copy-start.12
  202.3 0.7 copy-start.6
  202.4 0.8 copy-start.7
  205.3 0.8 copy-start

commit v2 on v1

--- a/solution.py
+++ b/solution.py
@@ -7,6 +7,7 @@
 from jax.experimental import pallas as pl
 from jax.experimental.pallas import tpu as pltpu
 from jax.sharding import PartitionSpec as P
+
 
 HALO = 128
 SUB, LANE = 8, 128
@@ -36,8 +37,9 @@
 def device_groups(down, across):
     far = down // NEAR
     near_groups = [
-        [(y * NEAR + z) * across + c for z in range(NEAR) for c in range(across)]
+        [(y * NEAR + z) * across + x * 2 + core for z in range(NEAR) for x in range(across // 2)]
         for y in range(far)
+        for core in range(2)
     ]
     far_groups = [
         [(y * NEAR + z) * across + c for y in range(far)]
@@ -45,6 +47,11 @@
         for c in range(across)
     ]
     return near_groups, far_groups
+
+
+def swap_cores(value):
+    across = lax.axis_size("col")
+    return lax.ppermute(value, "col", [(c, c ^ 1) for c in range(across)])
 
 
 def exchange(rows, groups):
@@ -111,7 +118,7 @@
                 ]
 
 
-def halves(row, col):
+def halves(row):
     rest = jnp.bitwise_and(row, SUB - 1)
     base = pl.multiple_of(row - rest, SUB)
     at_row = lax.broadcasted_iota(jnp.int32, (1, SUB, LANE), 1)
@@ -120,7 +127,7 @@
 
 
 def take_window(ext, part, row, col, size):
-    rest, base, at_row, at_col = halves(row, col)
+    rest, base, at_row, at_col = halves(row)
     wide = ext[part, pl.ds(base, size + SUB), :]
     wide = wide.reshape(size // SUB + 1, SUB, wide.shape[1])
     turn_col = jnp.bitwise_and(LANE - col, LANE - 1)
@@ -139,7 +146,7 @@
 
 def add_window(ext, part, row, col, value):
     size = value.shape[0]
-    rest, base, at_row, at_col = halves(row, col)
+    rest, base, at_row, at_col = halves(row)
     turn_col = jnp.bitwise_and(col, LANE - 1)
     blocks = []
     for t in range(size // LANE):
@@ -163,11 +170,11 @@
 
 def solve_kernel(first, members, *refs):
     if first:
-        (offsets, counts, tile, low, right, corner, probe, amp, tables) = refs[:9]
-        message, terms, ext = refs[9:]
+        (offsets, marks, tile, low, right, corner, probe, amp, tables) = refs[:9]
+        keep, give, terms, ext = refs[9:]
     else:
-        (offsets, counts, tile, low, right, corner, probe, grad, power, amp, tables) = refs[:11]
-        message, terms, new_probe, ext = refs[11:]
+        (offsets, marks, tile, low, right, corner, probe, mine, other, power, amp, tables) = refs[:12]
+        keep, give, terms, new_probe, ext = refs[12:]
     size = tile.shape[1]
     half = size // 2
     slots = amp.shape[0]
@@ -181,7 +188,7 @@
         p_real = probe[0]
         p_imag = probe[1]
     else:
-        p_real, p_imag = moved_probe(probe, grad, power)
+        p_real, p_imag = moved_probe(marks, probe, mine, other, power)
         new_probe[0] = p_real
         new_probe[1] = p_imag
     mean = jnp.sum(p_real * p_real + p_imag * p_imag) / (size * size)
@@ -196,7 +203,7 @@
     for slot in range(slots):
         row = jnp.clip(offsets[slot, 0], 0, HALO)
         col = jnp.clip(offsets[slot, 1], 0, HALO)
-        live = slot < counts[0]
+        live = slot < marks[0]
         z_real = take_window(ext, 0, row, col, size)
         z_imag = take_window(ext, 1, row, col, size)
         psi_real = p_real * z_real - p_imag * z_imag
@@ -254,33 +261,37 @@
         window_power = jnp.sum(z_real * z_real + z_imag * z_imag)
         power_sum = power_sum + jnp.where(live, window_power, 0.0)
 
-    pieces = [pg_real[:, :half], pg_real[:, half:], pg_imag[:, :half], pg_imag[:, half:]]
-    per = 4 * size // members
-    for m in range(members):
-        source = pieces[m * per // size]
-        at = m * per % size
-        message[m * (per + 2) : m * (per + 2) + per, :] = source[at : at + per, :]
-        message[m * (per + 2) + per : (m + 1) * (per + 2), :] = jnp.full((2, half), power_sum)
-
-
-def moved_probe(probe, grad, power):
+    second = marks[1] == 1
+    per = 2 * size // members
+    for half_at in range(2):
+        columns = slice(half_at * half, (half_at + 1) * half)
+        kept = jnp.where(second, pg_imag[:, columns], pg_real[:, columns])
+        given = jnp.where(second, pg_real[:, columns], pg_imag[:, columns])
+        for m in range(members // 2):
+            at = (half_at * members // 2 + m) * (per + 2)
+            for ref, value in ((keep, kept), (give, given)):
+                ref[at : at + per, :] = value[m * per : (m + 1) * per, :]
+                ref[at + per : at + per + 2, :] = jnp.full((2, half), power_sum)
+
+
+def moved_probe(marks, probe, mine, other, power):
     size = probe.shape[1]
-    half = size // 2
+    second = marks[1] == 1
     factor = 1.0 / (power[0:1, 0:1] / (size * size) + tiny_value)
     p_real = probe[0]
     p_imag = probe[1]
-    g_real = jnp.concatenate([grad[:size, :], grad[size : 2 * size, :]], axis=1)
-    g_imag = jnp.concatenate([grad[2 * size : 3 * size, :], grad[3 * size :, :]], axis=1)
-    m_real = p_real + g_real * factor
-    m_imag = p_imag + g_imag * factor
+    one = jnp.concatenate([mine[:size, :], mine[size:, :]], axis=1)
+    two = jnp.concatenate([other[:size, :], other[size:, :]], axis=1)
+    m_real = p_real + jnp.where(second, two, one) * factor
+    m_imag = p_imag + jnp.where(second, one, two) * factor
     old = jnp.sum(p_real * p_real + p_imag * p_imag)
     new = jnp.sum(m_real * m_real + m_imag * m_imag)
     gain = jnp.sqrt(jnp.full((1, 1), old) / (jnp.full((1, 1), new) + tiny_value))
     return m_real * gain, m_imag * gain
 
 
-def probe_kernel(probe, grad, power, out):
-    real, imag = moved_probe(probe, grad, power)
+def probe_kernel(marks, probe, mine, other, power, out):
+    real, imag = moved_probe(marks, probe, mine, other, power)
     out[0] = real
     out[1] = imag
 
@@ -301,7 +312,6 @@
 
 
 def update_kernel(with_edges, partial, from_left, from_above, from_corner, out, *edges):
-    size = partial.shape[1]
     out[...] = partial[...]
     out[:, :, :HALO] += from_left[...]
     out[:, :HALO, :] += from_above[...]
@@ -325,14 +335,19 @@
         power[0][...] = jnp.broadcast_to(summed[n - 1 : n], power[0].shape)
 
 
-def call(kernel, outs, specs, *args, scratch=()):
+def call(kernel, outs, specs, *args, scratch=(), grant=6):
     return pl.pallas_call(
         kernel,
         out_shape=[jax.ShapeDtypeStruct(shape, jnp.float32) for shape in outs],
         in_specs=specs,
         out_specs=[VMEM] * len(outs),
         scratch_shapes=[pltpu.VMEM(shape, jnp.float32) for shape in scratch],
+        compiler_params=pltpu.CompilerParams(vmem_limit_bytes=grant << 20),
     )(*args)
+
+
+def halo(edges):
+    return shifted(edges[0], -1, 0), shifted(edges[1], 0, -1), shifted(edges[2], -1, -1)
 
 
 def shards(object_field, probe_field, amplitudes, offsets, counts):
@@ -343,12 +358,14 @@
     edge_shapes = [(2, margin, size), (2, size, margin), (2, margin, margin)]
     near_groups, far_groups = device_groups(lax.axis_size("row"), lax.axis_size("col"))
     near, far = len(near_groups[0]), len(far_groups[0])
-    per = 4 * size // near
+    per = 2 * size // near
+    held = near * (per + 2)
     tables = jnp.asarray(make_tables(size))
     order = np.concatenate([np.arange(0, size, 2), np.arange(1, size, 2)])
     pick = jnp.asarray(np.eye(size)[:, order].astype(jnp.bfloat16))
     spots = offsets.reshape(slots, 2)
-    live = counts.reshape(1)
+    core = jnp.bitwise_and(lax.axis_index("col"), 1).astype(jnp.int32)
+    marks = jnp.concatenate([counts.reshape(1), core.reshape(1)])
 
     current = object_field
     probe_now = probe_field
@@ -361,17 +378,15 @@
         pick,
         scratch=[(2 * slots, size, half)],
     )
-    grad = power = None
+    low, right, corner = halo(edges)
+    mine = other = power = None
     for outer_step in range(OUTER):
-        low = shifted(edges[0], -1, 0)
-        right = shifted(edges[1], 0, -1)
-        corner = shifted(edges[2], -1, -1)
         first = outer_step == 0
-        outs = [(near * (per + 2), half), (slots, 2, size, size)]
-        args = [spots, live, current, low, right, corner, probe_now]
+        outs = [(held, half), (held, half), (slots, 2, size, size)]
+        args = [spots, marks, current, low, right, corner, probe_now]
         if not first:
             outs.append((2, size, size))
-            args += [grad, power]
+            args += [mine, other, power]
         args += [amp, tables]
         done = call(
             functools.partial(solve_kernel, first, near),
@@ -379,11 +394,12 @@
             [SMEM, SMEM] + [VMEM] * (len(args) - 2),
             *args,
             scratch=[(2, size + margin + SUB, size + margin)],
-        )
-        message, terms = done[:2]
+            grant=14,
+        )
+        keep, give, terms = done[:3]
         if not first:
-            probe_now = done[2]
-        arrived = exchange(message, near_groups)
+            probe_now = done[3]
+        given = swap_cores(give)
         partial, rim_right, rim_low, rim_corner = call(
             place_kernel,
             [current.shape, edge_shapes[1], edge_shapes[0], edge_shapes[2]],
@@ -392,7 +408,9 @@
             current,
             terms,
             scratch=[(2, size + margin + SUB, size + margin)],
-        )
+            grant=6,
+        )
+        arrived = exchange(keep + given, near_groups)
         from_left = shifted(rim_right, 0, 1)
         from_above = shifted(rim_low, 1, 0)
         from_corner = shifted(rim_corner, 1, 1)
@@ -409,7 +427,8 @@
             [VMEM],
             arrived,
         )
-        grad = exchange(copies, near_groups)
+        mine = exchange(copies, near_groups)
+        other = swap_cores(mine)
         last = outer_step == OUTER - 1
         current, *edges = call(
             functools.partial(update_kernel, not last),
@@ -420,8 +439,17 @@
             from_above,
             from_corner,
         )
+        if not last:
+            low, right, corner = halo(edges)
     (probe_now,) = call(
-        probe_kernel, [probe_field.shape], [VMEM] * 3, probe_now, grad, power
+        probe_kernel,
+        [probe_field.shape],
+        [SMEM] + [VMEM] * 4,
+        marks,
+        probe_now,
+        mine,
+        other,
+        power,
     )
     return (current, probe_now)
 

time: 210 us -> 184 us (0.88)
  the two profiles are of different devices: /device:TPU:14 before, /device:TPU:9 now
where the time goes in v2:
time: 184 us; the launch traced here: 183 us
  starting transfers between devices  67.2 us (37%)
  blocking collectives  64.4 us (35%)
  waiting for transfers between devices  24 us (13%)
  Pallas kernels  15.1 us (8%)
  local copies, waits for them, and re-layouts  10.9 us (6%)
    all_to_all x4, blocking collectives, exchange(): lax.all_to_all(paired, ('row', 'col'), 0, 0, tiled=True, axis_index_group...  64.4 us
    ppermute x12, starting transfers between devices, shifted(): return lax.ppermute(value, ('row', 'col'), pairs)  47.1 us
    ppermute x12, waiting for transfers between devices, shifted(): return lax.ppermute(value, ('row', 'col'), pairs)  20.9 us
    pallas_call x13, Pallas kernels, call(): pl.pallas_call(kernel, out_shape=[jax.ShapeDtypeStruct(shape, jnp.float32...  15.1 us
    ppermute x4, starting transfers between devices, swap_cores(): return lax.ppermute(value, 'col', [(c, c ^ 1) for c in range(across)])  11 us
    unnamed x36, local copies, waits for them, and re-layouts  10.9 us
    all_to_all x2, starting transfers between devices, exchange(): lax.all_to_all(paired, ('row', 'col'), 0, 0, tiled=True, axis_index_group...  9.01 us
  transfers between devices with their start and end apart: 18, of which 6 were waited for; matrix products, arithmetic and copies ran while one was open for 0% of the time, Pallas kernels for 2%

profile of v2, /device:TPU:9, one launch (start us, length us, event | category | flops | bytes accessed | tf_op | source)
XLA Modules:
  0.0 183.3 jit_solution(2748718478251289316)
XLA Ops:
  1.7 10.7 %collective-permute-start = (f32[2,128,256]{2,1,0:T(8,128)S(1)}, f32[2,128,256]{2,1,0:T(8,128)S(1)}, u32[]{:S(2)}, u32[]{:S(2)}) collective-permute-start(f32[2,128,256]{2,1,0:T(8,128)S(1)} %get-tuple-element.28), channel_id=1, source_target_pairs={{8,0},{9,1},{10,2},{11,3},{12,4},{13,5},{14,6},{15,7},{16,8},{17,9... | collective-permute-start | bytes 786440 | tf_op jit(solution)/shard_map/ppermute | solution.py:34
  12.4 2.9 %collective-permute-start.1 = (f32[2,256,128]{2,1,0:T(8,128)S(1)}, f32[2,256,128]{2,1,0:T(8,128)S(1)}, u32[]{:S(2)}, u32[]{:S(2)}) collective-permute-start(f32[2,256,128]{2,1,0:T(8,128)S(1)} %get-tuple-element.29), channel_id=1, source_target_pairs={{1,0},{2,1},{3,2},{4,3},{5,4},{6,5},{7,6},{9,8},{10,9},{11,10},{12... | collective-permute-start | bytes 786440 | tf_op jit(solution)/shard_map/ppermute | solution.py:34
  15.3 1.9 %collective-permute-start.2 = (f32[2,128,128]{2,1,0:T(8,128)S(1)}, f32[2,128,128]{2,1,0:T(8,128)S(1)}, u32[]{:S(2)}, u32[]{:S(2)}) collective-permute-start(f32[2,128,128]{2,1,0:T(8,128)S(1)} %get-tuple-element.30), channel_id=1, source_target_pairs={{9,0},{10,1},{11,2},{12,3},{13,4},{14,5},{15,6},{17,8},{18,9},{19,... | collective-permute-start | bytes 393224 | tf_op jit(solution)/shard_map/ppermute | solution.py:34
  20.3 2.9 %collective-permute-done.2.refs_5_ = f32[2,128,128]{2,1,0:T(8,128)S(1)} collective-permute-done((f32[2,128,128]{2,1,0:T(8,128)S(1)}, f32[2,128,128]{2,1,0:T(8,128)S(1)}, u32[]{:S(2)}, u32[]{:S(2)}) %collective-permute-start.2) | collective-permute-done | bytes 131104 | tf_op jit(solution)/shard_map/ppermute | solution.py:34
  25.9 4.1 %shard_map.88 = (f32[576,128]{1,0:T(8,128)S(1)}, f32[576,128]{1,0:T(8,128)S(1)}, f32[2,2,256,256]{3,2,1,0:T(8,128)S(1)}) custom-call(s32[2,2]{1,0:T(2,128)S(1)} %bitcast.27, s32[2]{0:T(128)S(1)} %pad_add_fusion.refs_1_.marks, f32[2,256,256]{2,1,0:T(8,128)S(1)} %copy-done.1, f32[2,128,256]{2,1,0:T(8,128)S(1)} %collective-permute-done.refs_3_, ...), custom_call_target="tpu_custom_call" | custom-call | tf_op jit(solution)/shard_map/pallas_call | solution.py:339
  30.1 1.9 %collective-permute-start.9 = (f32[576,128]{1,0:T(8,128)S(1)}, f32[576,128]{1,0:T(8,128)S(1)}, u32[]{:S(2)}, u32[]{:S(2)}) collective-permute-start(f32[576,128]{1,0:T(8,128)S(1)} %get-tuple-element.41), channel_id=1, source_target_pairs={{0,1},{1,0},{2,3},{3,2},{4,5},{5,4},{6,7},{7,6},{8,9},{9,8},{10,11... | collective-permute-start | bytes 884744 | tf_op jit(solution)/shard_map/ppermute | solution.py:54
  32.0 1.5 collective-permute-done.9
  33.6 19.2 %all_to_all.30 = f32[288,2,128]{2,1,0:T(2,128)S(1)} all-to-all(f32[288,2,128]{2,1,0:T(2,128)S(1)} %bitcast.31), channel_id=1, replica_groups={{0,2,4,6,8,10,12,14,16,18,20,22,24,26,28,30,32,34,36,38,40,42,44,46,48,..., dimensions={0} | all-to-all | bytes 589824 | tf_op jit(solution)/shard_map/all_to_all | solution.py:60
  52.8 12.9 %all_to_all.31 = f32[72,2,128]{2,1,0:T(2,128)S(1)} all-to-all(f32[72,2,128]{2,1,0:T(2,128)S(1)} %bitcast.24), channel_id=1, replica_groups={{0,64,128,192,256,320,384,448},{1,65,129,193,257,321,385,449},{2,66,130..., dimensions={0} | all-to-all | bytes 147456 | tf_op jit(solution)/shard_map/all_to_all | solution.py:60
  66.5 4.6 %all-to-all-start.2 = ((f32[256,2,128]{2,1,0:T(2,128)}), f32[256,2,128]{2,1,0:T(2,128)S(1)}, u32[]{:S(2)}, u32[]{:S(2)}) async-start(f32[256,2,128]{2,1,0:T(2,128)} %bitcast.26), calls=%async_computation.2 | async-start | bytes 524288 | tf_op jit(solution)/shard_map/all_to_all | solution.py:60
  72.0 6.2 %collective-permute-start.3 = (f32[2,256,128]{2,1,0:T(8,128)S(1)}, f32[2,256,128]{2,1,0:T(8,128)S(1)}, u32[]{:S(2)}, u32[]{:S(2)}) collective-permute-start(f32[2,256,128]{2,1,0:T(8,128)S(1)} %get-tuple-element.33), channel_id=1, source_target_pairs={{0,1},{1,2},{2,3},{3,4},{4,5},{5,6},{6,7},{8,9},{9,10},{10,11},{11... | collective-permute-start | bytes 786440 | tf_op jit(solution)/shard_map/ppermute | solution.py:34
  78.3 3.1 %collective-permute-start.4 = (f32[2,128,256]{2,1,0:T(8,128)S(1)}, f32[2,128,256]{2,1,0:T(8,128)S(1)}, u32[]{:S(2)}, u32[]{:S(2)}) collective-permute-start(f32[2,128,256]{2,1,0:T(8,128)S(1)} %get-tuple-element.34), channel_id=1, source_target_pairs={{0,8},{1,9},{2,10},{3,11},{4,12},{5,13},{6,14},{7,15},{8,16},{9,17... | collective-permute-start | bytes 786440 | tf_op jit(solution)/shard_map/ppermute | solution.py:34
  81.4 3.1 %collective-permute-start.5 = (f32[2,128,128]{2,1,0:T(8,128)S(1)}, f32[2,128,128]{2,1,0:T(8,128)S(1)}, u32[]{:S(2)}, u32[]{:S(2)}) collective-permute-start(f32[2,128,128]{2,1,0:T(8,128)S(1)} %get-tuple-element.35), channel_id=1, source_target_pairs={{0,9},{1,10},{2,11},{3,12},{4,13},{5,14},{6,15},{8,17},{9,18},{10,... | collective-permute-start | bytes 393224 | tf_op jit(solution)/shard_map/ppermute | solution.py:34
  84.5 6.7 %collective-permute-done.5.from_corner = f32[2,128,128]{2,1,0:T(8,128)S(1)} collective-permute-done((f32[2,128,128]{2,1,0:T(8,128)S(1)}, f32[2,128,128]{2,1,0:T(8,128)S(1)}, u32[]{:S(2)}, u32[]{:S(2)}) %collective-permute-start.5) | collective-permute-done | bytes 131104 | tf_op jit(solution)/shard_map/ppermute | solution.py:34
  92.1 2.7 %collective-permute-start.6 = (f32[2,128,256]{2,1,0:T(8,128)}, f32[2,128,256]{2,1,0:T(8,128)S(1)}, u32[]{:S(2)}, u32[]{:S(2)}) collective-permute-start(f32[2,128,256]{2,1,0:T(8,128)} %get-tuple-element.37), channel_id=1, source_target_pairs={{8,0},{9,1},{10,2},{11,3},{12,4},{13,5},{14,6},{15,7},{16,8},{17,9... | collective-permute-start | bytes 786440 | tf_op jit(solution)/shard_map/ppermute | solution.py:34
  94.8 1.9 %collective-permute-start.7 = (f32[2,256,128]{2,1,0:T(8,128)}, f32[2,256,128]{2,1,0:T(8,128)S(1)}, u32[]{:S(2)}, u32[]{:S(2)}) collective-permute-start(f32[2,256,128]{2,1,0:T(8,128)} %get-tuple-element.38), channel_id=1, source_target_pairs={{1,0},{2,1},{3,2},{4,3},{5,4},{6,5},{7,6},{9,8},{10,9},{11,10},{12... | collective-permute-start | bytes 786440 | tf_op jit(solution)/shard_map/ppermute | solution.py:34
  96.7 1.9 %collective-permute-start.10 = (f32[512,128]{1,0:T(8,128)S(1)}, f32[512,128]{1,0:T(8,128)S(1)}, u32[]{:S(2)}, u32[]{:S(2)}) collective-permute-start(f32[512,128]{1,0:T(8,128)S(1)} %bitcast.20), channel_id=1, source_target_pairs={{0,1},{1,0},{2,3},{3,2},{4,5},{5,4},{6,7},{7,6},{8,9},{9,8},{10,11... | collective-permute-start | bytes 786440 | tf_op jit(solution)/shard_map/ppermute | solution.py:54
  98.7 3.4 %collective-permute-start.8 = (f32[2,128,128]{2,1,0:T(8,128)}, f32[2,128,128]{2,1,0:T(8,128)S(1)}, u32[]{:S(2)}, u32[]{:S(2)}) collective-permute-start(f32[2,128,128]{2,1,0:T(8,128)} %copy-done.17), channel_id=1, source_target_pairs={{9,0},{10,1},{11,2},{12,3},{13,4},{14,5},{15,6},{17,8},{18,9},{19,... | collective-permute-start | bytes 393224 | tf_op jit(solution)/shard_map/ppermute | solution.py:34
  102.1 4.9 %collective-permute-done.8.refs_5_ = f32[2,128,128]{2,1,0:T(8,128)S(1)} collective-permute-done((f32[2,128,128]{2,1,0:T(8,128)}, f32[2,128,128]{2,1,0:T(8,128)S(1)}, u32[]{:S(2)}, u32[]{:S(2)}) %collective-permute-start.8) | collective-permute-done | bytes 131104 | tf_op jit(solution)/shard_map/ppermute | solution.py:34
  110.4 4.3 %shard_map.93 = (f32[576,128]{1,0:T(8,128)S(1)}, f32[576,128]{1,0:T(8,128)S(1)}, f32[2,2,256,256]{3,2,1,0:T(8,128)S(1)}, f32[2,256,256]{2,1,0:T(8,128)S(1)}) custom-call(s32[2,2]{1,0:T(2,128)S(1)} %bitcast.29, s32[2]{0:T(128)S(1)} %pad_add_fusion.refs_1_.marks, f32[2,256,256]{2,1,0:T(8,128)S(1)} %get-tuple-element.36.refs_2_.tile, ...), custom_call_target="tpu_custom_call" | custom-call | tf_op jit(solution)/shard_map/pallas_call | solution.py:339
  114.7 1.9 %collective-permute-start.14 = (f32[576,128]{1,0:T(8,128)S(1)}, f32[576,128]{1,0:T(8,128)S(1)}, u32[]{:S(2)}, u32[]{:S(2)}) collective-permute-start(f32[576,128]{1,0:T(8,128)S(1)} %get-tuple-element.51), channel_id=1, source_target_pairs={{0,1},{1,0},{2,3},{3,2},{4,5},{5,4},{6,7},{7,6},{8,9},{9,8},{10,11... | collective-permute-start | bytes 884744 | tf_op jit(solution)/shard_map/ppermute | solution.py:54
  116.6 1.5 collective-permute-done.14
  118.2 22.5 %all_to_all.32 = f32[288,2,128]{2,1,0:T(2,128)S(1)} all-to-all(f32[288,2,128]{2,1,0:T(2,128)S(1)} %bitcast.32), channel_id=1, replica_groups={{0,2,4,6,8,10,12,14,16,18,20,22,24,26,28,30,32,34,36,38,40,42,44,46,48,..., dimensions={0} | all-to-all | bytes 589824 | tf_op jit(solution)/shard_map/all_to_all | solution.py:60
  140.8 9.7 %all_to_all.33 = f32[72,2,128]{2,1,0:T(2,128)S(1)} all-to-all(f32[72,2,128]{2,1,0:T(2,128)S(1)} %bitcast.25), channel_id=1, replica_groups={{0,64,128,192,256,320,384,448},{1,65,129,193,257,321,385,449},{2,66,130..., dimensions={0} | all-to-all | bytes 147456 | tf_op jit(solution)/shard_map/all_to_all | solution.py:60
  151.2 4.4 %all-to-all-start.5 = ((f32[256,2,128]{2,1,0:T(2,128)}), f32[256,2,128]{2,1,0:T(2,128)S(1)}, u32[]{:S(2)}, u32[]{:S(2)}) async-start(f32[256,2,128]{2,1,0:T(2,128)} %bitcast.13), calls=%async_computation.5 | async-start | bytes 524288 | tf_op jit(solution)/shard_map/all_to_all | solution.py:60
  155.7 1.2 copy-done.6
  157.9 6.0 %collective-permute-start.11 = (f32[2,256,128]{2,1,0:T(8,128)S(1)}, f32[2,256,128]{2,1,0:T(8,128)S(1)}, u32[]{:S(2)}, u32[]{:S(2)}) collective-permute-start(f32[2,256,128]{2,1,0:T(8,128)S(1)} %get-tuple-element.46), channel_id=1, source_target_pairs={{0,1},{1,2},{2,3},{3,4},{4,5},{5,6},{6,7},{8,9},{9,10},{10,11},{11... | collective-permute-start | bytes 786440 | tf_op jit(solution)/shard_map/ppermute | solution.py:34
  164.0 3.1 %collective-permute-start.12 = (f32[2,128,256]{2,1,0:T(8,128)S(1)}, f32[2,128,256]{2,1,0:T(8,128)S(1)}, u32[]{:S(2)}, u32[]{:S(2)}) collective-permute-start(f32[2,128,256]{2,1,0:T(8,128)S(1)} %get-tuple-element.47), channel_id=1, source_target_pairs={{0,8},{1,9},{2,10},{3,11},{4,12},{5,13},{6,14},{7,15},{8,16},{9,17... | collective-permute-start | bytes 786440 | tf_op jit(solution)/shard_map/ppermute | solution.py:34
  167.1 5.3 %collective-permute-start.15 = (f32[512,128]{1,0:T(8,128)S(1)}, f32[512,128]{1,0:T(8,128)S(1)}, u32[]{:S(2)}, u32[]{:S(2)}) collective-permute-start(f32[512,128]{1,0:T(8,128)S(1)} %bitcast.18), channel_id=1, source_target_pairs={{0,1},{1,0},{2,3},{3,2},{4,5},{5,4},{6,7},{7,6},{8,9},{9,8},{10,11... | collective-permute-start | bytes 786440 | tf_op jit(solution)/shard_map/ppermute | solution.py:54
  172.4 2.1 %collective-permute-start.13 = (f32[2,128,128]{2,1,0:T(8,128)S(1)}, f32[2,128,128]{2,1,0:T(8,128)S(1)}, u32[]{:S(2)}, u32[]{:S(2)}) collective-permute-start(f32[2,128,128]{2,1,0:T(8,128)S(1)} %get-tuple-element.48), channel_id=1, source_target_pairs={{0,9},{1,10},{2,11},{3,12},{4,13},{5,14},{6,15},{8,17},{9,18},{10,... | collective-permute-start | bytes 393224 | tf_op jit(solution)/shard_map/ppermute | solution.py:34
  174.5 6.3 %collective-permute-done.13.from_corner = f32[2,128,128]{2,1,0:T(8,128)S(1)} collective-permute-done((f32[2,128,128]{2,1,0:T(8,128)S(1)}, f32[2,128,128]{2,1,0:T(8,128)S(1)}, u32[]{:S(2)}, u32[]{:S(2)}) %collective-permute-start.13) | collective-permute-done | bytes 131104 | tf_op jit(solution)/shard_map/ppermute | solution.py:34
  181.6 1.7 shard_map.98
  (60 shorter events, 14.9 us)
Async XLA Ops:
  0.6 1.0 copy-start
  1.7 22.3 %copy-start.2 = (bf16[8,256,256]{2,1,0:T(8,128)(2,1)S(1)}, bf16[8,256,256]{2,1,0:T(8,128)(2,1)}, u32[]{:S(2)}) copy-start(bf16[8,256,256]{2,1,0:T(8,128)(2,1)} %constant.10.clone.refs_8_.refs_11_) | copy-start | bytes 3145732
  1.7 21.5 %collective-permute-start = (f32[2,128,256]{2,1,0:T(8,128)S(1)}, f32[2,128,256]{2,1,0:T(8,128)S(1)}, u32[]{:S(2)}, u32[]{:S(2)}) collective-permute-start(f32[2,128,256]{2,1,0:T(8,128)S(1)} %get-tuple-element.28), channel_id=1, source_target_pairs={{8,0},{9,1},{10,2},{11,3},{12,4},{13,5},{14,6},{15,7},{16,8},{17,9... | collective-permute-start | bytes 786440 | tf_op jit(solution)/shard_map/ppermute | solution.py:34
  12.4 10.8 %collective-permute-start.1 = (f32[2,256,128]{2,1,0:T(8,128)S(1)}, f32[2,256,128]{2,1,0:T(8,128)S(1)}, u32[]{:S(2)}, u32[]{:S(2)}) collective-permute-start(f32[2,256,128]{2,1,0:T(8,128)S(1)} %get-tuple-element.29), channel_id=1, source_target_pairs={{1,0},{2,1},{3,2},{4,3},{5,4},{6,5},{7,6},{9,8},{10,9},{11,10},{12... | collective-permute-start | bytes 786440 | tf_op jit(solution)/shard_map/ppermute | solution.py:34
  15.3 7.9 %collective-permute-start.2 = (f32[2,128,128]{2,1,0:T(8,128)S(1)}, f32[2,128,128]{2,1,0:T(8,128)S(1)}, u32[]{:S(2)}, u32[]{:S(2)}) collective-permute-start(f32[2,128,128]{2,1,0:T(8,128)S(1)} %get-tuple-element.30), channel_id=1, source_target_pairs={{9,0},{10,1},{11,2},{12,3},{13,4},{14,5},{15,6},{17,8},{18,9},{19,... | collective-permute-start | bytes 393224 | tf_op jit(solution)/shard_map/ppermute | solution.py:34
  17.9 1.0 copy-start.7
  18.9 0.9 copy-start.15
  19.8 4.1 %copy-start.1 = (f32[2,256,256]{2,1,0:T(8,128)S(1)}, f32[2,256,256]{2,1,0:T(8,128)}, u32[]{:S(2)}) copy-start(f32[2,256,256]{2,1,0:T(8,128)} %tile.3) | copy-start | bytes 1572868
  20.3 3.6 %copy-start.16 = (s32[1,1,2,2]{3,2,1,0:T(2,128)S(1)}, s32[1,1,2,2]{3,2,1,0:T(2,128)}, u32[]{:S(2)}) copy-start(s32[1,1,2,2]{3,2,1,0:T(2,128)} %param.10) | copy-start | bytes 52
  23.9 1.0 copy-start.3
  25.0 0.9 copy-start.9
  30.1 3.5 %collective-permute-start.9 = (f32[576,128]{1,0:T(8,128)S(1)}, f32[576,128]{1,0:T(8,128)S(1)}, u32[]{:S(2)}, u32[]{:S(2)}) collective-permute-start(f32[576,128]{1,0:T(8,128)S(1)} %get-tuple-element.41), channel_id=1, source_target_pairs={{0,1},{1,0},{2,3},{3,2},{4,5},{5,4},{6,7},{7,6},{8,9},{9,8},{10,11... | collective-permute-start | bytes 884744 | tf_op jit(solution)/shard_map/ppermute | solution.py:54
  66.5 30.3 %all-to-all-start.2 = ((f32[256,2,128]{2,1,0:T(2,128)}), f32[256,2,128]{2,1,0:T(2,128)S(1)}, u32[]{:S(2)}, u32[]{:S(2)}) async-start(f32[256,2,128]{2,1,0:T(2,128)} %bitcast.26), calls=%async_computation.2 | async-start | bytes 524288 | tf_op jit(solution)/shard_map/all_to_all | solution.py:60
  72.0 19.2 %collective-permute-start.3 = (f32[2,256,128]{2,1,0:T(8,128)S(1)}, f32[2,256,128]{2,1,0:T(8,128)S(1)}, u32[]{:S(2)}, u32[]{:S(2)}) collective-permute-start(f32[2,256,128]{2,1,0:T(8,128)S(1)} %get-tuple-element.33), channel_id=1, source_target_pairs={{0,1},{1,2},{2,3},{3,4},{4,5},{5,6},{6,7},{8,9},{9,10},{10,11},{11... | collective-permute-start | bytes 786440 | tf_op jit(solution)/shard_map/ppermute | solution.py:34
  78.3 13.0 %collective-permute-start.4 = (f32[2,128,256]{2,1,0:T(8,128)S(1)}, f32[2,128,256]{2,1,0:T(8,128)S(1)}, u32[]{:S(2)}, u32[]{:S(2)}) collective-permute-start(f32[2,128,256]{2,1,0:T(8,128)S(1)} %get-tuple-element.34), channel_id=1, source_target_pairs={{0,8},{1,9},{2,10},{3,11},{4,12},{5,13},{6,14},{7,15},{8,16},{9,17... | collective-permute-start | bytes 786440 | tf_op jit(solution)/shard_map/ppermute | solution.py:34
  81.4 9.9 %collective-permute-start.5 = (f32[2,128,128]{2,1,0:T(8,128)S(1)}, f32[2,128,128]{2,1,0:T(8,128)S(1)}, u32[]{:S(2)}, u32[]{:S(2)}) collective-permute-start(f32[2,128,128]{2,1,0:T(8,128)S(1)} %get-tuple-element.35), channel_id=1, source_target_pairs={{0,9},{1,10},{2,11},{3,12},{4,13},{5,14},{6,15},{8,17},{9,18},{10,... | collective-permute-start | bytes 393224 | tf_op jit(solution)/shard_map/ppermute | solution.py:34
  91.2 17.2 %copy-start.4 = (f32[2,256,256]{2,1,0:T(8,128)S(1)}, f32[2,256,256]{2,1,0:T(8,128)}, u32[]{:S(2)}) copy-start(f32[2,256,256]{2,1,0:T(8,128)} %refs_6_.3) | copy-start | bytes 1572868
  92.1 2.7 %copy-start.17 = (f32[2,128,128]{2,1,0:T(8,128)}, f32[2,128,128]{2,1,0:T(8,128)S(1)}, u32[]{:S(2)}) copy-start(f32[2,128,128]{2,1,0:T(8,128)S(1)} %get-tuple-element.39) | copy-start | bytes 393220
  92.1 14.9 %collective-permute-start.6 = (f32[2,128,256]{2,1,0:T(8,128)}, f32[2,128,256]{2,1,0:T(8,128)S(1)}, u32[]{:S(2)}, u32[]{:S(2)}) collective-permute-start(f32[2,128,256]{2,1,0:T(8,128)} %get-tuple-element.37), channel_id=1, source_target_pairs={{8,0},{9,1},{10,2},{11,3},{12,4},{13,5},{14,6},{15,7},{16,8},{17,9... | collective-permute-start | bytes 786440 | tf_op jit(solution)/shard_map/ppermute | solution.py:34
  94.8 13.0 %collective-permute-start.7 = (f32[2,256,128]{2,1,0:T(8,128)}, f32[2,256,128]{2,1,0:T(8,128)S(1)}, u32[]{:S(2)}, u32[]{:S(2)}) collective-permute-start(f32[2,256,128]{2,1,0:T(8,128)} %get-tuple-element.38), channel_id=1, source_target_pairs={{1,0},{2,1},{3,2},{4,3},{5,4},{6,5},{7,6},{9,8},{10,9},{11,10},{12... | collective-permute-start | bytes 786440 | tf_op jit(solution)/shard_map/ppermute | solution.py:34
  96.7 11.7 %collective-permute-start.10 = (f32[512,128]{1,0:T(8,128)S(1)}, f32[512,128]{1,0:T(8,128)S(1)}, u32[]{:S(2)}, u32[]{:S(2)}) collective-permute-start(f32[512,128]{1,0:T(8,128)S(1)} %bitcast.20), channel_id=1, source_target_pairs={{0,1},{1,0},{2,3},{3,2},{4,5},{5,4},{6,7},{7,6},{8,9},{9,8},{10,11... | collective-permute-start | bytes 786440 | tf_op jit(solution)/shard_map/ppermute | solution.py:54
  98.7 8.4 %collective-permute-start.8 = (f32[2,128,128]{2,1,0:T(8,128)}, f32[2,128,128]{2,1,0:T(8,128)S(1)}, u32[]{:S(2)}, u32[]{:S(2)}) collective-permute-start(f32[2,128,128]{2,1,0:T(8,128)} %copy-done.17), channel_id=1, source_target_pairs={{9,0},{10,1},{11,2},{12,3},{13,4},{14,5},{15,6},{17,8},{18,9},{19,... | collective-permute-start | bytes 393224 | tf_op jit(solution)/shard_map/ppermute | solution.py:34
  108.5 1.0 copy-start.12
  109.4 0.9 copy-start.14
  114.7 26.1 %copy-start.5 = (f32[2,2,256,256]{3,2,1,0:T(8,128)}, f32[2,2,256,256]{3,2,1,0:T(8,128)S(1)}, u32[]{:S(2)}) copy-start(f32[2,2,256,256]{3,2,1,0:T(8,128)S(1)} %get-tuple-element.44.terms) | copy-start | bytes 3145732
  114.7 3.5 %collective-permute-start.14 = (f32[576,128]{1,0:T(8,128)S(1)}, f32[576,128]{1,0:T(8,128)S(1)}, u32[]{:S(2)}, u32[]{:S(2)}) collective-permute-start(f32[576,128]{1,0:T(8,128)S(1)} %get-tuple-element.51), channel_id=1, source_target_pairs={{0,1},{1,0},{2,3},{3,2},{4,5},{5,4},{6,7},{7,6},{8,9},{9,8},{10,11... | collective-permute-start | bytes 884744 | tf_op jit(solution)/shard_map/ppermute | solution.py:54
  151.2 15.8 %all-to-all-start.5 = ((f32[256,2,128]{2,1,0:T(2,128)}), f32[256,2,128]{2,1,0:T(2,128)S(1)}, u32[]{:S(2)}, u32[]{:S(2)}) async-start(f32[256,2,128]{2,1,0:T(2,128)} %bitcast.13), calls=%async_computation.5 | async-start | bytes 524288 | tf_op jit(solution)/shard_map/all_to_all | solution.py:60
  155.7 1.2 copy-start.6
  157.9 22.8 %collective-permute-start.11 = (f32[2,256,128]{2,1,0:T(8,128)S(1)}, f32[2,256,128]{2,1,0:T(8,128)S(1)}, u32[]{:S(2)}, u32[]{:S(2)}) collective-permute-start(f32[2,256,128]{2,1,0:T(8,128)S(1)} %get-tuple-element.46), channel_id=1, source_target_pairs={{0,1},{1,2},{2,3},{3,4},{4,5},{5,6},{6,7},{8,9},{9,10},{10,11},{11... | collective-permute-start | bytes 786440 | tf_op jit(solution)/shard_map/ppermute | solution.py:34
  164.0 16.8 %collective-permute-start.12 = (f32[2,128,256]{2,1,0:T(8,128)S(1)}, f32[2,128,256]{2,1,0:T(8,128)S(1)}, u32[]{:S(2)}, u32[]{:S(2)}) collective-permute-start(f32[2,128,256]{2,1,0:T(8,128)S(1)} %get-tuple-element.47), channel_id=1, source_target_pairs={{0,8},{1,9},{2,10},{3,11},{4,12},{5,13},{6,14},{7,15},{8,16},{9,17... | collective-permute-start | bytes 786440 | tf_op jit(solution)/shard_map/ppermute | solution.py:34
  167.1 14.5 %collective-permute-start.15 = (f32[512,128]{1,0:T(8,128)S(1)}, f32[512,128]{1,0:T(8,128)S(1)}, u32[]{:S(2)}, u32[]{:S(2)}) collective-permute-start(f32[512,128]{1,0:T(8,128)S(1)} %bitcast.18), channel_id=1, source_target_pairs={{0,1},{1,0},{2,3},{3,2},{4,5},{5,4},{6,7},{7,6},{8,9},{9,8},{10,11... | collective-permute-start | bytes 786440 | tf_op jit(solution)/shard_map/ppermute | solution.py:54
  172.4 8.4 %collective-permute-start.13 = (f32[2,128,128]{2,1,0:T(8,128)S(1)}, f32[2,128,128]{2,1,0:T(8,128)S(1)}, u32[]{:S(2)}, u32[]{:S(2)}) collective-permute-start(f32[2,128,128]{2,1,0:T(8,128)S(1)} %get-tuple-element.48), channel_id=1, source_target_pairs={{0,9},{1,10},{2,11},{3,12},{4,13},{5,14},{6,15},{8,17},{9,18},{10,... | collective-permute-start | bytes 393224 | tf_op jit(solution)/shard_map/ppermute | solution.py:34
  (4 other events, 2.8 us)

commit v3 on v2

--- a/solution.py
+++ b/solution.py
@@ -100,9 +100,10 @@
     corner[...] = tile[:, :HALO, :HALO]
 
 
-def order_kernel(amplitudes, pick, out, held):
+def order_kernel(amplitudes, pick, probe, out, probe_out, held):
     slots, size, _ = amplitudes.shape
     half = size // 2
+    probe_out[...] = probe[...]
     for slot in range(slots):
         rest = amplitudes[slot]
         total = jnp.zeros((size, size), jnp.float32)
@@ -335,7 +336,7 @@
         power[0][...] = jnp.broadcast_to(summed[n - 1 : n], power[0].shape)
 
 
-def call(kernel, outs, specs, *args, scratch=(), grant=6):
+def call(kernel, outs, specs, *args, scratch=(), grant=2):
     return pl.pallas_call(
         kernel,
         out_shape=[jax.ShapeDtypeStruct(shape, jnp.float32) for shape in outs],
@@ -368,14 +369,14 @@
     marks = jnp.concatenate([counts.reshape(1), core.reshape(1)])
 
     current = object_field
-    probe_now = probe_field
     edges = call(edges_kernel, edge_shapes, [VMEM], current)
-    (amp,) = call(
+    amp, probe_now = call(
         order_kernel,
-        [amplitudes.shape],
-        [VMEM, VMEM],
+        [amplitudes.shape, probe_field.shape],
+        [VMEM] * 3,
         amplitudes,
         pick,
+        probe_field,
         scratch=[(2 * slots, size, half)],
     )
     low, right, corner = halo(edges)
@@ -394,7 +395,7 @@
             [SMEM, SMEM] + [VMEM] * (len(args) - 2),
             *args,
             scratch=[(2, size + margin + SUB, size + margin)],
-            grant=14,
+            grant=8,
         )
         keep, give, terms = done[:3]
         if not first:
@@ -408,12 +409,12 @@
             current,
             terms,
             scratch=[(2, size + margin + SUB, size + margin)],
-            grant=6,
-        )
-        arrived = exchange(keep + given, near_groups)
+            grant=3,
+        )
         from_left = shifted(rim_right, 0, 1)
         from_above = shifted(rim_low, 1, 0)
         from_corner = shifted(rim_corner, 1, 1)
+        arrived = exchange(keep + given, near_groups)
         (copies,) = call(
             functools.partial(fold_kernel, near, far, per + 2),
             [(far * (per + 2), half)],

time: 184 us -> 187 us (1.016)
  Pallas kernels: 15.1 us -> 17.4 us
    pallas_call x13, Pallas kernels: 15.1 us -> 17.4 us  [call(): pl.pallas_call(kernel, out_shape=[jax.ShapeDtypeStruct(shape, jnp.float32...]
    unnamed x36 -> x30, local copies, waits for them, and re-layouts: 10.9 us -> 11.2 us
  transfers between devices with their start and end apart: 18 -> 18, of which waited for: 6 -> 6; matrix products, arithmetic and copies ran while one was open for 0% -> 0% of each run, Pallas kernels for 2% -> 3%
where the time goes in v3:
time: 187 us; the launch traced here: 185 us
  starting transfers between devices  67.5 us (36%)
  blocking collectives  64.9 us (35%)
  waiting for transfers between devices  22.7 us (12%)
  Pallas kernels  17.4 us (9%)
  local copies, waits for them, and re-layouts  11.2 us (6%)
    all_to_all x4, blocking collectives, exchange(): lax.all_to_all(paired, ('row', 'col'), 0, 0, tiled=True, axis_index_group...  64.9 us
    ppermute x12, starting transfers between devices, shifted(): return lax.ppermute(value, ('row', 'col'), pairs)  46.8 us
    ppermute x12, waiting for transfers between devices, shifted(): return lax.ppermute(value, ('row', 'col'), pairs)  19.6 us
    pallas_call x13, Pallas kernels, call(): pl.pallas_call(kernel, out_shape=[jax.ShapeDtypeStruct(shape, jnp.float32...  17.4 us
    ppermute x4, starting transfers between devices, swap_cores(): return lax.ppermute(value, 'col', [(c, c ^ 1) for c in range(across)])  11.7 us
    unnamed x30, local copies, waits for them, and re-layouts  11.2 us
    all_to_all x2, starting transfers between devices, exchange(): lax.all_to_all(paired, ('row', 'col'), 0, 0, tiled=True, axis_index_group...  9 us
  transfers between devices with their start and end apart: 18, of which 6 were waited for; matrix products, arithmetic and copies ran while one was open for 0% of the time, Pallas kernels for 3%

profile of v3, /device:TPU:9, one launch (start us, length us, event | category | flops | bytes accessed | tf_op | source)
XLA Modules:
  0.0 185.4 jit_solution(16715760329591821802)
XLA Ops:
  2.5 10.5 %collective-permute-start = (f32[2,128,256]{2,1,0:T(8,128)}, f32[2,128,256]{2,1,0:T(8,128)S(1)}, u32[]{:S(2)}, u32[]{:S(2)}) collective-permute-start(f32[2,128,256]{2,1,0:T(8,128)} %get-tuple-element.30), channel_id=1, source_target_pairs={{8,0},{9,1},{10,2},{11,3},{12,4},{13,5},{14,6},{15,7},{16,8},{17,9... | collective-permute-start | bytes 786440 | tf_op jit(solution)/shard_map/ppermute | solution.py:34
  13.0 2.9 %collective-permute-start.1 = (f32[2,256,128]{2,1,0:T(8,128)}, f32[2,256,128]{2,1,0:T(8,128)S(1)}, u32[]{:S(2)}, u32[]{:S(2)}) collective-permute-start(f32[2,256,128]{2,1,0:T(8,128)} %get-tuple-element.31), channel_id=1, source_target_pairs={{1,0},{2,1},{3,2},{4,3},{5,4},{6,5},{7,6},{9,8},{10,9},{11,10},{12... | collective-permute-start | bytes 786440 | tf_op jit(solution)/shard_map/ppermute | solution.py:34
  15.9 1.9 %collective-permute-start.2 = (f32[2,128,128]{2,1,0:T(8,128)S(1)}, f32[2,128,128]{2,1,0:T(8,128)S(1)}, u32[]{:S(2)}, u32[]{:S(2)}) collective-permute-start(f32[2,128,128]{2,1,0:T(8,128)S(1)} %get-tuple-element.32), channel_id=1, source_target_pairs={{9,0},{10,1},{11,2},{12,3},{13,4},{14,5},{15,6},{17,8},{18,9},{19,... | collective-permute-start | bytes 393224 | tf_op jit(solution)/shard_map/ppermute | solution.py:34
  22.0 1.8 collective-permute-done.2.refs_5_
  24.5 4.1 %shard_map.88 = (f32[576,128]{1,0:T(8,128)S(1)}, f32[576,128]{1,0:T(8,128)S(1)}, f32[2,2,256,256]{3,2,1,0:T(8,128)S(1)}) custom-call(s32[2,2]{1,0:T(2,128)S(1)} %bitcast.26, s32[2]{0:T(128)S(1)} %pad_add_fusion.refs_1_.marks, f32[2,256,256]{2,1,0:T(8,128)S(1)} %copy-done.1, f32[2,128,256]{2,1,0:T(8,128)S(1)} %collective-permute-done.refs_3_, ...), custom_call_target="tpu_custom_call" | custom-call | tf_op jit(solution)/shard_map/pallas_call | solution.py:340
  29.6 1.9 %collective-permute-start.9 = (f32[576,128]{1,0:T(8,128)S(1)}, f32[576,128]{1,0:T(8,128)S(1)}, u32[]{:S(2)}, u32[]{:S(2)}) collective-permute-start(f32[576,128]{1,0:T(8,128)S(1)} %get-tuple-element.45), channel_id=1, source_target_pairs={{0,1},{1,0},{2,3},{3,2},{4,5},{5,4},{6,7},{7,6},{8,9},{9,8},{10,11... | collective-permute-start | bytes 884744 | tf_op jit(solution)/shard_map/ppermute | solution.py:54
  31.6 1.5 collective-permute-done.9
  33.1 19.4 %all_to_all.30 = f32[288,2,128]{2,1,0:T(2,128)S(1)} all-to-all(f32[288,2,128]{2,1,0:T(2,128)S(1)} %bitcast.30), channel_id=1, replica_groups={{0,2,4,6,8,10,12,14,16,18,20,22,24,26,28,30,32,34,36,38,40,42,44,46,48,..., dimensions={0} | all-to-all | bytes 589824 | tf_op jit(solution)/shard_map/all_to_all | solution.py:60
  52.6 12.9 %all_to_all.31 = f32[72,2,128]{2,1,0:T(2,128)S(1)} all-to-all(f32[72,2,128]{2,1,0:T(2,128)S(1)} %bitcast.24), channel_id=1, replica_groups={{0,64,128,192,256,320,384,448},{1,65,129,193,257,321,385,449},{2,66,130..., dimensions={0} | all-to-all | bytes 147456 | tf_op jit(solution)/shard_map/all_to_all | solution.py:60
  66.3 4.6 %all-to-all-start.2 = ((f32[256,2,128]{2,1,0:T(2,128)}), f32[256,2,128]{2,1,0:T(2,128)S(1)}, u32[]{:S(2)}, u32[]{:S(2)}) async-start(f32[256,2,128]{2,1,0:T(2,128)} %bitcast.7), calls=%async_computation.2 | async-start | bytes 524288 | tf_op jit(solution)/shard_map/all_to_all | solution.py:60
  73.1 6.2 %collective-permute-start.3 = (f32[2,256,128]{2,1,0:T(8,128)S(1)}, f32[2,256,128]{2,1,0:T(8,128)S(1)}, u32[]{:S(2)}, u32[]{:S(2)}) collective-permute-start(f32[2,256,128]{2,1,0:T(8,128)S(1)} %get-tuple-element.37), channel_id=1, source_target_pairs={{0,1},{1,2},{2,3},{3,4},{4,5},{5,6},{6,7},{8,9},{9,10},{10,11},{11... | collective-permute-start | bytes 786440 | tf_op jit(solution)/shard_map/ppermute | solution.py:34
  79.3 3.1 %collective-permute-start.4 = (f32[2,128,256]{2,1,0:T(8,128)S(1)}, f32[2,128,256]{2,1,0:T(8,128)S(1)}, u32[]{:S(2)}, u32[]{:S(2)}) collective-permute-start(f32[2,128,256]{2,1,0:T(8,128)S(1)} %get-tuple-element.38), channel_id=1, source_target_pairs={{0,8},{1,9},{2,10},{3,11},{4,12},{5,13},{6,14},{7,15},{8,16},{9,17... | collective-permute-start | bytes 786440 | tf_op jit(solution)/shard_map/ppermute | solution.py:34
  82.4 3.1 %collective-permute-start.5 = (f32[2,128,128]{2,1,0:T(8,128)S(1)}, f32[2,128,128]{2,1,0:T(8,128)S(1)}, u32[]{:S(2)}, u32[]{:S(2)}) collective-permute-start(f32[2,128,128]{2,1,0:T(8,128)S(1)} %get-tuple-element.39), channel_id=1, source_target_pairs={{0,9},{1,10},{2,11},{3,12},{4,13},{5,14},{6,15},{8,17},{9,18},{10,... | collective-permute-start | bytes 393224 | tf_op jit(solution)/shard_map/ppermute | solution.py:34
  85.5 6.7 %collective-permute-done.5.from_corner = f32[2,128,128]{2,1,0:T(8,128)S(1)} collective-permute-done((f32[2,128,128]{2,1,0:T(8,128)S(1)}, f32[2,128,128]{2,1,0:T(8,128)S(1)}, u32[]{:S(2)}, u32[]{:S(2)}) %collective-permute-start.5) | collective-permute-done | bytes 131104 | tf_op jit(solution)/shard_map/ppermute | solution.py:34
  93.1 2.7 %collective-permute-start.6 = (f32[2,128,256]{2,1,0:T(8,128)}, f32[2,128,256]{2,1,0:T(8,128)S(1)}, u32[]{:S(2)}, u32[]{:S(2)}) collective-permute-start(f32[2,128,256]{2,1,0:T(8,128)} %get-tuple-element.41), channel_id=1, source_target_pairs={{8,0},{9,1},{10,2},{11,3},{12,4},{13,5},{14,6},{15,7},{16,8},{17,9... | collective-permute-start | bytes 786440 | tf_op jit(solution)/shard_map/ppermute | solution.py:34
  95.8 1.9 %collective-permute-start.7 = (f32[2,256,128]{2,1,0:T(8,128)}, f32[2,256,128]{2,1,0:T(8,128)S(1)}, u32[]{:S(2)}, u32[]{:S(2)}) collective-permute-start(f32[2,256,128]{2,1,0:T(8,128)} %get-tuple-element.42), channel_id=1, source_target_pairs={{1,0},{2,1},{3,2},{4,3},{5,4},{6,5},{7,6},{9,8},{10,9},{11,10},{12... | collective-permute-start | bytes 786440 | tf_op jit(solution)/shard_map/ppermute | solution.py:34
  97.7 1.9 %collective-permute-start.10 = (f32[512,128]{1,0:T(8,128)S(1)}, f32[512,128]{1,0:T(8,128)S(1)}, u32[]{:S(2)}, u32[]{:S(2)}) collective-permute-start(f32[512,128]{1,0:T(8,128)S(1)} %bitcast.20), channel_id=1, source_target_pairs={{0,1},{1,0},{2,3},{3,2},{4,5},{5,4},{6,7},{7,6},{8,9},{9,8},{10,11... | collective-permute-start | bytes 786440 | tf_op jit(solution)/shard_map/ppermute | solution.py:54
  99.6 3.4 %collective-permute-start.8 = (f32[2,128,128]{2,1,0:T(8,128)S(1)}, f32[2,128,128]{2,1,0:T(8,128)S(1)}, u32[]{:S(2)}, u32[]{:S(2)}) collective-permute-start(f32[2,128,128]{2,1,0:T(8,128)S(1)} %get-tuple-element.43), channel_id=1, source_target_pairs={{9,0},{10,1},{11,2},{12,3},{13,4},{14,5},{15,6},{17,8},{18,9},{19,... | collective-permute-start | bytes 393224 | tf_op jit(solution)/shard_map/ppermute | solution.py:34
  103.1 4.6 %collective-permute-done.8.refs_5_ = f32[2,128,128]{2,1,0:T(8,128)S(1)} collective-permute-done((f32[2,128,128]{2,1,0:T(8,128)S(1)}, f32[2,128,128]{2,1,0:T(8,128)S(1)}, u32[]{:S(2)}, u32[]{:S(2)}) %collective-permute-start.8) | collective-permute-done | bytes 131104 | tf_op jit(solution)/shard_map/ppermute | solution.py:34
  111.0 4.3 %shard_map.93 = (f32[576,128]{1,0:T(8,128)S(1)}, f32[576,128]{1,0:T(8,128)S(1)}, f32[2,2,256,256]{3,2,1,0:T(8,128)S(1)}, f32[2,256,256]{2,1,0:T(8,128)S(1)}) custom-call(s32[2,2]{1,0:T(2,128)S(1)} %bitcast.28, s32[2]{0:T(128)S(1)} %pad_add_fusion.refs_1_.marks, f32[2,256,256]{2,1,0:T(8,128)S(1)} %get-tuple-element.40.refs_2_.tile, ...), custom_call_target="tpu_custom_call" | custom-call | tf_op jit(solution)/shard_map/pallas_call | solution.py:340
  116.3 1.9 %collective-permute-start.14 = (f32[576,128]{1,0:T(8,128)S(1)}, f32[576,128]{1,0:T(8,128)S(1)}, u32[]{:S(2)}, u32[]{:S(2)}) collective-permute-start(f32[576,128]{1,0:T(8,128)S(1)} %get-tuple-element.55), channel_id=1, source_target_pairs={{0,1},{1,0},{2,3},{3,2},{4,5},{5,4},{6,7},{7,6},{8,9},{9,8},{10,11... | collective-permute-start | bytes 884744 | tf_op jit(solution)/shard_map/ppermute | solution.py:54
  118.3 1.5 collective-permute-done.14
  119.9 22.8 %all_to_all.32 = f32[288,2,128]{2,1,0:T(2,128)S(1)} all-to-all(f32[288,2,128]{2,1,0:T(2,128)S(1)} %bitcast.31), channel_id=1, replica_groups={{0,2,4,6,8,10,12,14,16,18,20,22,24,26,28,30,32,34,36,38,40,42,44,46,48,..., dimensions={0} | all-to-all | bytes 589824 | tf_op jit(solution)/shard_map/all_to_all | solution.py:60
  142.7 9.7 %all_to_all.33 = f32[72,2,128]{2,1,0:T(2,128)S(1)} all-to-all(f32[72,2,128]{2,1,0:T(2,128)S(1)} %bitcast.25), channel_id=1, replica_groups={{0,64,128,192,256,320,384,448},{1,65,129,193,257,321,385,449},{2,66,130..., dimensions={0} | all-to-all | bytes 147456 | tf_op jit(solution)/shard_map/all_to_all | solution.py:60
  153.1 4.4 %all-to-all-start.5 = ((f32[256,2,128]{2,1,0:T(2,128)}), f32[256,2,128]{2,1,0:T(2,128)S(1)}, u32[]{:S(2)}, u32[]{:S(2)}) async-start(f32[256,2,128]{2,1,0:T(2,128)} %bitcast.13), calls=%async_computation.5 | async-start | bytes 524288 | tf_op jit(solution)/shard_map/all_to_all | solution.py:60
  157.6 1.8 shard_map.94
  159.4 6.0 %collective-permute-start.11 = (f32[2,256,128]{2,1,0:T(8,128)}, f32[2,256,128]{2,1,0:T(8,128)S(1)}, u32[]{:S(2)}, u32[]{:S(2)}) collective-permute-start(f32[2,256,128]{2,1,0:T(8,128)} %get-tuple-element.50), channel_id=1, source_target_pairs={{0,1},{1,2},{2,3},{3,4},{4,5},{5,6},{6,7},{8,9},{9,10},{10,11},{11... | collective-permute-start | bytes 786440 | tf_op jit(solution)/shard_map/ppermute | solution.py:34
  165.4 3.1 %collective-permute-start.12 = (f32[2,128,256]{2,1,0:T(8,128)}, f32[2,128,256]{2,1,0:T(8,128)S(1)}, u32[]{:S(2)}, u32[]{:S(2)}) collective-permute-start(f32[2,128,256]{2,1,0:T(8,128)} %get-tuple-element.51), channel_id=1, source_target_pairs={{0,8},{1,9},{2,10},{3,11},{4,12},{5,13},{6,14},{7,15},{8,16},{9,17... | collective-permute-start | bytes 786440 | tf_op jit(solution)/shard_map/ppermute | solution.py:34
  168.5 5.9 %collective-permute-start.15 = (f32[512,128]{1,0:T(8,128)S(1)}, f32[512,128]{1,0:T(8,128)S(1)}, u32[]{:S(2)}, u32[]{:S(2)}) collective-permute-start(f32[512,128]{1,0:T(8,128)S(1)} %bitcast.18), channel_id=1, source_target_pairs={{0,1},{1,0},{2,3},{3,2},{4,5},{5,4},{6,7},{7,6},{8,9},{9,8},{10,11... | collective-permute-start | bytes 786440 | tf_op jit(solution)/shard_map/ppermute | solution.py:54
  174.5 1.9 %collective-permute-start.13 = (f32[2,128,128]{2,1,0:T(8,128)S(1)}, f32[2,128,128]{2,1,0:T(8,128)S(1)}, u32[]{:S(2)}, u32[]{:S(2)}) collective-permute-start(f32[2,128,128]{2,1,0:T(8,128)S(1)} %get-tuple-element.52), channel_id=1, source_target_pairs={{0,9},{1,10},{2,11},{3,12},{4,13},{5,14},{6,15},{8,17},{9,18},{10,... | collective-permute-start | bytes 393224 | tf_op jit(solution)/shard_map/ppermute | solution.py:34
  176.4 6.5 %collective-permute-done.13.from_corner = f32[2,128,128]{2,1,0:T(8,128)S(1)} collective-permute-done((f32[2,128,128]{2,1,0:T(8,128)S(1)}, f32[2,128,128]{2,1,0:T(8,128)S(1)}, u32[]{:S(2)}, u32[]{:S(2)}) %collective-permute-start.13) | collective-permute-done | bytes 131104 | tf_op jit(solution)/shard_map/ppermute | solution.py:34
  183.7 1.7 shard_map.98
  (54 shorter events, 16.9 us)
Async XLA Ops:
  0.6 1.0 copy-start
  1.7 22.2 %copy-start.2 = (bf16[8,256,256]{2,1,0:T(8,128)(2,1)S(1)}, bf16[8,256,256]{2,1,0:T(8,128)(2,1)}, u32[]{:S(2)}) copy-start(bf16[8,256,256]{2,1,0:T(8,128)(2,1)} %constant.10.clone.refs_8_.refs_11_) | copy-start | bytes 3145732
  2.5 21.4 %collective-permute-start = (f32[2,128,256]{2,1,0:T(8,128)}, f32[2,128,256]{2,1,0:T(8,128)S(1)}, u32[]{:S(2)}, u32[]{:S(2)}) collective-permute-start(f32[2,128,256]{2,1,0:T(8,128)} %get-tuple-element.30), channel_id=1, source_target_pairs={{8,0},{9,1},{10,2},{11,3},{12,4},{13,5},{14,6},{15,7},{16,8},{17,9... | collective-permute-start | bytes 786440 | tf_op jit(solution)/shard_map/ppermute | solution.py:34
  13.0 10.8 %collective-permute-start.1 = (f32[2,256,128]{2,1,0:T(8,128)}, f32[2,256,128]{2,1,0:T(8,128)S(1)}, u32[]{:S(2)}, u32[]{:S(2)}) collective-permute-start(f32[2,256,128]{2,1,0:T(8,128)} %get-tuple-element.31), channel_id=1, source_target_pairs={{1,0},{2,1},{3,2},{4,3},{5,4},{6,5},{7,6},{9,8},{10,9},{11,10},{12... | collective-permute-start | bytes 786440 | tf_op jit(solution)/shard_map/ppermute | solution.py:34
  15.9 7.9 %collective-permute-start.2 = (f32[2,128,128]{2,1,0:T(8,128)S(1)}, f32[2,128,128]{2,1,0:T(8,128)S(1)}, u32[]{:S(2)}, u32[]{:S(2)}) collective-permute-start(f32[2,128,128]{2,1,0:T(8,128)S(1)} %get-tuple-element.32), channel_id=1, source_target_pairs={{9,0},{10,1},{11,2},{12,3},{13,4},{14,5},{15,6},{17,8},{18,9},{19,... | collective-permute-start | bytes 393224 | tf_op jit(solution)/shard_map/ppermute | solution.py:34
  18.5 1.0 copy-start.7
  19.5 1.0 copy-start.8
  20.6 0.9 copy-start.13
  21.5 2.4 %copy-start.1 = (f32[2,256,256]{2,1,0:T(8,128)S(1)}, f32[2,256,256]{2,1,0:T(8,128)}, u32[]{:S(2)}) copy-start(f32[2,256,256]{2,1,0:T(8,128)} %tile.3) | copy-start | bytes 1572868
  28.7 1.0 copy-start.5
  29.6 3.5 %collective-permute-start.9 = (f32[576,128]{1,0:T(8,128)S(1)}, f32[576,128]{1,0:T(8,128)S(1)}, u32[]{:S(2)}, u32[]{:S(2)}) collective-permute-start(f32[576,128]{1,0:T(8,128)S(1)} %get-tuple-element.45), channel_id=1, source_target_pairs={{0,1},{1,0},{2,3},{3,2},{4,5},{5,4},{6,7},{7,6},{8,9},{9,8},{10,11... | collective-permute-start | bytes 884744 | tf_op jit(solution)/shard_map/ppermute | solution.py:54
  66.3 31.5 %all-to-all-start.2 = ((f32[256,2,128]{2,1,0:T(2,128)}), f32[256,2,128]{2,1,0:T(2,128)S(1)}, u32[]{:S(2)}, u32[]{:S(2)}) async-start(f32[256,2,128]{2,1,0:T(2,128)} %bitcast.7), calls=%async_computation.2 | async-start | bytes 524288 | tf_op jit(solution)/shard_map/all_to_all | solution.py:60
  70.8 1.2 copy-start.6
  73.1 19.1 %collective-permute-start.3 = (f32[2,256,128]{2,1,0:T(8,128)S(1)}, f32[2,256,128]{2,1,0:T(8,128)S(1)}, u32[]{:S(2)}, u32[]{:S(2)}) collective-permute-start(f32[2,256,128]{2,1,0:T(8,128)S(1)} %get-tuple-element.37), channel_id=1, source_target_pairs={{0,1},{1,2},{2,3},{3,4},{4,5},{5,6},{6,7},{8,9},{9,10},{10,11},{11... | collective-permute-start | bytes 786440 | tf_op jit(solution)/shard_map/ppermute | solution.py:34
  79.3 12.9 %collective-permute-start.4 = (f32[2,128,256]{2,1,0:T(8,128)S(1)}, f32[2,128,256]{2,1,0:T(8,128)S(1)}, u32[]{:S(2)}, u32[]{:S(2)}) collective-permute-start(f32[2,128,256]{2,1,0:T(8,128)S(1)} %get-tuple-element.38), channel_id=1, source_target_pairs={{0,8},{1,9},{2,10},{3,11},{4,12},{5,13},{6,14},{7,15},{8,16},{9,17... | collective-permute-start | bytes 786440 | tf_op jit(solution)/shard_map/ppermute | solution.py:34
  82.4 9.8 %collective-permute-start.5 = (f32[2,128,128]{2,1,0:T(8,128)S(1)}, f32[2,128,128]{2,1,0:T(8,128)S(1)}, u32[]{:S(2)}, u32[]{:S(2)}) collective-permute-start(f32[2,128,128]{2,1,0:T(8,128)S(1)} %get-tuple-element.39), channel_id=1, source_target_pairs={{0,9},{1,10},{2,11},{3,12},{4,13},{5,14},{6,15},{8,17},{9,18},{10,... | collective-permute-start | bytes 393224 | tf_op jit(solution)/shard_map/ppermute | solution.py:34
  93.1 14.6 %collective-permute-start.6 = (f32[2,128,256]{2,1,0:T(8,128)}, f32[2,128,256]{2,1,0:T(8,128)S(1)}, u32[]{:S(2)}, u32[]{:S(2)}) collective-permute-start(f32[2,128,256]{2,1,0:T(8,128)} %get-tuple-element.41), channel_id=1, source_target_pairs={{8,0},{9,1},{10,2},{11,3},{12,4},{13,5},{14,6},{15,7},{16,8},{17,9... | collective-permute-start | bytes 786440 | tf_op jit(solution)/shard_map/ppermute | solution.py:34
  95.8 12.6 %collective-permute-start.7 = (f32[2,256,128]{2,1,0:T(8,128)}, f32[2,256,128]{2,1,0:T(8,128)S(1)}, u32[]{:S(2)}, u32[]{:S(2)}) collective-permute-start(f32[2,256,128]{2,1,0:T(8,128)} %get-tuple-element.42), channel_id=1, source_target_pairs={{1,0},{2,1},{3,2},{4,3},{5,4},{6,5},{7,6},{9,8},{10,9},{11,10},{12... | collective-permute-start | bytes 786440 | tf_op jit(solution)/shard_map/ppermute | solution.py:34
  97.7 11.4 %collective-permute-start.10 = (f32[512,128]{1,0:T(8,128)S(1)}, f32[512,128]{1,0:T(8,128)S(1)}, u32[]{:S(2)}, u32[]{:S(2)}) collective-permute-start(f32[512,128]{1,0:T(8,128)S(1)} %bitcast.20), channel_id=1, source_target_pairs={{0,1},{1,0},{2,3},{3,2},{4,5},{5,4},{6,7},{7,6},{8,9},{9,8},{10,11... | collective-permute-start | bytes 786440 | tf_op jit(solution)/shard_map/ppermute | solution.py:54
  99.6 8.0 %collective-permute-start.8 = (f32[2,128,128]{2,1,0:T(8,128)S(1)}, f32[2,128,128]{2,1,0:T(8,128)S(1)}, u32[]{:S(2)}, u32[]{:S(2)}) collective-permute-start(f32[2,128,128]{2,1,0:T(8,128)S(1)} %get-tuple-element.43), channel_id=1, source_target_pairs={{9,0},{10,1},{11,2},{12,3},{13,4},{14,5},{15,6},{17,8},{18,9},{19,... | collective-permute-start | bytes 393224 | tf_op jit(solution)/shard_map/ppermute | solution.py:34
  107.7 0.7 copy-start.9
  108.4 0.7 copy-start.11
  109.1 1.0 copy-start.10
  110.1 0.9 copy-start.12
  115.3 1.0 copy-start.3
  116.3 3.5 %collective-permute-start.14 = (f32[576,128]{1,0:T(8,128)S(1)}, f32[576,128]{1,0:T(8,128)S(1)}, u32[]{:S(2)}, u32[]{:S(2)}) collective-permute-start(f32[576,128]{1,0:T(8,128)S(1)} %get-tuple-element.55), channel_id=1, source_target_pairs={{0,1},{1,0},{2,3},{3,2},{4,5},{5,4},{6,7},{7,6},{8,9},{9,8},{10,11... | collective-permute-start | bytes 884744 | tf_op jit(solution)/shard_map/ppermute | solution.py:54
  119.8 37.7 %copy-start.4 = (f32[2,2,256,256]{3,2,1,0:T(8,128)S(1)}, f32[2,2,256,256]{3,2,1,0:T(8,128)}, u32[]{:S(2)}) copy-start(f32[2,2,256,256]{3,2,1,0:T(8,128)} %copy-done.3) | copy-start | bytes 3145732
  153.1 15.4 %all-to-all-start.5 = ((f32[256,2,128]{2,1,0:T(2,128)}), f32[256,2,128]{2,1,0:T(2,128)S(1)}, u32[]{:S(2)}, u32[]{:S(2)}) async-start(f32[256,2,128]{2,1,0:T(2,128)} %bitcast.13), calls=%async_computation.5 | async-start | bytes 524288 | tf_op jit(solution)/shard_map/all_to_all | solution.py:60
  159.4 23.5 %collective-permute-start.11 = (f32[2,256,128]{2,1,0:T(8,128)}, f32[2,256,128]{2,1,0:T(8,128)S(1)}, u32[]{:S(2)}, u32[]{:S(2)}) collective-permute-start(f32[2,256,128]{2,1,0:T(8,128)} %get-tuple-element.50), channel_id=1, source_target_pairs={{0,1},{1,2},{2,3},{3,4},{4,5},{5,6},{6,7},{8,9},{9,10},{10,11},{11... | collective-permute-start | bytes 786440 | tf_op jit(solution)/shard_map/ppermute | solution.py:34
  165.4 17.5 %collective-permute-start.12 = (f32[2,128,256]{2,1,0:T(8,128)}, f32[2,128,256]{2,1,0:T(8,128)S(1)}, u32[]{:S(2)}, u32[]{:S(2)}) collective-permute-start(f32[2,128,256]{2,1,0:T(8,128)} %get-tuple-element.51), channel_id=1, source_target_pairs={{0,8},{1,9},{2,10},{3,11},{4,12},{5,13},{6,14},{7,15},{8,16},{9,17... | collective-permute-start | bytes 786440 | tf_op jit(solution)/shard_map/ppermute | solution.py:34
  168.5 15.2 %collective-permute-start.15 = (f32[512,128]{1,0:T(8,128)S(1)}, f32[512,128]{1,0:T(8,128)S(1)}, u32[]{:S(2)}, u32[]{:S(2)}) collective-permute-start(f32[512,128]{1,0:T(8,128)S(1)} %bitcast.18), channel_id=1, source_target_pairs={{0,1},{1,0},{2,3},{3,2},{4,5},{5,4},{6,7},{7,6},{8,9},{9,8},{10,11... | collective-permute-start | bytes 786440 | tf_op jit(solution)/shard_map/ppermute | solution.py:54
  174.5 8.4 %collective-permute-start.13 = (f32[2,128,128]{2,1,0:T(8,128)S(1)}, f32[2,128,128]{2,1,0:T(8,128)S(1)}, u32[]{:S(2)}, u32[]{:S(2)}) collective-permute-start(f32[2,128,128]{2,1,0:T(8,128)S(1)} %get-tuple-element.52), channel_id=1, source_target_pairs={{0,9},{1,10},{2,11},{3,12},{4,13},{5,14},{6,15},{8,17},{9,18},{10,... | collective-permute-start | bytes 393224 | tf_op jit(solution)/shard_map/ppermute | solution.py:34
  (1 other events, 0.7 us)

commit v4 on v3

--- a/solution.py
+++ b/solution.py
@@ -36,17 +36,17 @@
 
 def device_groups(down, across):
     far = down // NEAR
-    near_groups = [
-        [(y * NEAR + z) * across + x * 2 + core for z in range(NEAR) for x in range(across // 2)]
-        for y in range(far)
+    wide_groups = [
+        [(y * NEAR + z) * across + x * 2 + core for y in range(far) for x in range(across // 2)]
+        for z in range(NEAR)
         for core in range(2)
     ]
-    far_groups = [
-        [(y * NEAR + z) * across + c for y in range(far)]
-        for z in range(NEAR)
+    line_groups = [
+        [(y * NEAR + z) * across + c for z in range(NEAR)]
+        for y in range(far)
         for c in range(across)
     ]
-    return near_groups, far_groups
+    return wide_groups, line_groups
 
 
 def swap_cores(value):
@@ -171,11 +171,11 @@
 
 def solve_kernel(first, members, *refs):
     if first:
-        (offsets, marks, tile, low, right, corner, probe, amp, tables) = refs[:9]
-        keep, give, terms, ext = refs[9:]
+        (marks, tile, low, right, corner, probe, amp, tables) = refs[:8]
+        keep, give, terms, ext = refs[8:]
     else:
-        (offsets, marks, tile, low, right, corner, probe, mine, other, power, amp, tables) = refs[:12]
-        keep, give, terms, new_probe, ext = refs[12:]
+        (marks, tile, low, right, corner, probe, mine, other, power, amp, tables) = refs[:11]
+        keep, give, terms, new_probe, ext = refs[11:]
     size = tile.shape[1]
     half = size // 2
     slots = amp.shape[0]
@@ -202,8 +202,8 @@
     pg_imag = jnp.zeros((size, size), jnp.float32)
     power_sum = jnp.zeros((), jnp.float32)
     for slot in range(slots):
-        row = jnp.clip(offsets[slot, 0], 0, HALO)
-        col = jnp.clip(offsets[slot, 1], 0, HALO)
+        row = jnp.clip(marks[2 + 2 * slot], 0, HALO)
+        col = jnp.clip(marks[3 + 2 * slot], 0, HALO)
         live = slot < marks[0]
         z_real = take_window(ext, 0, row, col, size)
         z_imag = take_window(ext, 1, row, col, size)
@@ -297,13 +297,13 @@
     out[1] = imag
 
 
-def place_kernel(offsets, tile, terms, partial, rim_right, rim_low, rim_corner, ext):
+def place_kernel(marks, tile, terms, partial, rim_right, rim_low, rim_corner, ext):
     size = tile.shape[1]
     slots = terms.shape[0]
     ext[...] = jnp.zeros_like(ext)
     for slot in range(slots):
-        row = jnp.clip(offsets[slot, 0], 0, HALO)
-        col = jnp.clip(offsets[slot, 1], 0, HALO)
+        row = jnp.clip(marks[2 + 2 * slot], 0, HALO)
+        col = jnp.clip(marks[3 + 2 * slot], 0, HALO)
         for part in range(2):
             add_window(ext, part, row, col, terms[slot, part])
     partial[...] = tile[...] + ext[:, :size, :size]
@@ -357,16 +357,15 @@
     slots = amplitudes.shape[0]
     margin = HALO
     edge_shapes = [(2, margin, size), (2, size, margin), (2, margin, margin)]
-    near_groups, far_groups = device_groups(lax.axis_size("row"), lax.axis_size("col"))
-    near, far = len(near_groups[0]), len(far_groups[0])
-    per = 2 * size // near
-    held = near * (per + 2)
+    wide_groups, line_groups = device_groups(lax.axis_size("row"), lax.axis_size("col"))
+    wide, line = len(wide_groups[0]), len(line_groups[0])
+    per = 2 * size // wide
+    held = wide * (per + 2)
     tables = jnp.asarray(make_tables(size))
     order = np.concatenate([np.arange(0, size, 2), np.arange(1, size, 2)])
     pick = jnp.asarray(np.eye(size)[:, order].astype(jnp.bfloat16))
-    spots = offsets.reshape(slots, 2)
     core = jnp.bitwise_and(lax.axis_index("col"), 1).astype(jnp.int32)
-    marks = jnp.concatenate([counts.reshape(1), core.reshape(1)])
+    marks = jnp.concatenate([counts.reshape(1), core.reshape(1), offsets.reshape(2 * slots)])
 
     current = object_field
     edges = call(edges_kernel, edge_shapes, [VMEM], current)
@@ -384,15 +383,15 @@
     for outer_step in range(OUTER):
         first = outer_step == 0
         outs = [(held, half), (held, half), (slots, 2, size, size)]
-        args = [spots, marks, current, low, right, corner, probe_now]
+        args = [marks, current, low, right, corner, probe_now]
         if not first:
             outs.append((2, size, size))
             args += [mine, other, power]
         args += [amp, tables]
         done = call(
-            functools.partial(solve_kernel, first, near),
+            functools.partial(solve_kernel, first, wide),
             outs,
-            [SMEM, SMEM] + [VMEM] * (len(args) - 2),
+            [SMEM] + [VMEM] * (len(args) - 1),
             *args,
             scratch=[(2, size + margin + SUB, size + margin)],
             grant=8,
@@ -405,7 +404,7 @@
             place_kernel,
             [current.shape, edge_shapes[1], edge_shapes[0], edge_shapes[2]],
             [SMEM, VMEM, VMEM],
-            spots,
+            marks,
             current,
             terms,
             scratch=[(2, size + margin + SUB, size + margin)],
@@ -414,21 +413,21 @@
         from_left = shifted(rim_right, 0, 1)
         from_above = shifted(rim_low, 1, 0)
         from_corner = shifted(rim_corner, 1, 1)
-        arrived = exchange(keep + given, near_groups)
+        arrived = exchange(keep + given, wide_groups)
         (copies,) = call(
-            functools.partial(fold_kernel, near, far, per + 2),
-            [(far * (per + 2), half)],
+            functools.partial(fold_kernel, wide, line, per + 2),
+            [(line * (per + 2), half)],
             [VMEM],
             arrived,
         )
-        arrived = exchange(copies, far_groups)
+        arrived = exchange(copies, line_groups)
         copies, power = call(
-            functools.partial(fold_kernel, far, near, per),
-            [(near * per, half), (8, half)],
+            functools.partial(fold_kernel, line, wide, per),
+            [(wide * per, half), (8, half)],
             [VMEM],
             arrived,
         )
-        mine = exchange(copies, near_groups)
+        mine = exchange(copies, wide_groups)
         other = swap_cores(mine)
         last = outer_step == OUTER - 1
         current, *edges = call(

time: 187 us -> 189 us (1.011)
  waiting for transfers between devices: 22.7 us -> 26.6 us
  starting transfers between devices: 67.5 us -> 64.6 us
    ppermute x12, waiting for transfers between devices: 19.6 us -> 23.5 us  [shifted(): return lax.ppermute(value, ('row', 'col'), pairs)]
    ppermute x12, starting transfers between devices: 46.8 us -> 43.1 us  [shifted(): return lax.ppermute(value, ('row', 'col'), pairs)]
    unnamed x30 -> x28, local copies, waits for them, and re-layouts: 11.2 us -> 10.5 us
where the time goes in v4:
time: 189 us; the launch traced here: 188 us
  blocking collectives  66 us (35%)
  starting transfers between devices  64.6 us (34%)
  waiting for transfers between devices  26.6 us (14%)
  Pallas kernels  17.4 us (9%)
  local copies, waits for them, and re-layouts  11.3 us (6%)
    all_to_all x4, blocking collectives, exchange(): lax.all_to_all(paired, ('row', 'col'), 0, 0, tiled=True, axis_index_group...  66 us
    ppermute x12, starting transfers between devices, shifted(): return lax.ppermute(value, ('row', 'col'), pairs)  43.1 us
    ppermute x12, waiting for transfers between devices, shifted(): return lax.ppermute(value, ('row', 'col'), pairs)  23.5 us
    pallas_call x13, Pallas kernels, call(): pl.pallas_call(kernel, out_shape=[jax.ShapeDtypeStruct(shape, jnp.float32...  17.4 us
    ppermute x4, starting transfers between devices, swap_cores(): return lax.ppermute(value, 'col', [(c, c ^ 1) for c in range(across)])  11.5 us
    unnamed x28, local copies, waits for them, and re-layouts  10.5 us
    all_to_all x2, starting transfers between devices, exchange(): lax.all_to_all(paired, ('row', 'col'), 0, 0, tiled=True, axis_index_group...  9.98 us
  transfers between devices with their start and end apart: 18, of which 6 were waited for; matrix products, arithmetic and copies ran while one was open for 0% of the time, Pallas kernels for 3%

profile of v4, /device:TPU:9, one launch (start us, length us, event | category | flops | bytes accessed | tf_op | source)
XLA Modules:
  0.0 187.5 jit_solution(3648299043131664984)
XLA Ops:
  2.5 10.5 %collective-permute-start = (f32[2,128,256]{2,1,0:T(8,128)}, f32[2,128,256]{2,1,0:T(8,128)S(1)}, u32[]{:S(2)}, u32[]{:S(2)}) collective-permute-start(f32[2,128,256]{2,1,0:T(8,128)} %get-tuple-element.30), channel_id=1, source_target_pairs={{8,0},{9,1},{10,2},{11,3},{12,4},{13,5},{14,6},{15,7},{16,8},{17,9... | collective-permute-start | bytes 786440 | tf_op jit(solution)/shard_map/ppermute | solution.py:34
  13.0 2.9 %collective-permute-start.1 = (f32[2,256,128]{2,1,0:T(8,128)}, f32[2,256,128]{2,1,0:T(8,128)S(1)}, u32[]{:S(2)}, u32[]{:S(2)}) collective-permute-start(f32[2,256,128]{2,1,0:T(8,128)} %get-tuple-element.31), channel_id=1, source_target_pairs={{1,0},{2,1},{3,2},{4,3},{5,4},{6,5},{7,6},{9,8},{10,9},{11,10},{12... | collective-permute-start | bytes 786440 | tf_op jit(solution)/shard_map/ppermute | solution.py:34
  15.9 1.9 %collective-permute-start.2 = (f32[2,128,128]{2,1,0:T(8,128)S(1)}, f32[2,128,128]{2,1,0:T(8,128)S(1)}, u32[]{:S(2)}, u32[]{:S(2)}) collective-permute-start(f32[2,128,128]{2,1,0:T(8,128)S(1)} %get-tuple-element.32), channel_id=1, source_target_pairs={{9,0},{10,1},{11,2},{12,3},{13,4},{14,5},{15,6},{17,8},{18,9},{19,... | collective-permute-start | bytes 393224 | tf_op jit(solution)/shard_map/ppermute | solution.py:34
  23.9 4.1 %shard_map.88 = (f32[576,128]{1,0:T(8,128)S(1)}, f32[576,128]{1,0:T(8,128)S(1)}, f32[2,2,256,256]{3,2,1,0:T(8,128)S(1)}) custom-call(s32[6]{0:T(128)S(1)} %pad_add_fusion.refs_0_.marks, f32[2,256,256]{2,1,0:T(8,128)S(1)} %copy-done.1, f32[2,128,256]{2,1,0:T(8,128)S(1)} %collective-permute-done.refs_2_, f32[2,256,128]{2,1,0:T(8,128)S(1)} %collective-permute-done.1.refs_3_, ...), custom_call_target="tpu_custom_call" | custom-call | tf_op jit(solution)/shard_map/pallas_call | solution.py:340
  29.0 1.9 %collective-permute-start.9 = (f32[576,128]{1,0:T(8,128)S(1)}, f32[576,128]{1,0:T(8,128)S(1)}, u32[]{:S(2)}, u32[]{:S(2)}) collective-permute-start(f32[576,128]{1,0:T(8,128)S(1)} %get-tuple-element.45), channel_id=1, source_target_pairs={{0,1},{1,0},{2,3},{3,2},{4,5},{5,4},{6,7},{7,6},{8,9},{9,8},{10,11... | collective-permute-start | bytes 884744 | tf_op jit(solution)/shard_map/ppermute | solution.py:54
  30.9 1.5 collective-permute-done.9
  32.5 20.6 %all_to_all.30 = f32[288,2,128]{2,1,0:T(2,128)S(1)} all-to-all(f32[288,2,128]{2,1,0:T(2,128)S(1)} %bitcast.25), channel_id=1, replica_groups={{0,2,4,6,64,66,68,70,128,130,132,134,192,194,196,198,256,258,260,262,32..., dimensions={0} | all-to-all | bytes 589824 | tf_op jit(solution)/shard_map/all_to_all | solution.py:60
  53.1 12.2 %all_to_all.31 = f32[72,2,128]{2,1,0:T(2,128)S(1)} all-to-all(f32[72,2,128]{2,1,0:T(2,128)S(1)} %bitcast.23), channel_id=1, replica_groups={{0,8,16,24,32,40,48,56},{1,9,17,25,33,41,49,57},{2,10,18,26,34,42,50,58..., dimensions={0} | all-to-all | bytes 147456 | tf_op jit(solution)/shard_map/all_to_all | solution.py:60
  66.1 5.0 %all-to-all-start.2 = ((f32[256,2,128]{2,1,0:T(2,128)}), f32[256,2,128]{2,1,0:T(2,128)S(1)}, u32[]{:S(2)}, u32[]{:S(2)}) async-start(f32[256,2,128]{2,1,0:T(2,128)} %bitcast.6), calls=%async_computation.2 | async-start | bytes 524288 | tf_op jit(solution)/shard_map/all_to_all | solution.py:60
  71.1 1.2 copy-done.6
  73.3 6.2 %collective-permute-start.3 = (f32[2,256,128]{2,1,0:T(8,128)S(1)}, f32[2,256,128]{2,1,0:T(8,128)S(1)}, u32[]{:S(2)}, u32[]{:S(2)}) collective-permute-start(f32[2,256,128]{2,1,0:T(8,128)S(1)} %get-tuple-element.37), channel_id=1, source_target_pairs={{0,1},{1,2},{2,3},{3,4},{4,5},{5,6},{6,7},{8,9},{9,10},{10,11},{11... | collective-permute-start | bytes 786440 | tf_op jit(solution)/shard_map/ppermute | solution.py:34
  79.5 2.2 %collective-permute-start.4 = (f32[2,128,256]{2,1,0:T(8,128)S(1)}, f32[2,128,256]{2,1,0:T(8,128)S(1)}, u32[]{:S(2)}, u32[]{:S(2)}) collective-permute-start(f32[2,128,256]{2,1,0:T(8,128)S(1)} %get-tuple-element.38), channel_id=1, source_target_pairs={{0,8},{1,9},{2,10},{3,11},{4,12},{5,13},{6,14},{7,15},{8,16},{9,17... | collective-permute-start | bytes 786440 | tf_op jit(solution)/shard_map/ppermute | solution.py:34
  81.7 2.1 %collective-permute-start.5 = (f32[2,128,128]{2,1,0:T(8,128)S(1)}, f32[2,128,128]{2,1,0:T(8,128)S(1)}, u32[]{:S(2)}, u32[]{:S(2)}) collective-permute-start(f32[2,128,128]{2,1,0:T(8,128)S(1)} %get-tuple-element.39), channel_id=1, source_target_pairs={{0,9},{1,10},{2,11},{3,12},{4,13},{5,14},{6,15},{8,17},{9,18},{10,... | collective-permute-start | bytes 393224 | tf_op jit(solution)/shard_map/ppermute | solution.py:34
  83.8 8.1 %collective-permute-done.5.from_corner = f32[2,128,128]{2,1,0:T(8,128)S(1)} collective-permute-done((f32[2,128,128]{2,1,0:T(8,128)S(1)}, f32[2,128,128]{2,1,0:T(8,128)S(1)}, u32[]{:S(2)}, u32[]{:S(2)}) %collective-permute-start.5) | collective-permute-done | bytes 131104 | tf_op jit(solution)/shard_map/ppermute | solution.py:34
  92.8 2.7 %collective-permute-start.6 = (f32[2,128,256]{2,1,0:T(8,128)}, f32[2,128,256]{2,1,0:T(8,128)S(1)}, u32[]{:S(2)}, u32[]{:S(2)}) collective-permute-start(f32[2,128,256]{2,1,0:T(8,128)} %get-tuple-element.41), channel_id=1, source_target_pairs={{8,0},{9,1},{10,2},{11,3},{12,4},{13,5},{14,6},{15,7},{16,8},{17,9... | collective-permute-start | bytes 786440 | tf_op jit(solution)/shard_map/ppermute | solution.py:34
  95.5 1.9 %collective-permute-start.7 = (f32[2,256,128]{2,1,0:T(8,128)}, f32[2,256,128]{2,1,0:T(8,128)S(1)}, u32[]{:S(2)}, u32[]{:S(2)}) collective-permute-start(f32[2,256,128]{2,1,0:T(8,128)} %get-tuple-element.42), channel_id=1, source_target_pairs={{1,0},{2,1},{3,2},{4,3},{5,4},{6,5},{7,6},{9,8},{10,9},{11,10},{12... | collective-permute-start | bytes 786440 | tf_op jit(solution)/shard_map/ppermute | solution.py:34
  97.4 1.9 %collective-permute-start.10 = (f32[512,128]{1,0:T(8,128)S(1)}, f32[512,128]{1,0:T(8,128)S(1)}, u32[]{:S(2)}, u32[]{:S(2)}) collective-permute-start(f32[512,128]{1,0:T(8,128)S(1)} %bitcast.17), channel_id=1, source_target_pairs={{0,1},{1,0},{2,3},{3,2},{4,5},{5,4},{6,7},{7,6},{8,9},{9,8},{10,11... | collective-permute-start | bytes 786440 | tf_op jit(solution)/shard_map/ppermute | solution.py:54
  99.4 2.3 %collective-permute-start.8 = (f32[2,128,128]{2,1,0:T(8,128)S(1)}, f32[2,128,128]{2,1,0:T(8,128)S(1)}, u32[]{:S(2)}, u32[]{:S(2)}) collective-permute-start(f32[2,128,128]{2,1,0:T(8,128)S(1)} %get-tuple-element.43), channel_id=1, source_target_pairs={{9,0},{10,1},{11,2},{12,3},{13,4},{14,5},{15,6},{17,8},{18,9},{19,... | collective-permute-start | bytes 393224 | tf_op jit(solution)/shard_map/ppermute | solution.py:34
  101.7 7.2 %collective-permute-done.8.refs_4_ = f32[2,128,128]{2,1,0:T(8,128)S(1)} collective-permute-done((f32[2,128,128]{2,1,0:T(8,128)S(1)}, f32[2,128,128]{2,1,0:T(8,128)S(1)}, u32[]{:S(2)}, u32[]{:S(2)}) %collective-permute-start.8) | collective-permute-done | bytes 131104 | tf_op jit(solution)/shard_map/ppermute | solution.py:34
  112.2 4.3 %shard_map.93 = (f32[576,128]{1,0:T(8,128)S(1)}, f32[576,128]{1,0:T(8,128)S(1)}, f32[2,2,256,256]{3,2,1,0:T(8,128)S(1)}, f32[2,256,256]{2,1,0:T(8,128)S(1)}) custom-call(s32[6]{0:T(128)S(1)} %pad_add_fusion.refs_0_.marks, f32[2,256,256]{2,1,0:T(8,128)S(1)} %get-tuple-element.40.refs_1_.tile, f32[2,128,256]{2,1,0:T(8,128)S(1)} %copy-done.10, ...), custom_call_target="tpu_custom_call" | custom-call | tf_op jit(solution)/shard_map/pallas_call | solution.py:340
  117.5 1.9 %collective-permute-start.14 = (f32[576,128]{1,0:T(8,128)S(1)}, f32[576,128]{1,0:T(8,128)S(1)}, u32[]{:S(2)}, u32[]{:S(2)}) collective-permute-start(f32[576,128]{1,0:T(8,128)S(1)} %get-tuple-element.55), channel_id=1, source_target_pairs={{0,1},{1,0},{2,3},{3,2},{4,5},{5,4},{6,7},{7,6},{8,9},{9,8},{10,11... | collective-permute-start | bytes 884744 | tf_op jit(solution)/shard_map/ppermute | solution.py:54
  119.5 1.5 collective-permute-done.14
  121.1 23.0 %all_to_all.32 = f32[288,2,128]{2,1,0:T(2,128)S(1)} all-to-all(f32[288,2,128]{2,1,0:T(2,128)S(1)} %bitcast.26), channel_id=1, replica_groups={{0,2,4,6,64,66,68,70,128,130,132,134,192,194,196,198,256,258,260,262,32..., dimensions={0} | all-to-all | bytes 589824 | tf_op jit(solution)/shard_map/all_to_all | solution.py:60
  144.1 10.1 %all_to_all.33 = f32[72,2,128]{2,1,0:T(2,128)S(1)} all-to-all(f32[72,2,128]{2,1,0:T(2,128)S(1)} %bitcast.24), channel_id=1, replica_groups={{0,8,16,24,32,40,48,56},{1,9,17,25,33,41,49,57},{2,10,18,26,34,42,50,58..., dimensions={0} | all-to-all | bytes 147456 | tf_op jit(solution)/shard_map/all_to_all | solution.py:60
  154.9 5.0 %all-to-all-start.5 = ((f32[256,2,128]{2,1,0:T(2,128)}), f32[256,2,128]{2,1,0:T(2,128)S(1)}, u32[]{:S(2)}, u32[]{:S(2)}) async-start(f32[256,2,128]{2,1,0:T(2,128)} %bitcast.12), calls=%async_computation.5 | async-start | bytes 524288 | tf_op jit(solution)/shard_map/all_to_all | solution.py:60
  159.9 1.8 shard_map.94
  161.7 6.2 %collective-permute-start.11 = (f32[2,256,128]{2,1,0:T(8,128)}, f32[2,256,128]{2,1,0:T(8,128)S(1)}, u32[]{:S(2)}, u32[]{:S(2)}) collective-permute-start(f32[2,256,128]{2,1,0:T(8,128)} %get-tuple-element.50), channel_id=1, source_target_pairs={{0,1},{1,2},{2,3},{3,4},{4,5},{5,6},{6,7},{8,9},{9,10},{10,11},{11... | collective-permute-start | bytes 786440 | tf_op jit(solution)/shard_map/ppermute | solution.py:34
  167.9 2.2 %collective-permute-start.12 = (f32[2,128,256]{2,1,0:T(8,128)}, f32[2,128,256]{2,1,0:T(8,128)S(1)}, u32[]{:S(2)}, u32[]{:S(2)}) collective-permute-start(f32[2,128,256]{2,1,0:T(8,128)} %get-tuple-element.51), channel_id=1, source_target_pairs={{0,8},{1,9},{2,10},{3,11},{4,12},{5,13},{6,14},{7,15},{8,16},{9,17... | collective-permute-start | bytes 786440 | tf_op jit(solution)/shard_map/ppermute | solution.py:34
  170.1 5.8 %collective-permute-start.15 = (f32[512,128]{1,0:T(8,128)S(1)}, f32[512,128]{1,0:T(8,128)S(1)}, u32[]{:S(2)}, u32[]{:S(2)}) collective-permute-start(f32[512,128]{1,0:T(8,128)S(1)} %bitcast.19), channel_id=1, source_target_pairs={{0,1},{1,0},{2,3},{3,2},{4,5},{5,4},{6,7},{7,6},{8,9},{9,8},{10,11... | collective-permute-start | bytes 786440 | tf_op jit(solution)/shard_map/ppermute | solution.py:54
  175.9 2.1 %collective-permute-start.13 = (f32[2,128,128]{2,1,0:T(8,128)S(1)}, f32[2,128,128]{2,1,0:T(8,128)S(1)}, u32[]{:S(2)}, u32[]{:S(2)}) collective-permute-start(f32[2,128,128]{2,1,0:T(8,128)S(1)} %get-tuple-element.52), channel_id=1, source_target_pairs={{0,9},{1,10},{2,11},{3,12},{4,13},{5,14},{6,15},{8,17},{9,18},{10,... | collective-permute-start | bytes 393224 | tf_op jit(solution)/shard_map/ppermute | solution.py:34
  178.0 7.0 %collective-permute-done.13.from_corner = f32[2,128,128]{2,1,0:T(8,128)S(1)} collective-permute-done((f32[2,128,128]{2,1,0:T(8,128)S(1)}, f32[2,128,128]{2,1,0:T(8,128)S(1)}, u32[]{:S(2)}, u32[]{:S(2)}) %collective-permute-start.13) | collective-permute-done | bytes 131104 | tf_op jit(solution)/shard_map/ppermute | solution.py:34
  185.9 1.7 shard_map.98
  (53 shorter events, 16.9 us)
Async XLA Ops:
  0.6 1.0 copy-start
  1.7 22.2 %copy-start.2 = (bf16[8,256,256]{2,1,0:T(8,128)(2,1)S(1)}, bf16[8,256,256]{2,1,0:T(8,128)(2,1)}, u32[]{:S(2)}) copy-start(bf16[8,256,256]{2,1,0:T(8,128)(2,1)} %constant.10.clone.refs_7_.refs_10_) | copy-start | bytes 3145732
  2.5 21.4 %collective-permute-start = (f32[2,128,256]{2,1,0:T(8,128)}, f32[2,128,256]{2,1,0:T(8,128)S(1)}, u32[]{:S(2)}, u32[]{:S(2)}) collective-permute-start(f32[2,128,256]{2,1,0:T(8,128)} %get-tuple-element.30), channel_id=1, source_target_pairs={{8,0},{9,1},{10,2},{11,3},{12,4},{13,5},{14,6},{15,7},{16,8},{17,9... | collective-permute-start | bytes 786440 | tf_op jit(solution)/shard_map/ppermute | solution.py:34
  13.0 10.8 %collective-permute-start.1 = (f32[2,256,128]{2,1,0:T(8,128)}, f32[2,256,128]{2,1,0:T(8,128)S(1)}, u32[]{:S(2)}, u32[]{:S(2)}) collective-permute-start(f32[2,256,128]{2,1,0:T(8,128)} %get-tuple-element.31), channel_id=1, source_target_pairs={{1,0},{2,1},{3,2},{4,3},{5,4},{6,5},{7,6},{9,8},{10,9},{11,10},{12... | collective-permute-start | bytes 786440 | tf_op jit(solution)/shard_map/ppermute | solution.py:34
  15.9 7.9 %collective-permute-start.2 = (f32[2,128,128]{2,1,0:T(8,128)S(1)}, f32[2,128,128]{2,1,0:T(8,128)S(1)}, u32[]{:S(2)}, u32[]{:S(2)}) collective-permute-start(f32[2,128,128]{2,1,0:T(8,128)S(1)} %get-tuple-element.32), channel_id=1, source_target_pairs={{9,0},{10,1},{11,2},{12,3},{13,4},{14,5},{15,6},{17,8},{18,9},{19,... | collective-permute-start | bytes 393224 | tf_op jit(solution)/shard_map/ppermute | solution.py:34
  19.3 1.0 copy-start.7
  20.3 1.0 copy-start.8
  21.3 0.9 copy-start.13
  22.3 1.6 copy-start.1
  28.0 1.0 copy-start.5
  29.0 3.5 %collective-permute-start.9 = (f32[576,128]{1,0:T(8,128)S(1)}, f32[576,128]{1,0:T(8,128)S(1)}, u32[]{:S(2)}, u32[]{:S(2)}) collective-permute-start(f32[576,128]{1,0:T(8,128)S(1)} %get-tuple-element.45), channel_id=1, source_target_pairs={{0,1},{1,0},{2,3},{3,2},{4,5},{5,4},{6,7},{7,6},{8,9},{9,8},{10,11... | collective-permute-start | bytes 884744 | tf_op jit(solution)/shard_map/ppermute | solution.py:54
  66.1 31.3 %all-to-all-start.2 = ((f32[256,2,128]{2,1,0:T(2,128)}), f32[256,2,128]{2,1,0:T(2,128)S(1)}, u32[]{:S(2)}, u32[]{:S(2)}) async-start(f32[256,2,128]{2,1,0:T(2,128)} %bitcast.6), calls=%async_computation.2 | async-start | bytes 524288 | tf_op jit(solution)/shard_map/all_to_all | solution.py:60
  71.1 1.2 copy-start.6
  73.3 18.6 %collective-permute-start.3 = (f32[2,256,128]{2,1,0:T(8,128)S(1)}, f32[2,256,128]{2,1,0:T(8,128)S(1)}, u32[]{:S(2)}, u32[]{:S(2)}) collective-permute-start(f32[2,256,128]{2,1,0:T(8,128)S(1)} %get-tuple-element.37), channel_id=1, source_target_pairs={{0,1},{1,2},{2,3},{3,4},{4,5},{5,6},{6,7},{8,9},{9,10},{10,11},{11... | collective-permute-start | bytes 786440 | tf_op jit(solution)/shard_map/ppermute | solution.py:34
  79.5 12.4 %collective-permute-start.4 = (f32[2,128,256]{2,1,0:T(8,128)S(1)}, f32[2,128,256]{2,1,0:T(8,128)S(1)}, u32[]{:S(2)}, u32[]{:S(2)}) collective-permute-start(f32[2,128,256]{2,1,0:T(8,128)S(1)} %get-tuple-element.38), channel_id=1, source_target_pairs={{0,8},{1,9},{2,10},{3,11},{4,12},{5,13},{6,14},{7,15},{8,16},{9,17... | collective-permute-start | bytes 786440 | tf_op jit(solution)/shard_map/ppermute | solution.py:34
  81.7 10.2 %collective-permute-start.5 = (f32[2,128,128]{2,1,0:T(8,128)S(1)}, f32[2,128,128]{2,1,0:T(8,128)S(1)}, u32[]{:S(2)}, u32[]{:S(2)}) collective-permute-start(f32[2,128,128]{2,1,0:T(8,128)S(1)} %get-tuple-element.39), channel_id=1, source_target_pairs={{0,9},{1,10},{2,11},{3,12},{4,13},{5,14},{6,15},{8,17},{9,18},{10,... | collective-permute-start | bytes 393224 | tf_op jit(solution)/shard_map/ppermute | solution.py:34
  92.8 16.1 %collective-permute-start.6 = (f32[2,128,256]{2,1,0:T(8,128)}, f32[2,128,256]{2,1,0:T(8,128)S(1)}, u32[]{:S(2)}, u32[]{:S(2)}) collective-permute-start(f32[2,128,256]{2,1,0:T(8,128)} %get-tuple-element.41), channel_id=1, source_target_pairs={{8,0},{9,1},{10,2},{11,3},{12,4},{13,5},{14,6},{15,7},{16,8},{17,9... | collective-permute-start | bytes 786440 | tf_op jit(solution)/shard_map/ppermute | solution.py:34
  95.5 14.1 %collective-permute-start.7 = (f32[2,256,128]{2,1,0:T(8,128)}, f32[2,256,128]{2,1,0:T(8,128)S(1)}, u32[]{:S(2)}, u32[]{:S(2)}) collective-permute-start(f32[2,256,128]{2,1,0:T(8,128)} %get-tuple-element.42), channel_id=1, source_target_pairs={{1,0},{2,1},{3,2},{4,3},{5,4},{6,5},{7,6},{9,8},{10,9},{11,10},{12... | collective-permute-start | bytes 786440 | tf_op jit(solution)/shard_map/ppermute | solution.py:34
  97.4 12.9 %collective-permute-start.10 = (f32[512,128]{1,0:T(8,128)S(1)}, f32[512,128]{1,0:T(8,128)S(1)}, u32[]{:S(2)}, u32[]{:S(2)}) collective-permute-start(f32[512,128]{1,0:T(8,128)S(1)} %bitcast.17), channel_id=1, source_target_pairs={{0,1},{1,0},{2,3},{3,2},{4,5},{5,4},{6,7},{7,6},{8,9},{9,8},{10,11... | collective-permute-start | bytes 786440 | tf_op jit(solution)/shard_map/ppermute | solution.py:54
  99.4 9.5 %collective-permute-start.8 = (f32[2,128,128]{2,1,0:T(8,128)S(1)}, f32[2,128,128]{2,1,0:T(8,128)S(1)}, u32[]{:S(2)}, u32[]{:S(2)}) collective-permute-start(f32[2,128,128]{2,1,0:T(8,128)S(1)} %get-tuple-element.43), channel_id=1, source_target_pairs={{9,0},{10,1},{11,2},{12,3},{13,4},{14,5},{15,6},{17,8},{18,9},{19,... | collective-permute-start | bytes 393224 | tf_op jit(solution)/shard_map/ppermute | solution.py:34
  108.9 0.7 copy-start.9
  109.6 0.7 copy-start.11
  110.3 1.0 copy-start.10
  111.3 0.9 copy-start.12
  116.5 1.0 copy-start.3
  117.5 3.5 %collective-permute-start.14 = (f32[576,128]{1,0:T(8,128)S(1)}, f32[576,128]{1,0:T(8,128)S(1)}, u32[]{:S(2)}, u32[]{:S(2)}) collective-permute-start(f32[576,128]{1,0:T(8,128)S(1)} %get-tuple-element.55), channel_id=1, source_target_pairs={{0,1},{1,0},{2,3},{3,2},{4,5},{5,4},{6,7},{7,6},{8,9},{9,8},{10,11... | collective-permute-start | bytes 884744 | tf_op jit(solution)/shard_map/ppermute | solution.py:54
  121.0 38.9 %copy-start.4 = (f32[2,2,256,256]{3,2,1,0:T(8,128)S(1)}, f32[2,2,256,256]{3,2,1,0:T(8,128)}, u32[]{:S(2)}) copy-start(f32[2,2,256,256]{3,2,1,0:T(8,128)} %copy-done.3) | copy-start | bytes 3145732
  154.9 15.2 %all-to-all-start.5 = ((f32[256,2,128]{2,1,0:T(2,128)}), f32[256,2,128]{2,1,0:T(2,128)S(1)}, u32[]{:S(2)}, u32[]{:S(2)}) async-start(f32[256,2,128]{2,1,0:T(2,128)} %bitcast.12), calls=%async_computation.5 | async-start | bytes 524288 | tf_op jit(solution)/shard_map/all_to_all | solution.py:60
  161.7 23.3 %collective-permute-start.11 = (f32[2,256,128]{2,1,0:T(8,128)}, f32[2,256,128]{2,1,0:T(8,128)S(1)}, u32[]{:S(2)}, u32[]{:S(2)}) collective-permute-start(f32[2,256,128]{2,1,0:T(8,128)} %get-tuple-element.50), channel_id=1, source_target_pairs={{0,1},{1,2},{2,3},{3,4},{4,5},{5,6},{6,7},{8,9},{9,10},{10,11},{11... | collective-permute-start | bytes 786440 | tf_op jit(solution)/shard_map/ppermute | solution.py:34
  167.9 17.1 %collective-permute-start.12 = (f32[2,128,256]{2,1,0:T(8,128)}, f32[2,128,256]{2,1,0:T(8,128)S(1)}, u32[]{:S(2)}, u32[]{:S(2)}) collective-permute-start(f32[2,128,256]{2,1,0:T(8,128)} %get-tuple-element.51), channel_id=1, source_target_pairs={{0,8},{1,9},{2,10},{3,11},{4,12},{5,13},{6,14},{7,15},{8,16},{9,17... | collective-permute-start | bytes 786440 | tf_op jit(solution)/shard_map/ppermute | solution.py:34
  170.1 15.8 %collective-permute-start.15 = (f32[512,128]{1,0:T(8,128)S(1)}, f32[512,128]{1,0:T(8,128)S(1)}, u32[]{:S(2)}, u32[]{:S(2)}) collective-permute-start(f32[512,128]{1,0:T(8,128)S(1)} %bitcast.19), channel_id=1, source_target_pairs={{0,1},{1,0},{2,3},{3,2},{4,5},{5,4},{6,7},{7,6},{8,9},{9,8},{10,11... | collective-permute-start | bytes 786440 | tf_op jit(solution)/shard_map/ppermute | solution.py:54
  175.9 9.1 %collective-permute-start.13 = (f32[2,128,128]{2,1,0:T(8,128)S(1)}, f32[2,128,128]{2,1,0:T(8,128)S(1)}, u32[]{:S(2)}, u32[]{:S(2)}) collective-permute-start(f32[2,128,128]{2,1,0:T(8,128)S(1)} %get-tuple-element.52), channel_id=1, source_target_pairs={{0,9},{1,10},{2,11},{3,12},{4,13},{5,14},{6,15},{8,17},{9,18},{10,... | collective-permute-start | bytes 393224 | tf_op jit(solution)/shard_map/ppermute | solution.py:34

commit v5 on v4

--- a/solution.py
+++ b/solution.py
@@ -174,15 +174,18 @@
         (marks, tile, low, right, corner, probe, amp, tables) = refs[:8]
         keep, give, terms, ext = refs[8:]
     else:
-        (marks, tile, low, right, corner, probe, mine, other, power, amp, tables) = refs[:11]
-        keep, give, terms, new_probe, ext = refs[11:]
+        (marks, tile, low, right, probe, mine, other, power, amp, tables) = refs[:10]
+        keep, give, terms, new_probe, ext = refs[10:]
     size = tile.shape[1]
     half = size // 2
     slots = amp.shape[0]
     ext[:, :size, :size] = tile[...]
-    ext[:, size : size + HALO, :size] = low[...]
     ext[:, :size, size:] = right[...]
-    ext[:, size : size + HALO, size:] = corner[...]
+    if first:
+        ext[:, size : size + HALO, :size] = low[...]
+        ext[:, size : size + HALO, size:] = corner[...]
+    else:
+        ext[:, size : size + HALO, :] = low[...]
     ext[:, size + HALO :, :] = jnp.zeros((2, SUB, size + HALO), jnp.float32)
 
     if first:
@@ -312,13 +315,19 @@
     rim_corner[...] = ext[:, size : size + HALO, size:]
 
 
-def update_kernel(with_edges, partial, from_left, from_above, from_corner, out, *edges):
+def update_kernel(partial, from_left, from_above, from_corner, out, *side):
     out[...] = partial[...]
     out[:, :, :HALO] += from_left[...]
     out[:, :HALO, :] += from_above[...]
     out[:, :HALO, :HALO] += from_corner[...]
-    if with_edges:
-        edges_kernel(out, *edges)
+    if side:
+        side[0][...] = out[:, :, :HALO]
+
+
+def join_kernel(tile, right, out):
+    size = tile.shape[1]
+    out[:, :, :size] = tile[:, :HALO, :]
+    out[:, :, size:] = right[:, :HALO, :]
 
 
 def fold_kernel(members, copies, keep, source, out, *power):
@@ -345,10 +354,6 @@
         scratch_shapes=[pltpu.VMEM(shape, jnp.float32) for shape in scratch],
         compiler_params=pltpu.CompilerParams(vmem_limit_bytes=grant << 20),
     )(*args)
-
-
-def halo(edges):
-    return shifted(edges[0], -1, 0), shifted(edges[1], 0, -1), shifted(edges[2], -1, -1)
 
 
 def shards(object_field, probe_field, amplitudes, offsets, counts):
@@ -378,12 +383,14 @@
         probe_field,
         scratch=[(2 * slots, size, half)],
     )
-    low, right, corner = halo(edges)
+    low = shifted(edges[0], -1, 0)
+    right = shifted(edges[1], 0, -1)
+    corner = shifted(edges[2], -1, -1)
     mine = other = power = None
     for outer_step in range(OUTER):
         first = outer_step == 0
         outs = [(held, half), (held, half), (slots, 2, size, size)]
-        args = [marks, current, low, right, corner, probe_now]
+        args = [marks, current, low, right] + ([corner] if first else []) + [probe_now]
         if not first:
             outs.append((2, size, size))
             args += [mine, other, power]
@@ -430,9 +437,9 @@
         mine = exchange(copies, wide_groups)
         other = swap_cores(mine)
         last = outer_step == OUTER - 1
-        current, *edges = call(
-            functools.partial(update_kernel, not last),
-            [current.shape] + ([] if last else edge_shapes),
+        current, *side = call(
+            update_kernel,
+            [current.shape] + ([] if last else [edge_shapes[1]]),
             [VMEM] * 4,
             partial,
             from_left,
@@ -440,7 +447,9 @@
             from_corner,
         )
         if not last:
-            low, right, corner = halo(edges)
+            right = shifted(side[0], 0, -1)
+            (joined,) = call(join_kernel, [(2, margin, size + margin)], [VMEM] * 2, current, right)
+            low = shifted(joined, -1, 0)
     (probe_now,) = call(
         probe_kernel,
         [probe_field.shape],

time: 189 us -> 177 us (0.937)
  blocking collectives: 66 us -> 33.3 us
  starting transfers between devices: 64.6 us -> 81.6 us
    all_to_all x4 -> x2, blocking collectives: 66 us -> 33.3 us  [exchange(): lax.all_to_all(paired, ('row', 'col'), 0, 0, tiled=True, axis_index_group...]
    all_to_all x2 -> x4, starting transfers between devices: 9.98 us -> 26.2 us  [exchange(): lax.all_to_all(paired, ('row', 'col'), 0, 0, tiled=True, axis_index_group...]
    all_to_all x2 -> x4, waiting for transfers between devices: 0.01 us -> 4.26 us  [exchange(): lax.all_to_all(paired, ('row', 'col'), 0, 0, tiled=True, axis_index_group...]
    ppermute x12 -> x11, waiting for transfers between devices: 23.5 us -> 19.4 us  [shifted(): return lax.ppermute(value, ('row', 'col'), pairs)]
    pallas_call x13 -> x14, Pallas kernels: 17.4 us -> 18.9 us  [call(): pl.pallas_call(kernel, out_shape=[jax.ShapeDtypeStruct(shape, jnp.float32...]
    unnamed x28 -> x32, local copies, waits for them, and re-layouts: 10.5 us -> 11.7 us
    ppermute x12 -> x11, starting transfers between devices: 43.1 us -> 43.7 us  [shifted(): return lax.ppermute(value, ('row', 'col'), pairs)]
  transfers between devices with their start and end apart: 18 -> 19, of which waited for: 6 -> 9; matrix products, arithmetic and copies ran while one was open for 0% -> 0% of each run, Pallas kernels for 3% -> 4%
where the time goes in v5:
time: 177 us; the launch traced here: 175 us
  starting transfers between devices  81.6 us (46%)
  blocking collectives  33.3 us (19%)
  waiting for transfers between devices  26.8 us (15%)
  Pallas kernels  18.9 us (11%)
  local copies, waits for them, and re-layouts  12.5 us (7%)
    ppermute x11, starting transfers between devices, shifted(): return lax.ppermute(value, ('row', 'col'), pairs)  43.7 us
    all_to_all x2, blocking collectives, exchange(): lax.all_to_all(paired, ('row', 'col'), 0, 0, tiled=True, axis_index_group...  33.3 us
    all_to_all x4, starting transfers between devices, exchange(): lax.all_to_all(paired, ('row', 'col'), 0, 0, tiled=True, axis_index_group...  26.2 us
    ppermute x11, waiting for transfers between devices, shifted(): return lax.ppermute(value, ('row', 'col'), pairs)  19.4 us
    pallas_call x14, Pallas kernels, call(): pl.pallas_call(kernel, out_shape=[jax.ShapeDtypeStruct(shape, jnp.float32...  18.9 us
    ppermute x4, starting transfers between devices, swap_cores(): return lax.ppermute(value, 'col', [(c, c ^ 1) for c in range(across)])  11.8 us
    unnamed x32, local copies, waits for them, and re-layouts  11.7 us
    all_to_all x4, waiting for transfers between devices, exchange(): lax.all_to_all(paired, ('row', 'col'), 0, 0, tiled=True, axis_index_group...  4.26 us
  transfers between devices with their start and end apart: 19, of which 9 were waited for; matrix products, arithmetic and copies ran while one was open for 0% of the time, Pallas kernels for 4%

profile of v5, /device:TPU:9, one launch (start us, length us, event | category | flops | bytes accessed | tf_op | source)
XLA Modules:
  0.0 175.5 jit_solution(6671928908947629616)
XLA Ops:
  2.5 10.5 %collective-permute-start = (f32[2,128,256]{2,1,0:T(8,128)}, f32[2,128,256]{2,1,0:T(8,128)S(1)}, u32[]{:S(2)}, u32[]{:S(2)}) collective-permute-start(f32[2,128,256]{2,1,0:T(8,128)} %get-tuple-element.28), channel_id=1, source_target_pairs={{8,0},{9,1},{10,2},{11,3},{12,4},{13,5},{14,6},{15,7},{16,8},{17,9... | collective-permute-start | bytes 786440 | tf_op jit(solution)/shard_map/ppermute | solution.py:34
  13.0 2.9 %collective-permute-start.1 = (f32[2,256,128]{2,1,0:T(8,128)S(1)}, f32[2,256,128]{2,1,0:T(8,128)S(1)}, u32[]{:S(2)}, u32[]{:S(2)}) collective-permute-start(f32[2,256,128]{2,1,0:T(8,128)S(1)} %get-tuple-element.29), channel_id=1, source_target_pairs={{1,0},{2,1},{3,2},{4,3},{5,4},{6,5},{7,6},{9,8},{10,9},{11,10},{12... | collective-permute-start | bytes 786440 | tf_op jit(solution)/shard_map/ppermute | solution.py:34
  15.9 1.9 %collective-permute-start.2 = (f32[2,128,128]{2,1,0:T(8,128)}, f32[2,128,128]{2,1,0:T(8,128)S(1)}, u32[]{:S(2)}, u32[]{:S(2)}) collective-permute-start(f32[2,128,128]{2,1,0:T(8,128)} %get-tuple-element.30), channel_id=1, source_target_pairs={{9,0},{10,1},{11,2},{12,3},{13,4},{14,5},{15,6},{17,8},{18,9},{19,... | collective-permute-start | bytes 393224 | tf_op jit(solution)/shard_map/ppermute | solution.py:34
  24.1 4.1 %shard_map.88 = (f32[576,128]{1,0:T(8,128)S(1)}, f32[576,128]{1,0:T(8,128)S(1)}, f32[2,2,256,256]{3,2,1,0:T(8,128)S(1)}) custom-call(s32[6]{0:T(128)S(1)} %pad_add_fusion.refs_0_.marks, f32[2,256,256]{2,1,0:T(8,128)S(1)} %copy-done.1, f32[2,128,256]{2,1,0:T(8,128)S(1)} %collective-permute-done.refs_2_, f32[2,256,128]{2,1,0:T(8,128)S(1)} %collective-permute-done.1.refs_3_, ...), custom_call_target="tpu_custom_call" | custom-call | tf_op jit(solution)/shard_map/pallas_call | solution.py:349
  29.2 1.9 %collective-permute-start.8 = (f32[576,128]{1,0:T(8,128)S(1)}, f32[576,128]{1,0:T(8,128)S(1)}, u32[]{:S(2)}, u32[]{:S(2)}) collective-permute-start(f32[576,128]{1,0:T(8,128)S(1)} %get-tuple-element.41), channel_id=1, source_target_pairs={{0,1},{1,0},{2,3},{3,2},{4,5},{5,4},{6,7},{7,6},{8,9},{9,8},{10,11... | collective-permute-start | bytes 884744 | tf_op jit(solution)/shard_map/ppermute | solution.py:54
  31.1 1.5 collective-permute-done.8
  33.4 9.4 %all-to-all-start = ((f32[288,2,128]{2,1,0:T(2,128)}), f32[288,2,128]{2,1,0:T(2,128)S(1)}, u32[]{:S(2)}, u32[]{:S(2)}) async-start(f32[288,2,128]{2,1,0:T(2,128)} %bitcast.2), calls=%async_computation | async-start | bytes 589824 | tf_op jit(solution)/shard_map/all_to_all | solution.py:60
  44.1 1.7 shard_map.89
  45.8 3.7 %collective-permute-start.3 = (f32[2,256,128]{2,1,0:T(8,128)}, f32[2,256,128]{2,1,0:T(8,128)S(1)}, u32[]{:S(2)}, u32[]{:S(2)}) collective-permute-start(f32[2,256,128]{2,1,0:T(8,128)} %get-tuple-element.35), channel_id=1, source_target_pairs={{0,1},{1,2},{2,3},{3,4},{4,5},{5,6},{6,7},{8,9},{9,10},{10,11},{11... | collective-permute-start | bytes 786440 | tf_op jit(solution)/shard_map/ppermute | solution.py:34
  49.5 3.1 %collective-permute-start.4 = (f32[2,128,256]{2,1,0:T(8,128)}, f32[2,128,256]{2,1,0:T(8,128)S(1)}, u32[]{:S(2)}, u32[]{:S(2)}) collective-permute-start(f32[2,128,256]{2,1,0:T(8,128)} %get-tuple-element.36), channel_id=1, source_target_pairs={{0,8},{1,9},{2,10},{3,11},{4,12},{5,13},{6,14},{7,15},{8,16},{9,17... | collective-permute-start | bytes 786440 | tf_op jit(solution)/shard_map/ppermute | solution.py:34
  52.6 2.2 %all-to-all-done = f32[288,2,128]{2,1,0:T(2,128)S(1)} async-done(((f32[288,2,128]{2,1,0:T(2,128)}), f32[288,2,128]{2,1,0:T(2,128)S(1)}, u32[]{:S(2)}, u32[]{:S(2)}) %all-to-all-start) | async-done | bytes 294944 | tf_op jit(solution)/shard_map/all_to_all | solution.py:60
  55.4 4.4 %all-to-all-start.1 = ((f32[72,2,128]{2,1,0:T(2,128)}), f32[72,2,128]{2,1,0:T(2,128)S(1)}, u32[]{:S(2)}, u32[]{:S(2)}) async-start(f32[72,2,128]{2,1,0:T(2,128)} %bitcast.4), calls=%async_computation.1 | async-start | bytes 147456 | tf_op jit(solution)/shard_map/all_to_all | solution.py:60
  59.8 5.7 %collective-permute-start.5 = (f32[2,128,128]{2,1,0:T(8,128)}, f32[2,128,128]{2,1,0:T(8,128)}, u32[]{:S(2)}, u32[]{:S(2)}) collective-permute-start(f32[2,128,128]{2,1,0:T(8,128)} %get-tuple-element.37), channel_id=1, source_target_pairs={{0,9},{1,10},{2,11},{3,12},{4,13},{5,14},{6,15},{8,17},{9,18},{10,... | collective-permute-start | bytes 393224 | tf_op jit(solution)/shard_map/ppermute | solution.py:34
  65.5 1.6 all-to-all-done.1
  67.8 7.3 %all-to-all-start.2 = ((f32[256,2,128]{2,1,0:T(2,128)}), f32[256,2,128]{2,1,0:T(2,128)S(1)}, u32[]{:S(2)}, u32[]{:S(2)}) async-start(f32[256,2,128]{2,1,0:T(2,128)} %bitcast.6), calls=%async_computation.2 | async-start | bytes 524288 | tf_op jit(solution)/shard_map/all_to_all | solution.py:60
  79.4 3.5 %collective-permute-start.6 = (f32[2,256,128]{2,1,0:T(8,128)S(1)}, f32[2,256,128]{2,1,0:T(8,128)S(1)}, u32[]{:S(2)}, u32[]{:S(2)}) collective-permute-start(f32[2,256,128]{2,1,0:T(8,128)S(1)} %get-tuple-element.39), channel_id=1, source_target_pairs={{1,0},{2,1},{3,2},{4,3},{5,4},{6,5},{7,6},{9,8},{10,9},{11,10},{12... | collective-permute-start | bytes 786440 | tf_op jit(solution)/shard_map/ppermute | solution.py:34
  82.9 5.3 %collective-permute-done.6.right.refs_3_ = f32[2,256,128]{2,1,0:T(8,128)S(1)} collective-permute-done((f32[2,256,128]{2,1,0:T(8,128)S(1)}, f32[2,256,128]{2,1,0:T(8,128)S(1)}, u32[]{:S(2)}, u32[]{:S(2)}) %collective-permute-start.6) | collective-permute-done | bytes 262176 | tf_op jit(solution)/shard_map/ppermute | solution.py:34
  89.0 1.9 %collective-permute-start.7 = (f32[2,128,384]{2,1,0:T(8,128)}, f32[2,128,384]{2,1,0:T(8,128)S(1)}, u32[]{:S(2)}, u32[]{:S(2)}) collective-permute-start(f32[2,128,384]{2,1,0:T(8,128)} %shard_map.91), channel_id=1, source_target_pairs={{8,0},{9,1},{10,2},{11,3},{12,4},{13,5},{14,6},{15,7},{16,8},{17,9... | collective-permute-start | bytes 1179656 | tf_op jit(solution)/shard_map/ppermute | solution.py:34
  90.9 1.9 %collective-permute-start.9 = (f32[512,128]{1,0:T(8,128)S(1)}, f32[512,128]{1,0:T(8,128)S(1)}, u32[]{:S(2)}, u32[]{:S(2)}) collective-permute-start(f32[512,128]{1,0:T(8,128)S(1)} %bitcast.17), channel_id=1, source_target_pairs={{0,1},{1,0},{2,3},{3,2},{4,5},{5,4},{6,7},{7,6},{8,9},{9,8},{10,11... | collective-permute-start | bytes 786440 | tf_op jit(solution)/shard_map/ppermute | solution.py:54
  92.9 5.8 %collective-permute-done.7.refs_2_ = f32[2,128,384]{2,1,0:T(8,128)S(1)} collective-permute-done((f32[2,128,384]{2,1,0:T(8,128)}, f32[2,128,384]{2,1,0:T(8,128)S(1)}, u32[]{:S(2)}, u32[]{:S(2)}) %collective-permute-start.7) | collective-permute-done | bytes 393248 | tf_op jit(solution)/shard_map/ppermute | solution.py:34
  98.6 4.4 %shard_map.94 = (f32[576,128]{1,0:T(8,128)S(1)}, f32[576,128]{1,0:T(8,128)S(1)}, f32[2,2,256,256]{3,2,1,0:T(8,128)S(1)}, f32[2,256,256]{2,1,0:T(8,128)S(1)}) custom-call(s32[6]{0:T(128)S(1)} %pad_add_fusion.refs_0_.marks, f32[2,256,256]{2,1,0:T(8,128)S(1)} %get-tuple-element.38.tile.refs_1_, f32[2,128,384]{2,1,0:T(8,128)S(1)} %collective-permute-done.7.refs_2_, ...), custom_call_target="tpu_custom_call" | custom-call | tf_op jit(solution)/shard_map/pallas_call | solution.py:349
  104.9 1.9 %collective-permute-start.13 = (f32[576,128]{1,0:T(8,128)S(1)}, f32[576,128]{1,0:T(8,128)S(1)}, u32[]{:S(2)}, u32[]{:S(2)}) collective-permute-start(f32[576,128]{1,0:T(8,128)S(1)} %get-tuple-element.51), channel_id=1, source_target_pairs={{0,1},{1,0},{2,3},{3,2},{4,5},{5,4},{6,7},{7,6},{8,9},{9,8},{10,11... | collective-permute-start | bytes 884744 | tf_op jit(solution)/shard_map/ppermute | solution.py:54
  106.8 1.5 collective-permute-done.13
  108.4 23.4 %all_to_all.30 = f32[288,2,128]{2,1,0:T(2,128)S(1)} all-to-all(f32[288,2,128]{2,1,0:T(2,128)S(1)} %bitcast.24), channel_id=1, replica_groups={{0,2,4,6,64,66,68,70,128,130,132,134,192,194,196,198,256,258,260,262,32..., dimensions={0} | all-to-all | bytes 589824 | tf_op jit(solution)/shard_map/all_to_all | solution.py:60
  131.8 9.9 %all_to_all.31 = f32[72,2,128]{2,1,0:T(2,128)S(1)} all-to-all(f32[72,2,128]{2,1,0:T(2,128)S(1)} %bitcast.23), channel_id=1, replica_groups={{0,8,16,24,32,40,48,56},{1,9,17,25,33,41,49,57},{2,10,18,26,34,42,50,58..., dimensions={0} | all-to-all | bytes 147456 | tf_op jit(solution)/shard_map/all_to_all | solution.py:60
  142.4 5.1 %all-to-all-start.5 = ((f32[256,2,128]{2,1,0:T(2,128)}), f32[256,2,128]{2,1,0:T(2,128)S(1)}, u32[]{:S(2)}, u32[]{:S(2)}) async-start(f32[256,2,128]{2,1,0:T(2,128)} %bitcast.12), calls=%async_computation.5 | async-start | bytes 524288 | tf_op jit(solution)/shard_map/all_to_all | solution.py:60
  148.5 6.2 %collective-permute-start.10 = (f32[2,256,128]{2,1,0:T(8,128)S(1)}, f32[2,256,128]{2,1,0:T(8,128)S(1)}, u32[]{:S(2)}, u32[]{:S(2)}) collective-permute-start(f32[2,256,128]{2,1,0:T(8,128)S(1)} %get-tuple-element.46), channel_id=1, source_target_pairs={{0,1},{1,2},{2,3},{3,4},{4,5},{5,6},{6,7},{8,9},{9,10},{10,11},{11... | collective-permute-start | bytes 786440 | tf_op jit(solution)/shard_map/ppermute | solution.py:34
  154.7 2.2 %collective-permute-start.11 = (f32[2,128,256]{2,1,0:T(8,128)S(1)}, f32[2,128,256]{2,1,0:T(8,128)S(1)}, u32[]{:S(2)}, u32[]{:S(2)}) collective-permute-start(f32[2,128,256]{2,1,0:T(8,128)S(1)} %get-tuple-element.47), channel_id=1, source_target_pairs={{0,8},{1,9},{2,10},{3,11},{4,12},{5,13},{6,14},{7,15},{8,16},{9,17... | collective-permute-start | bytes 786440 | tf_op jit(solution)/shard_map/ppermute | solution.py:34
  157.4 6.0 %collective-permute-start.14 = (f32[512,128]{1,0:T(8,128)S(1)}, f32[512,128]{1,0:T(8,128)S(1)}, u32[]{:S(2)}, u32[]{:S(2)}) collective-permute-start(f32[512,128]{1,0:T(8,128)S(1)} %bitcast.19), channel_id=1, source_target_pairs={{0,1},{1,0},{2,3},{3,2},{4,5},{5,4},{6,7},{7,6},{8,9},{9,8},{10,11... | collective-permute-start | bytes 786440 | tf_op jit(solution)/shard_map/ppermute | solution.py:54
  163.4 2.1 %collective-permute-start.12 = (f32[2,128,128]{2,1,0:T(8,128)S(1)}, f32[2,128,128]{2,1,0:T(8,128)S(1)}, u32[]{:S(2)}, u32[]{:S(2)}) collective-permute-start(f32[2,128,128]{2,1,0:T(8,128)S(1)} %get-tuple-element.48), channel_id=1, source_target_pairs={{0,9},{1,10},{2,11},{3,12},{4,13},{5,14},{6,15},{8,17},{9,18},{10,... | collective-permute-start | bytes 393224 | tf_op jit(solution)/shard_map/ppermute | solution.py:34
  165.5 7.0 %collective-permute-done.12.from_corner = f32[2,128,128]{2,1,0:T(8,128)S(1)} collective-permute-done((f32[2,128,128]{2,1,0:T(8,128)S(1)}, f32[2,128,128]{2,1,0:T(8,128)S(1)}, u32[]{:S(2)}, u32[]{:S(2)}) %collective-permute-start.12) | collective-permute-done | bytes 131104 | tf_op jit(solution)/shard_map/ppermute | solution.py:34
  173.8 1.7 shard_map.99
  (58 shorter events, 22.2 us)
Async XLA Ops:
  0.6 1.0 copy-start
  1.7 22.4 %copy-start.2 = (bf16[8,256,256]{2,1,0:T(8,128)(2,1)S(1)}, bf16[8,256,256]{2,1,0:T(8,128)(2,1)}, u32[]{:S(2)}) copy-start(bf16[8,256,256]{2,1,0:T(8,128)(2,1)} %constant.10.clone.refs_7_.refs_9_) | copy-start | bytes 3145732
  2.5 21.6 %collective-permute-start = (f32[2,128,256]{2,1,0:T(8,128)}, f32[2,128,256]{2,1,0:T(8,128)S(1)}, u32[]{:S(2)}, u32[]{:S(2)}) collective-permute-start(f32[2,128,256]{2,1,0:T(8,128)} %get-tuple-element.28), channel_id=1, source_target_pairs={{8,0},{9,1},{10,2},{11,3},{12,4},{13,5},{14,6},{15,7},{16,8},{17,9... | collective-permute-start | bytes 786440 | tf_op jit(solution)/shard_map/ppermute | solution.py:34
  13.0 11.0 %collective-permute-start.1 = (f32[2,256,128]{2,1,0:T(8,128)S(1)}, f32[2,256,128]{2,1,0:T(8,128)S(1)}, u32[]{:S(2)}, u32[]{:S(2)}) collective-permute-start(f32[2,256,128]{2,1,0:T(8,128)S(1)} %get-tuple-element.29), channel_id=1, source_target_pairs={{1,0},{2,1},{3,2},{4,3},{5,4},{6,5},{7,6},{9,8},{10,9},{11,10},{12... | collective-permute-start | bytes 786440 | tf_op jit(solution)/shard_map/ppermute | solution.py:34
  15.9 8.2 %collective-permute-start.2 = (f32[2,128,128]{2,1,0:T(8,128)}, f32[2,128,128]{2,1,0:T(8,128)S(1)}, u32[]{:S(2)}, u32[]{:S(2)}) collective-permute-start(f32[2,128,128]{2,1,0:T(8,128)} %get-tuple-element.30), channel_id=1, source_target_pairs={{9,0},{10,1},{11,2},{12,3},{13,4},{14,5},{15,6},{17,8},{18,9},{19,... | collective-permute-start | bytes 393224 | tf_op jit(solution)/shard_map/ppermute | solution.py:34
  19.2 1.0 copy-start.7
  20.3 1.0 copy-start.8
  21.3 0.9 copy-start.15
  22.2 1.8 %copy-start.1 = (f32[2,256,256]{2,1,0:T(8,128)S(1)}, f32[2,256,256]{2,1,0:T(8,128)}, u32[]{:S(2)}) copy-start(f32[2,256,256]{2,1,0:T(8,128)} %tile.3) | copy-start | bytes 1572868
  28.2 1.0 copy-start.5
  29.2 3.5 %collective-permute-start.8 = (f32[576,128]{1,0:T(8,128)S(1)}, f32[576,128]{1,0:T(8,128)S(1)}, u32[]{:S(2)}, u32[]{:S(2)}) collective-permute-start(f32[576,128]{1,0:T(8,128)S(1)} %get-tuple-element.41), channel_id=1, source_target_pairs={{0,1},{1,0},{2,3},{3,2},{4,5},{5,4},{6,7},{7,6},{8,9},{9,8},{10,11... | collective-permute-start | bytes 884744 | tf_op jit(solution)/shard_map/ppermute | solution.py:54
  33.4 21.4 %all-to-all-start = ((f32[288,2,128]{2,1,0:T(2,128)}), f32[288,2,128]{2,1,0:T(2,128)S(1)}, u32[]{:S(2)}, u32[]{:S(2)}) async-start(f32[288,2,128]{2,1,0:T(2,128)} %bitcast.2), calls=%async_computation | async-start | bytes 589824 | tf_op jit(solution)/shard_map/all_to_all | solution.py:60
  42.8 1.2 copy-start.6
  45.8 29.3 %collective-permute-start.3 = (f32[2,256,128]{2,1,0:T(8,128)}, f32[2,256,128]{2,1,0:T(8,128)S(1)}, u32[]{:S(2)}, u32[]{:S(2)}) collective-permute-start(f32[2,256,128]{2,1,0:T(8,128)} %get-tuple-element.35), channel_id=1, source_target_pairs={{0,1},{1,2},{2,3},{3,4},{4,5},{5,6},{6,7},{8,9},{9,10},{10,11},{11... | collective-permute-start | bytes 786440 | tf_op jit(solution)/shard_map/ppermute | solution.py:34
  49.5 26.3 %collective-permute-start.4 = (f32[2,128,256]{2,1,0:T(8,128)}, f32[2,128,256]{2,1,0:T(8,128)S(1)}, u32[]{:S(2)}, u32[]{:S(2)}) collective-permute-start(f32[2,128,256]{2,1,0:T(8,128)} %get-tuple-element.36), channel_id=1, source_target_pairs={{0,8},{1,9},{2,10},{3,11},{4,12},{5,13},{6,14},{7,15},{8,16},{9,17... | collective-permute-start | bytes 786440 | tf_op jit(solution)/shard_map/ppermute | solution.py:34
  55.4 11.7 %all-to-all-start.1 = ((f32[72,2,128]{2,1,0:T(2,128)}), f32[72,2,128]{2,1,0:T(2,128)S(1)}, u32[]{:S(2)}, u32[]{:S(2)}) async-start(f32[72,2,128]{2,1,0:T(2,128)} %bitcast.4), calls=%async_computation.1 | async-start | bytes 147456 | tf_op jit(solution)/shard_map/all_to_all | solution.py:60
  59.8 15.3 %collective-permute-start.5 = (f32[2,128,128]{2,1,0:T(8,128)}, f32[2,128,128]{2,1,0:T(8,128)}, u32[]{:S(2)}, u32[]{:S(2)}) collective-permute-start(f32[2,128,128]{2,1,0:T(8,128)} %get-tuple-element.37), channel_id=1, source_target_pairs={{0,9},{1,10},{2,11},{3,12},{4,13},{5,14},{6,15},{8,17},{9,18},{10,... | collective-permute-start | bytes 393224 | tf_op jit(solution)/shard_map/ppermute | solution.py:34
  67.8 23.1 %all-to-all-start.2 = ((f32[256,2,128]{2,1,0:T(2,128)}), f32[256,2,128]{2,1,0:T(2,128)S(1)}, u32[]{:S(2)}, u32[]{:S(2)}) async-start(f32[256,2,128]{2,1,0:T(2,128)} %bitcast.6), calls=%async_computation.2 | async-start | bytes 524288 | tf_op jit(solution)/shard_map/all_to_all | solution.py:60
  76.5 0.9 copy-start.12
  77.5 0.9 copy-start.14
  79.4 8.8 %collective-permute-start.6 = (f32[2,256,128]{2,1,0:T(8,128)S(1)}, f32[2,256,128]{2,1,0:T(8,128)S(1)}, u32[]{:S(2)}, u32[]{:S(2)}) collective-permute-start(f32[2,256,128]{2,1,0:T(8,128)S(1)} %get-tuple-element.39), channel_id=1, source_target_pairs={{1,0},{2,1},{3,2},{4,3},{5,4},{6,5},{7,6},{9,8},{10,9},{11,10},{12... | collective-permute-start | bytes 786440 | tf_op jit(solution)/shard_map/ppermute | solution.py:34
  89.0 9.6 %collective-permute-start.7 = (f32[2,128,384]{2,1,0:T(8,128)}, f32[2,128,384]{2,1,0:T(8,128)S(1)}, u32[]{:S(2)}, u32[]{:S(2)}) collective-permute-start(f32[2,128,384]{2,1,0:T(8,128)} %shard_map.91), channel_id=1, source_target_pairs={{8,0},{9,1},{10,2},{11,3},{12,4},{13,5},{14,6},{15,7},{16,8},{17,9... | collective-permute-start | bytes 1179656 | tf_op jit(solution)/shard_map/ppermute | solution.py:34
  90.9 7.7 %collective-permute-start.9 = (f32[512,128]{1,0:T(8,128)S(1)}, f32[512,128]{1,0:T(8,128)S(1)}, u32[]{:S(2)}, u32[]{:S(2)}) collective-permute-start(f32[512,128]{1,0:T(8,128)S(1)} %bitcast.17), channel_id=1, source_target_pairs={{0,1},{1,0},{2,3},{3,2},{4,5},{5,4},{6,7},{7,6},{8,9},{9,8},{10,11... | collective-permute-start | bytes 786440 | tf_op jit(solution)/shard_map/ppermute | solution.py:54
  103.1 1.0 copy-start.3
  104.9 3.5 %collective-permute-start.13 = (f32[576,128]{1,0:T(8,128)S(1)}, f32[576,128]{1,0:T(8,128)S(1)}, u32[]{:S(2)}, u32[]{:S(2)}) collective-permute-start(f32[576,128]{1,0:T(8,128)S(1)} %get-tuple-element.51), channel_id=1, source_target_pairs={{0,1},{1,0},{2,3},{3,2},{4,5},{5,4},{6,7},{7,6},{8,9},{9,8},{10,11... | collective-permute-start | bytes 884744 | tf_op jit(solution)/shard_map/ppermute | solution.py:54
  108.4 39.1 %copy-start.4 = (f32[2,2,256,256]{3,2,1,0:T(8,128)S(1)}, f32[2,2,256,256]{3,2,1,0:T(8,128)}, u32[]{:S(2)}) copy-start(f32[2,2,256,256]{3,2,1,0:T(8,128)} %copy-done.3) | copy-start | bytes 3145732
  142.4 15.0 %all-to-all-start.5 = ((f32[256,2,128]{2,1,0:T(2,128)}), f32[256,2,128]{2,1,0:T(2,128)S(1)}, u32[]{:S(2)}, u32[]{:S(2)}) async-start(f32[256,2,128]{2,1,0:T(2,128)} %bitcast.12), calls=%async_computation.5 | async-start | bytes 524288 | tf_op jit(solution)/shard_map/all_to_all | solution.py:60
  148.5 24.1 %collective-permute-start.10 = (f32[2,256,128]{2,1,0:T(8,128)S(1)}, f32[2,256,128]{2,1,0:T(8,128)S(1)}, u32[]{:S(2)}, u32[]{:S(2)}) collective-permute-start(f32[2,256,128]{2,1,0:T(8,128)S(1)} %get-tuple-element.46), channel_id=1, source_target_pairs={{0,1},{1,2},{2,3},{3,4},{4,5},{5,6},{6,7},{8,9},{9,10},{10,11},{11... | collective-permute-start | bytes 786440 | tf_op jit(solution)/shard_map/ppermute | solution.py:34
  154.7 17.9 %collective-permute-start.11 = (f32[2,128,256]{2,1,0:T(8,128)S(1)}, f32[2,128,256]{2,1,0:T(8,128)S(1)}, u32[]{:S(2)}, u32[]{:S(2)}) collective-permute-start(f32[2,128,256]{2,1,0:T(8,128)S(1)} %get-tuple-element.47), channel_id=1, source_target_pairs={{0,8},{1,9},{2,10},{3,11},{4,12},{5,13},{6,14},{7,15},{8,16},{9,17... | collective-permute-start | bytes 786440 | tf_op jit(solution)/shard_map/ppermute | solution.py:34
  157.4 16.0 %collective-permute-start.14 = (f32[512,128]{1,0:T(8,128)S(1)}, f32[512,128]{1,0:T(8,128)S(1)}, u32[]{:S(2)}, u32[]{:S(2)}) collective-permute-start(f32[512,128]{1,0:T(8,128)S(1)} %bitcast.19), channel_id=1, source_target_pairs={{0,1},{1,0},{2,3},{3,2},{4,5},{5,4},{6,7},{7,6},{8,9},{9,8},{10,11... | collective-permute-start | bytes 786440 | tf_op jit(solution)/shard_map/ppermute | solution.py:54
  163.4 9.1 %collective-permute-start.12 = (f32[2,128,128]{2,1,0:T(8,128)S(1)}, f32[2,128,128]{2,1,0:T(8,128)S(1)}, u32[]{:S(2)}, u32[]{:S(2)}) collective-permute-start(f32[2,128,128]{2,1,0:T(8,128)S(1)} %get-tuple-element.48), channel_id=1, source_target_pairs={{0,9},{1,10},{2,11},{3,12},{4,13},{5,14},{6,15},{8,17},{9,18},{10,... | collective-permute-start | bytes 393224 | tf_op jit(solution)/shard_map/ppermute | solution.py:34
  172.6 1.2 copy-start.10
  (3 other events, 2.2 us)

commit v6 on v5

--- a/solution.py
+++ b/solution.py
@@ -300,7 +300,8 @@
     out[1] = imag
 
 
-def place_kernel(marks, tile, terms, partial, rim_right, rim_low, rim_corner, ext):
+def place_kernel(marks, tile, terms, partial, rim_right, rim_low, *rest):
+    ext = rest[-1]
     size = tile.shape[1]
     slots = terms.shape[0]
     ext[...] = jnp.zeros_like(ext)
@@ -310,18 +311,31 @@
         for part in range(2):
             add_window(ext, part, row, col, terms[slot, part])
     partial[...] = tile[...] + ext[:, :size, :size]
-    rim_right[...] = ext[:, :size, size:]
+    rim_right[...] = ext[:, : rim_right.shape[1], size:]
     rim_low[...] = ext[:, size : size + HALO, :size]
-    rim_corner[...] = ext[:, size : size + HALO, size:]
-
-
-def update_kernel(partial, from_left, from_above, from_corner, out, *side):
+    if len(rest) > 1:
+        rest[0][...] = ext[:, size : size + HALO, size:]
+
+
+def update_kernel(partial, from_left, from_above, from_corner, out, side):
     out[...] = partial[...]
     out[:, :, :HALO] += from_left[...]
     out[:, :HALO, :] += from_above[...]
     out[:, :HALO, :HALO] += from_corner[...]
-    if side:
-        side[0][...] = out[:, :, :HALO]
+    side[...] = out[:, :, :HALO]
+
+
+def merge_kernel(rim_low, from_left, out):
+    size = rim_low.shape[2]
+    out[...] = rim_low[...]
+    out[:, :, :HALO] += from_left[:, size:, :]
+
+
+def finish_kernel(partial, from_left, from_above, out):
+    size = partial.shape[1]
+    out[...] = partial[...]
+    out[:, :, :HALO] += from_left[:, :size, :]
+    out[:, :HALO, :] += from_above[...]
 
 
 def join_kernel(tile, right, out):
@@ -407,9 +421,14 @@
         if not first:
             probe_now = done[3]
         given = swap_cores(give)
-        partial, rim_right, rim_low, rim_corner = call(
+        last = outer_step == OUTER - 1
+        if last:
+            rim_shapes = [(2, size + margin, margin), edge_shapes[0]]
+        else:
+            rim_shapes = [edge_shapes[1], edge_shapes[0], edge_shapes[2]]
+        partial, rim_right, rim_low, *rim_corner = call(
             place_kernel,
-            [current.shape, edge_shapes[1], edge_shapes[0], edge_shapes[2]],
+            [current.shape] + rim_shapes,
             [SMEM, VMEM, VMEM],
             marks,
             current,
@@ -418,8 +437,14 @@
             grant=3,
         )
         from_left = shifted(rim_right, 0, 1)
-        from_above = shifted(rim_low, 1, 0)
-        from_corner = shifted(rim_corner, 1, 1)
+        if not last:
+            from_above = shifted(rim_low, 1, 0)
+            from_corner = shifted(rim_corner[0], 1, 1)
+        if last:
+            (merged,) = call(
+                merge_kernel, [edge_shapes[0]], [VMEM] * 2, rim_low, from_left
+            )
+            from_above = shifted(merged, 1, 0)
         arrived = exchange(keep + given, wide_groups)
         (copies,) = call(
             functools.partial(fold_kernel, wide, line, per + 2),
@@ -436,18 +461,26 @@
         )
         mine = exchange(copies, wide_groups)
         other = swap_cores(mine)
-        last = outer_step == OUTER - 1
-        current, *side = call(
-            update_kernel,
-            [current.shape] + ([] if last else [edge_shapes[1]]),
-            [VMEM] * 4,
-            partial,
-            from_left,
-            from_above,
-            from_corner,
-        )
-        if not last:
-            right = shifted(side[0], 0, -1)
+        if last:
+            (current,) = call(
+                finish_kernel,
+                [current.shape],
+                [VMEM] * 3,
+                partial,
+                from_left,
+                from_above,
+            )
+        else:
+            current, side = call(
+                update_kernel,
+                [current.shape, edge_shapes[1]],
+                [VMEM] * 4,
+                partial,
+                from_left,
+                from_above,
+                from_corner,
+            )
+            right = shifted(side, 0, -1)
             (joined,) = call(join_kernel, [(2, margin, size + margin)], [VMEM] * 2, current, right)
             low = shifted(joined, -1, 0)
     (probe_now,) = call(

time: 177 us -> 177 us (level)
  the two profiles are of different devices: /device:TPU:9 before, /device:TPU:34 now
where the time goes in v6:
time: 177 us; the launch traced here: 175 us
  starting transfers between devices  76 us (43%)
  waiting for transfers between devices  35 us (20%)
  blocking collectives  29.9 us (17%)
  Pallas kernels  19 us (11%)
  local copies, waits for them, and re-layouts  13 us (7%)
    all_to_all x4, starting transfers between devices, exchange(): lax.all_to_all(paired, ('row', 'col'), 0, 0, tiled=True, axis_index_group...  32.9 us
    ppermute x10, starting transfers between devices, shifted(): return lax.ppermute(value, ('row', 'col'), pairs)  32.4 us
    all_to_all x2, blocking collectives, exchange(): lax.all_to_all(paired, ('row', 'col'), 0, 0, tiled=True, axis_index_group...  29.9 us
    ppermute x10, waiting for transfers between devices, shifted(): return lax.ppermute(value, ('row', 'col'), pairs)  26.9 us
    pallas_call x15, Pallas kernels, call(): pl.pallas_call(kernel, out_shape=[jax.ShapeDtypeStruct(shape, jnp.float32...  19 us
    unnamed x32, local copies, waits for them, and re-layouts  12.2 us
    ppermute x4, starting transfers between devices, swap_cores(): return lax.ppermute(value, 'col', [(c, c ^ 1) for c in range(across)])  10.6 us
    all_to_all x4, waiting for transfers between devices, exchange(): lax.all_to_all(paired, ('row', 'col'), 0, 0, tiled=True, axis_index_group...  5.77 us
  transfers between devices with their start and end apart: 18, of which 8 were waited for; matrix products, arithmetic and copies ran while one was open for 0% of the time, Pallas kernels for 4%

profile of v6, /device:TPU:34, one launch (start us, length us, event | category | flops | bytes accessed | tf_op | source)
XLA Modules:
  0.0 175.3 jit_solution(18086703188050682915)
XLA Ops:
  2.5 10.8 %collective-permute-start = (f32[2,128,256]{2,1,0:T(8,128)}, f32[2,128,256]{2,1,0:T(8,128)S(1)}, u32[]{:S(2)}, u32[]{:S(2)}) collective-permute-start(f32[2,128,256]{2,1,0:T(8,128)} %get-tuple-element.27), channel_id=1, source_target_pairs={{8,0},{9,1},{10,2},{11,3},{12,4},{13,5},{14,6},{15,7},{16,8},{17,9... | collective-permute-start | bytes 786440 | tf_op jit(solution)/shard_map/ppermute | solution.py:34
  13.3 1.9 %collective-permute-start.1 = (f32[2,256,128]{2,1,0:T(8,128)S(1)}, f32[2,256,128]{2,1,0:T(8,128)S(1)}, u32[]{:S(2)}, u32[]{:S(2)}) collective-permute-start(f32[2,256,128]{2,1,0:T(8,128)S(1)} %get-tuple-element.28), channel_id=1, source_target_pairs={{1,0},{2,1},{3,2},{4,3},{5,4},{6,5},{7,6},{9,8},{10,9},{11,10},{12... | collective-permute-start | bytes 786440 | tf_op jit(solution)/shard_map/ppermute | solution.py:34
  15.2 2.5 %collective-permute-start.2 = (f32[2,128,128]{2,1,0:T(8,128)}, f32[2,128,128]{2,1,0:T(8,128)S(1)}, u32[]{:S(2)}, u32[]{:S(2)}) collective-permute-start(f32[2,128,128]{2,1,0:T(8,128)} %get-tuple-element.29), channel_id=1, source_target_pairs={{9,0},{10,1},{11,2},{12,3},{13,4},{14,5},{15,6},{17,8},{18,9},{19,... | collective-permute-start | bytes 393224 | tf_op jit(solution)/shard_map/ppermute | solution.py:34
  23.2 4.1 %shard_map.88 = (f32[576,128]{1,0:T(8,128)S(1)}, f32[576,128]{1,0:T(8,128)S(1)}, f32[2,2,256,256]{3,2,1,0:T(8,128)S(1)}) custom-call(s32[6]{0:T(128)S(1)} %pad_add_fusion.refs_0_.marks, f32[2,256,256]{2,1,0:T(8,128)S(1)} %copy-done.1, f32[2,128,256]{2,1,0:T(8,128)S(1)} %collective-permute-done.refs_2_, f32[2,256,128]{2,1,0:T(8,128)S(1)} %collective-permute-done.1.refs_3_, ...), custom_call_target="tpu_custom_call" | custom-call | tf_op jit(solution)/shard_map/pallas_call | solution.py:363
  28.3 2.6 %collective-permute-start.8 = (f32[576,128]{1,0:T(8,128)S(1)}, f32[576,128]{1,0:T(8,128)S(1)}, u32[]{:S(2)}, u32[]{:S(2)}) collective-permute-start(f32[576,128]{1,0:T(8,128)S(1)} %get-tuple-element.40), channel_id=1, source_target_pairs={{0,1},{1,0},{2,3},{3,2},{4,5},{5,4},{6,7},{7,6},{8,9},{9,8},{10,11... | collective-permute-start | bytes 884744 | tf_op jit(solution)/shard_map/ppermute | solution.py:54
  30.9 1.2 collective-permute-done.8
  32.9 9.6 %all-to-all-start = ((f32[288,2,128]{2,1,0:T(2,128)}), f32[288,2,128]{2,1,0:T(2,128)S(1)}, u32[]{:S(2)}, u32[]{:S(2)}) async-start(f32[288,2,128]{2,1,0:T(2,128)} %bitcast.2), calls=%async_computation | async-start | bytes 589824 | tf_op jit(solution)/shard_map/all_to_all | solution.py:60
  42.5 1.2 copy-done.6
  43.7 1.7 shard_map.89
  45.5 1.9 %collective-permute-start.3 = (f32[2,256,128]{2,1,0:T(8,128)}, f32[2,256,128]{2,1,0:T(8,128)S(1)}, u32[]{:S(2)}, u32[]{:S(2)}) collective-permute-start(f32[2,256,128]{2,1,0:T(8,128)} %get-tuple-element.34), channel_id=1, source_target_pairs={{0,1},{1,2},{2,3},{3,4},{4,5},{5,6},{6,7},{8,9},{9,10},{10,11},{11... | collective-permute-start | bytes 786440 | tf_op jit(solution)/shard_map/ppermute | solution.py:34
  47.4 3.4 %collective-permute-start.4 = (f32[2,128,256]{2,1,0:T(8,128)}, f32[2,128,256]{2,1,0:T(8,128)S(1)}, u32[]{:S(2)}, u32[]{:S(2)}) collective-permute-start(f32[2,128,256]{2,1,0:T(8,128)} %get-tuple-element.35), channel_id=1, source_target_pairs={{0,8},{1,9},{2,10},{3,11},{4,12},{5,13},{6,14},{7,15},{8,16},{9,17... | collective-permute-start | bytes 786440 | tf_op jit(solution)/shard_map/ppermute | solution.py:34
  52.0 4.6 %all-to-all-start.1 = ((f32[72,2,128]{2,1,0:T(2,128)}), f32[72,2,128]{2,1,0:T(2,128)S(1)}, u32[]{:S(2)}, u32[]{:S(2)}) async-start(f32[72,2,128]{2,1,0:T(2,128)} %bitcast.4), calls=%async_computation.1 | async-start | bytes 147456 | tf_op jit(solution)/shard_map/all_to_all | solution.py:60
  56.6 3.6 %collective-permute-start.5 = (f32[2,128,128]{2,1,0:T(8,128)}, f32[2,128,128]{2,1,0:T(8,128)}, u32[]{:S(2)}, u32[]{:S(2)}) collective-permute-start(f32[2,128,128]{2,1,0:T(8,128)} %get-tuple-element.36), channel_id=1, source_target_pairs={{0,9},{1,10},{2,11},{3,12},{4,13},{5,14},{6,15},{8,17},{9,18},{10,... | collective-permute-start | bytes 393224 | tf_op jit(solution)/shard_map/ppermute | solution.py:34
  60.3 5.2 %all-to-all-done.1 = f32[72,2,128]{2,1,0:T(2,128)S(1)} async-done(((f32[72,2,128]{2,1,0:T(2,128)}), f32[72,2,128]{2,1,0:T(2,128)S(1)}, u32[]{:S(2)}, u32[]{:S(2)}) %all-to-all-start.1) | async-done | bytes 73760 | tf_op jit(solution)/shard_map/all_to_all | solution.py:60
  66.2 9.5 %all-to-all-start.2 = ((f32[256,2,128]{2,1,0:T(2,128)}), f32[256,2,128]{2,1,0:T(2,128)S(1)}, u32[]{:S(2)}, u32[]{:S(2)}) async-start(f32[256,2,128]{2,1,0:T(2,128)} %bitcast.6), calls=%async_computation.2 | async-start | bytes 524288 | tf_op jit(solution)/shard_map/all_to_all | solution.py:60
  80.0 1.9 %collective-permute-start.6 = (f32[2,256,128]{2,1,0:T(8,128)S(1)}, f32[2,256,128]{2,1,0:T(8,128)S(1)}, u32[]{:S(2)}, u32[]{:S(2)}) collective-permute-start(f32[2,256,128]{2,1,0:T(8,128)S(1)} %get-tuple-element.38), channel_id=1, source_target_pairs={{1,0},{2,1},{3,2},{4,3},{5,4},{6,5},{7,6},{9,8},{10,9},{11,10},{12... | collective-permute-start | bytes 786440 | tf_op jit(solution)/shard_map/ppermute | solution.py:34
  81.9 3.9 %collective-permute-done.6.right.refs_3_ = f32[2,256,128]{2,1,0:T(8,128)S(1)} collective-permute-done((f32[2,256,128]{2,1,0:T(8,128)S(1)}, f32[2,256,128]{2,1,0:T(8,128)S(1)}, u32[]{:S(2)}, u32[]{:S(2)}) %collective-permute-start.6) | collective-permute-done | bytes 262176 | tf_op jit(solution)/shard_map/ppermute | solution.py:34
  86.6 1.9 %collective-permute-start.7 = (f32[2,128,384]{2,1,0:T(8,128)}, f32[2,128,384]{2,1,0:T(8,128)S(1)}, u32[]{:S(2)}, u32[]{:S(2)}) collective-permute-start(f32[2,128,384]{2,1,0:T(8,128)} %shard_map.91), channel_id=1, source_target_pairs={{8,0},{9,1},{10,2},{11,3},{12,4},{13,5},{14,6},{15,7},{16,8},{17,9... | collective-permute-start | bytes 1179656 | tf_op jit(solution)/shard_map/ppermute | solution.py:34
  88.5 3.6 %collective-permute-start.9 = (f32[512,128]{1,0:T(8,128)S(1)}, f32[512,128]{1,0:T(8,128)S(1)}, u32[]{:S(2)}, u32[]{:S(2)}) collective-permute-start(f32[512,128]{1,0:T(8,128)S(1)} %bitcast.17), channel_id=1, source_target_pairs={{0,1},{1,0},{2,3},{3,2},{4,5},{5,4},{6,7},{7,6},{8,9},{9,8},{10,11... | collective-permute-start | bytes 786440 | tf_op jit(solution)/shard_map/ppermute | solution.py:54
  92.2 7.7 %collective-permute-done.7.refs_2_ = f32[2,128,384]{2,1,0:T(8,128)S(1)} collective-permute-done((f32[2,128,384]{2,1,0:T(8,128)}, f32[2,128,384]{2,1,0:T(8,128)S(1)}, u32[]{:S(2)}, u32[]{:S(2)}) %collective-permute-start.7) | collective-permute-done | bytes 393248 | tf_op jit(solution)/shard_map/ppermute | solution.py:34
  99.9 4.4 %shard_map.94 = (f32[576,128]{1,0:T(8,128)S(1)}, f32[576,128]{1,0:T(8,128)S(1)}, f32[2,2,256,256]{3,2,1,0:T(8,128)S(1)}, f32[2,256,256]{2,1,0:T(8,128)S(1)}) custom-call(s32[6]{0:T(128)S(1)} %pad_add_fusion.refs_0_.marks, f32[2,256,256]{2,1,0:T(8,128)S(1)} %get-tuple-element.37.tile.refs_1_, f32[2,128,384]{2,1,0:T(8,128)S(1)} %collective-permute-done.7.refs_2_, ...), custom_call_target="tpu_custom_call" | custom-call | tf_op jit(solution)/shard_map/pallas_call | solution.py:363
  106.1 2.5 %collective-permute-start.12 = (f32[576,128]{1,0:T(8,128)S(1)}, f32[576,128]{1,0:T(8,128)S(1)}, u32[]{:S(2)}, u32[]{:S(2)}) collective-permute-start(f32[576,128]{1,0:T(8,128)S(1)} %get-tuple-element.49), channel_id=1, source_target_pairs={{0,1},{1,0},{2,3},{3,2},{4,5},{5,4},{6,7},{7,6},{8,9},{9,8},{10,11... | collective-permute-start | bytes 884744 | tf_op jit(solution)/shard_map/ppermute | solution.py:54
  108.6 1.2 collective-permute-done.12
  109.9 18.6 %all_to_all.30 = f32[288,2,128]{2,1,0:T(2,128)S(1)} all-to-all(f32[288,2,128]{2,1,0:T(2,128)S(1)} %bitcast.24), channel_id=1, replica_groups={{0,2,4,6,64,66,68,70,128,130,132,134,192,194,196,198,256,258,260,262,32..., dimensions={0} | all-to-all | bytes 589824 | tf_op jit(solution)/shard_map/all_to_all | solution.py:60
  128.5 11.3 %all_to_all.31 = f32[72,2,128]{2,1,0:T(2,128)S(1)} all-to-all(f32[72,2,128]{2,1,0:T(2,128)S(1)} %bitcast.23), channel_id=1, replica_groups={{0,8,16,24,32,40,48,56},{1,9,17,25,33,41,49,57},{2,10,18,26,34,42,50,58..., dimensions={0} | all-to-all | bytes 147456 | tf_op jit(solution)/shard_map/all_to_all | solution.py:60
  140.5 9.2 %all-to-all-start.5 = ((f32[256,2,128]{2,1,0:T(2,128)}), f32[256,2,128]{2,1,0:T(2,128)S(1)}, u32[]{:S(2)}, u32[]{:S(2)}) async-start(f32[256,2,128]{2,1,0:T(2,128)} %bitcast.12), calls=%async_computation.5 | async-start | bytes 524288 | tf_op jit(solution)/shard_map/all_to_all | solution.py:60
  150.7 1.9 %collective-permute-start.10 = (f32[2,384,128]{2,1,0:T(8,128)S(1)}, f32[2,384,128]{2,1,0:T(8,128)S(1)}, u32[]{:S(2)}, u32[]{:S(2)}) collective-permute-start(f32[2,384,128]{2,1,0:T(8,128)S(1)} %get-tuple-element.45), channel_id=1, source_target_pairs={{0,1},{1,2},{2,3},{3,4},{4,5},{5,6},{6,7},{8,9},{9,10},{10,11},{11... | collective-permute-start | bytes 1179656 | tf_op jit(solution)/shard_map/ppermute | solution.py:34
  152.7 7.2 %collective-permute-done.10.from_left = f32[2,384,128]{2,1,0:T(8,128)S(1)} collective-permute-done((f32[2,384,128]{2,1,0:T(8,128)S(1)}, f32[2,384,128]{2,1,0:T(8,128)S(1)}, u32[]{:S(2)}, u32[]{:S(2)}) %collective-permute-start.10) | collective-permute-done | bytes 393248 | tf_op jit(solution)/shard_map/ppermute | solution.py:34
  159.8 2.5 %collective-permute-start.11 = (f32[2,128,256]{2,1,0:T(8,128)S(1)}, f32[2,128,256]{2,1,0:T(8,128)S(1)}, u32[]{:S(2)}, u32[]{:S(2)}) collective-permute-start(f32[2,128,256]{2,1,0:T(8,128)S(1)} %shard_map.96), channel_id=1, source_target_pairs={{0,8},{1,9},{2,10},{3,11},{4,12},{5,13},{6,14},{7,15},{8,16},{9,17... | collective-permute-start | bytes 786440 | tf_op jit(solution)/shard_map/ppermute | solution.py:34
  162.3 1.9 %collective-permute-start.13 = (f32[512,128]{1,0:T(8,128)S(1)}, f32[512,128]{1,0:T(8,128)S(1)}, u32[]{:S(2)}, u32[]{:S(2)}) collective-permute-start(f32[512,128]{1,0:T(8,128)S(1)} %bitcast.19), channel_id=1, source_target_pairs={{0,1},{1,0},{2,3},{3,2},{4,5},{5,4},{6,7},{7,6},{8,9},{9,8},{10,11... | collective-permute-start | bytes 786440 | tf_op jit(solution)/shard_map/ppermute | solution.py:54
  164.3 8.1 %collective-permute-done.11.from_above = f32[2,128,256]{2,1,0:T(8,128)S(1)} collective-permute-done((f32[2,128,256]{2,1,0:T(8,128)S(1)}, f32[2,128,256]{2,1,0:T(8,128)S(1)}, u32[]{:S(2)}, u32[]{:S(2)}) %collective-permute-start.11) | collective-permute-done | bytes 262176 | tf_op jit(solution)/shard_map/ppermute | solution.py:34
  173.6 1.7 shard_map.100
  (57 shorter events, 20.3 us)
Async XLA Ops:
  0.6 1.0 copy-start
  1.7 21.0 %copy-start.2 = (bf16[8,256,256]{2,1,0:T(8,128)(2,1)S(1)}, bf16[8,256,256]{2,1,0:T(8,128)(2,1)}, u32[]{:S(2)}) copy-start(bf16[8,256,256]{2,1,0:T(8,128)(2,1)} %constant.10.clone.refs_7_.refs_9_) | copy-start | bytes 3145732
  2.5 20.2 %collective-permute-start = (f32[2,128,256]{2,1,0:T(8,128)}, f32[2,128,256]{2,1,0:T(8,128)S(1)}, u32[]{:S(2)}, u32[]{:S(2)}) collective-permute-start(f32[2,128,256]{2,1,0:T(8,128)} %get-tuple-element.27), channel_id=1, source_target_pairs={{8,0},{9,1},{10,2},{11,3},{12,4},{13,5},{14,6},{15,7},{16,8},{17,9... | collective-permute-start | bytes 786440 | tf_op jit(solution)/shard_map/ppermute | solution.py:34
  13.3 9.4 %collective-permute-start.1 = (f32[2,256,128]{2,1,0:T(8,128)S(1)}, f32[2,256,128]{2,1,0:T(8,128)S(1)}, u32[]{:S(2)}, u32[]{:S(2)}) collective-permute-start(f32[2,256,128]{2,1,0:T(8,128)S(1)} %get-tuple-element.28), channel_id=1, source_target_pairs={{1,0},{2,1},{3,2},{4,3},{5,4},{6,5},{7,6},{9,8},{10,9},{11,10},{12... | collective-permute-start | bytes 786440 | tf_op jit(solution)/shard_map/ppermute | solution.py:34
  15.2 7.5 %collective-permute-start.2 = (f32[2,128,128]{2,1,0:T(8,128)}, f32[2,128,128]{2,1,0:T(8,128)S(1)}, u32[]{:S(2)}, u32[]{:S(2)}) collective-permute-start(f32[2,128,128]{2,1,0:T(8,128)} %get-tuple-element.29), channel_id=1, source_target_pairs={{9,0},{10,1},{11,2},{12,3},{13,4},{14,5},{15,6},{17,8},{18,9},{19,... | collective-permute-start | bytes 393224 | tf_op jit(solution)/shard_map/ppermute | solution.py:34
  19.2 1.0 copy-start.7
  20.2 1.0 copy-start.8
  21.3 0.9 copy-start.15
  22.2 1.0 copy-start.1
  27.3 1.0 copy-start.5
  28.3 3.8 %collective-permute-start.8 = (f32[576,128]{1,0:T(8,128)S(1)}, f32[576,128]{1,0:T(8,128)S(1)}, u32[]{:S(2)}, u32[]{:S(2)}) collective-permute-start(f32[576,128]{1,0:T(8,128)S(1)} %get-tuple-element.40), channel_id=1, source_target_pairs={{0,1},{1,0},{2,3},{3,2},{4,5},{5,4},{6,7},{7,6},{8,9},{9,8},{10,11... | collective-permute-start | bytes 884744 | tf_op jit(solution)/shard_map/ppermute | solution.py:54
  32.9 18.5 %all-to-all-start = ((f32[288,2,128]{2,1,0:T(2,128)}), f32[288,2,128]{2,1,0:T(2,128)S(1)}, u32[]{:S(2)}, u32[]{:S(2)}) async-start(f32[288,2,128]{2,1,0:T(2,128)} %bitcast.2), calls=%async_computation | async-start | bytes 589824 | tf_op jit(solution)/shard_map/all_to_all | solution.py:60
  42.5 1.2 copy-start.6
  45.5 30.2 %collective-permute-start.3 = (f32[2,256,128]{2,1,0:T(8,128)}, f32[2,256,128]{2,1,0:T(8,128)S(1)}, u32[]{:S(2)}, u32[]{:S(2)}) collective-permute-start(f32[2,256,128]{2,1,0:T(8,128)} %get-tuple-element.34), channel_id=1, source_target_pairs={{0,1},{1,2},{2,3},{3,4},{4,5},{5,6},{6,7},{8,9},{9,10},{10,11},{11... | collective-permute-start | bytes 786440 | tf_op jit(solution)/shard_map/ppermute | solution.py:34
  47.4 29.0 %collective-permute-start.4 = (f32[2,128,256]{2,1,0:T(8,128)}, f32[2,128,256]{2,1,0:T(8,128)S(1)}, u32[]{:S(2)}, u32[]{:S(2)}) collective-permute-start(f32[2,128,256]{2,1,0:T(8,128)} %get-tuple-element.35), channel_id=1, source_target_pairs={{0,8},{1,9},{2,10},{3,11},{4,12},{5,13},{6,14},{7,15},{8,16},{9,17... | collective-permute-start | bytes 786440 | tf_op jit(solution)/shard_map/ppermute | solution.py:34
  52.0 13.4 %all-to-all-start.1 = ((f32[72,2,128]{2,1,0:T(2,128)}), f32[72,2,128]{2,1,0:T(2,128)S(1)}, u32[]{:S(2)}, u32[]{:S(2)}) async-start(f32[72,2,128]{2,1,0:T(2,128)} %bitcast.4), calls=%async_computation.1 | async-start | bytes 147456 | tf_op jit(solution)/shard_map/all_to_all | solution.py:60
  56.6 19.1 %collective-permute-start.5 = (f32[2,128,128]{2,1,0:T(8,128)}, f32[2,128,128]{2,1,0:T(8,128)}, u32[]{:S(2)}, u32[]{:S(2)}) collective-permute-start(f32[2,128,128]{2,1,0:T(8,128)} %get-tuple-element.36), channel_id=1, source_target_pairs={{0,9},{1,10},{2,11},{3,12},{4,13},{5,14},{6,15},{8,17},{9,18},{10,... | collective-permute-start | bytes 393224 | tf_op jit(solution)/shard_map/ppermute | solution.py:34
  66.2 22.3 %all-to-all-start.2 = ((f32[256,2,128]{2,1,0:T(2,128)}), f32[256,2,128]{2,1,0:T(2,128)S(1)}, u32[]{:S(2)}, u32[]{:S(2)}) async-start(f32[256,2,128]{2,1,0:T(2,128)} %bitcast.6), calls=%async_computation.2 | async-start | bytes 524288 | tf_op jit(solution)/shard_map/all_to_all | solution.py:60
  77.1 0.9 copy-start.12
  78.1 0.9 copy-start.14
  80.0 5.8 %collective-permute-start.6 = (f32[2,256,128]{2,1,0:T(8,128)S(1)}, f32[2,256,128]{2,1,0:T(8,128)S(1)}, u32[]{:S(2)}, u32[]{:S(2)}) collective-permute-start(f32[2,256,128]{2,1,0:T(8,128)S(1)} %get-tuple-element.38), channel_id=1, source_target_pairs={{1,0},{2,1},{3,2},{4,3},{5,4},{6,5},{7,6},{9,8},{10,9},{11,10},{12... | collective-permute-start | bytes 786440 | tf_op jit(solution)/shard_map/ppermute | solution.py:34
  86.6 13.3 %collective-permute-start.7 = (f32[2,128,384]{2,1,0:T(8,128)}, f32[2,128,384]{2,1,0:T(8,128)S(1)}, u32[]{:S(2)}, u32[]{:S(2)}) collective-permute-start(f32[2,128,384]{2,1,0:T(8,128)} %shard_map.91), channel_id=1, source_target_pairs={{8,0},{9,1},{10,2},{11,3},{12,4},{13,5},{14,6},{15,7},{16,8},{17,9... | collective-permute-start | bytes 1179656 | tf_op jit(solution)/shard_map/ppermute | solution.py:34
  88.5 11.4 %collective-permute-start.9 = (f32[512,128]{1,0:T(8,128)S(1)}, f32[512,128]{1,0:T(8,128)S(1)}, u32[]{:S(2)}, u32[]{:S(2)}) collective-permute-start(f32[512,128]{1,0:T(8,128)S(1)} %bitcast.17), channel_id=1, source_target_pairs={{0,1},{1,0},{2,3},{3,2},{4,5},{5,4},{6,7},{7,6},{8,9},{9,8},{10,11... | collective-permute-start | bytes 786440 | tf_op jit(solution)/shard_map/ppermute | solution.py:54
  104.3 1.0 copy-start.3
  105.3 0.8 copy-start.9
  106.1 3.7 %collective-permute-start.12 = (f32[576,128]{1,0:T(8,128)S(1)}, f32[576,128]{1,0:T(8,128)S(1)}, u32[]{:S(2)}, u32[]{:S(2)}) collective-permute-start(f32[576,128]{1,0:T(8,128)S(1)} %get-tuple-element.49), channel_id=1, source_target_pairs={{0,1},{1,0},{2,3},{3,2},{4,5},{5,4},{6,7},{7,6},{8,9},{9,8},{10,11... | collective-permute-start | bytes 884744 | tf_op jit(solution)/shard_map/ppermute | solution.py:54
  109.9 39.9 %copy-start.4 = (f32[2,2,256,256]{3,2,1,0:T(8,128)S(1)}, f32[2,2,256,256]{3,2,1,0:T(8,128)}, u32[]{:S(2)}) copy-start(f32[2,2,256,256]{3,2,1,0:T(8,128)} %copy-done.3) | copy-start | bytes 3145732
  140.5 21.8 %all-to-all-start.5 = ((f32[256,2,128]{2,1,0:T(2,128)}), f32[256,2,128]{2,1,0:T(2,128)S(1)}, u32[]{:S(2)}, u32[]{:S(2)}) async-start(f32[256,2,128]{2,1,0:T(2,128)} %bitcast.12), calls=%async_computation.5 | async-start | bytes 524288 | tf_op jit(solution)/shard_map/all_to_all | solution.py:60
  150.7 9.1 %collective-permute-start.10 = (f32[2,384,128]{2,1,0:T(8,128)S(1)}, f32[2,384,128]{2,1,0:T(8,128)S(1)}, u32[]{:S(2)}, u32[]{:S(2)}) collective-permute-start(f32[2,384,128]{2,1,0:T(8,128)S(1)} %get-tuple-element.45), channel_id=1, source_target_pairs={{0,1},{1,2},{2,3},{3,4},{4,5},{5,6},{6,7},{8,9},{9,10},{10,11},{11... | collective-permute-start | bytes 1179656 | tf_op jit(solution)/shard_map/ppermute | solution.py:34
  159.8 12.5 %collective-permute-start.11 = (f32[2,128,256]{2,1,0:T(8,128)S(1)}, f32[2,128,256]{2,1,0:T(8,128)S(1)}, u32[]{:S(2)}, u32[]{:S(2)}) collective-permute-start(f32[2,128,256]{2,1,0:T(8,128)S(1)} %shard_map.96), channel_id=1, source_target_pairs={{0,8},{1,9},{2,10},{3,11},{4,12},{5,13},{6,14},{7,15},{8,16},{9,17... | collective-permute-start | bytes 786440 | tf_op jit(solution)/shard_map/ppermute | solution.py:34
  162.3 10.9 %collective-permute-start.13 = (f32[512,128]{1,0:T(8,128)S(1)}, f32[512,128]{1,0:T(8,128)S(1)}, u32[]{:S(2)}, u32[]{:S(2)}) collective-permute-start(f32[512,128]{1,0:T(8,128)S(1)} %bitcast.19), channel_id=1, source_target_pairs={{0,1},{1,0},{2,3},{3,2},{4,5},{5,4},{6,7},{7,6},{8,9},{9,8},{10,11... | collective-permute-start | bytes 786440 | tf_op jit(solution)/shard_map/ppermute | solution.py:54
  172.4 1.2 copy-start.10
  (2 other events, 1.4 us)

commit v7 on v6

--- a/solution.py
+++ b/solution.py
@@ -180,12 +180,12 @@
     half = size // 2
     slots = amp.shape[0]
     ext[:, :size, :size] = tile[...]
-    ext[:, :size, size:] = right[...]
+    ext[:, size : size + HALO, :size] = low[...]
     if first:
-        ext[:, size : size + HALO, :size] = low[...]
+        ext[:, :size, size:] = right[...]
         ext[:, size : size + HALO, size:] = corner[...]
     else:
-        ext[:, size : size + HALO, :] = low[...]
+        ext[:, : size + HALO, size:] = right[...]
     ext[:, size + HALO :, :] = jnp.zeros((2, SUB, size + HALO), jnp.float32)
 
     if first:
@@ -317,12 +317,12 @@
         rest[0][...] = ext[:, size : size + HALO, size:]
 
 
-def update_kernel(partial, from_left, from_above, from_corner, out, side):
+def update_kernel(partial, from_left, from_above, from_corner, out, below):
     out[...] = partial[...]
     out[:, :, :HALO] += from_left[...]
     out[:, :HALO, :] += from_above[...]
     out[:, :HALO, :HALO] += from_corner[...]
-    side[...] = out[:, :, :HALO]
+    below[...] = out[:, :HALO, :]
 
 
 def merge_kernel(rim_low, from_left, out):
@@ -338,10 +338,10 @@
     out[:, :HALO, :] += from_above[...]
 
 
-def join_kernel(tile, right, out):
+def join_kernel(tile, low, out):
     size = tile.shape[1]
-    out[:, :, :size] = tile[:, :HALO, :]
-    out[:, :, size:] = right[:, :HALO, :]
+    out[:, :size, :] = tile[:, :, :HALO]
+    out[:, size:, :] = low[:, :, :HALO]
 
 
 def fold_kernel(members, copies, keep, source, out, *power):
@@ -471,18 +471,20 @@
                 from_above,
             )
         else:
-            current, side = call(
+            current, below = call(
                 update_kernel,
-                [current.shape, edge_shapes[1]],
+                [current.shape, edge_shapes[0]],
                 [VMEM] * 4,
                 partial,
                 from_left,
                 from_above,
                 from_corner,
             )
-            right = shifted(side, 0, -1)
-            (joined,) = call(join_kernel, [(2, margin, size + margin)], [VMEM] * 2, current, right)
-            low = shifted(joined, -1, 0)
+            low = shifted(below, -1, 0)
+            (joined,) = call(
+                join_kernel, [(2, size + margin, margin)], [VMEM] * 2, current, low
+            )
+            right = shifted(joined, 0, -1)
     (probe_now,) = call(
         probe_kernel,
         [probe_field.shape],

time: 177 us -> 175 us (0.989)
  no operation moved by 1% of the time
where the time goes in v7:
time: 175 us; the launch traced here: 174 us
  starting transfers between devices  75.7 us (43%)
  waiting for transfers between devices  33.7 us (19%)
  blocking collectives  29.7 us (17%)
  Pallas kernels  19 us (11%)
  local copies, waits for them, and re-layouts  13 us (7%)
    all_to_all x4, starting transfers between devices, exchange(): lax.all_to_all(paired, ('row', 'col'), 0, 0, tiled=True, axis_index_group...  32.9 us
    ppermute x10, starting transfers between devices, shifted(): return lax.ppermute(value, ('row', 'col'), pairs)  32.4 us
    all_to_all x2, blocking collectives, exchange(): lax.all_to_all(paired, ('row', 'col'), 0, 0, tiled=True, axis_index_group...  29.7 us
    ppermute x10, waiting for transfers between devices, shifted(): return lax.ppermute(value, ('row', 'col'), pairs)  25.5 us
    pallas_call x15, Pallas kernels, call(): pl.pallas_call(kernel, out_shape=[jax.ShapeDtypeStruct(shape, jnp.float32...  19 us
    unnamed x32, local copies, waits for them, and re-layouts  12.2 us
    ppermute x4, starting transfers between devices, swap_cores(): return lax.ppermute(value, 'col', [(c, c ^ 1) for c in range(across)])  10.4 us
    all_to_all x4, waiting for transfers between devices, exchange(): lax.all_to_all(paired, ('row', 'col'), 0, 0, tiled=True, axis_index_group...  5.77 us
  transfers between devices with their start and end apart: 18, of which 8 were waited for; matrix products, arithmetic and copies ran while one was open for 0% of the time, Pallas kernels for 4%

profile of v7, /device:TPU:34, one launch (start us, length us, event | category | flops | bytes accessed | tf_op | source)
XLA Modules:
  0.0 173.5 jit_solution(1819205478833803477)
XLA Ops:
  2.5 10.8 %collective-permute-start = (f32[2,128,256]{2,1,0:T(8,128)}, f32[2,128,256]{2,1,0:T(8,128)S(1)}, u32[]{:S(2)}, u32[]{:S(2)}) collective-permute-start(f32[2,128,256]{2,1,0:T(8,128)} %get-tuple-element.27), channel_id=1, source_target_pairs={{8,0},{9,1},{10,2},{11,3},{12,4},{13,5},{14,6},{15,7},{16,8},{17,9... | collective-permute-start | bytes 786440 | tf_op jit(solution)/shard_map/ppermute | solution.py:34
  13.3 1.9 %collective-permute-start.1 = (f32[2,256,128]{2,1,0:T(8,128)S(1)}, f32[2,256,128]{2,1,0:T(8,128)S(1)}, u32[]{:S(2)}, u32[]{:S(2)}) collective-permute-start(f32[2,256,128]{2,1,0:T(8,128)S(1)} %get-tuple-element.28), channel_id=1, source_target_pairs={{1,0},{2,1},{3,2},{4,3},{5,4},{6,5},{7,6},{9,8},{10,9},{11,10},{12... | collective-permute-start | bytes 786440 | tf_op jit(solution)/shard_map/ppermute | solution.py:34
  15.2 2.5 %collective-permute-start.2 = (f32[2,128,128]{2,1,0:T(8,128)}, f32[2,128,128]{2,1,0:T(8,128)S(1)}, u32[]{:S(2)}, u32[]{:S(2)}) collective-permute-start(f32[2,128,128]{2,1,0:T(8,128)} %get-tuple-element.29), channel_id=1, source_target_pairs={{9,0},{10,1},{11,2},{12,3},{13,4},{14,5},{15,6},{17,8},{18,9},{19,... | collective-permute-start | bytes 393224 | tf_op jit(solution)/shard_map/ppermute | solution.py:34
  23.2 4.1 %shard_map.88 = (f32[576,128]{1,0:T(8,128)S(1)}, f32[576,128]{1,0:T(8,128)S(1)}, f32[2,2,256,256]{3,2,1,0:T(8,128)S(1)}) custom-call(s32[6]{0:T(128)S(1)} %pad_add_fusion.refs_0_.marks, f32[2,256,256]{2,1,0:T(8,128)S(1)} %copy-done.1, f32[2,128,256]{2,1,0:T(8,128)S(1)} %collective-permute-done.refs_2_, f32[2,256,128]{2,1,0:T(8,128)S(1)} %collective-permute-done.1.refs_3_, ...), custom_call_target="tpu_custom_call" | custom-call | tf_op jit(solution)/shard_map/pallas_call | solution.py:363
  28.3 2.6 %collective-permute-start.8 = (f32[576,128]{1,0:T(8,128)S(1)}, f32[576,128]{1,0:T(8,128)S(1)}, u32[]{:S(2)}, u32[]{:S(2)}) collective-permute-start(f32[576,128]{1,0:T(8,128)S(1)} %get-tuple-element.40), channel_id=1, source_target_pairs={{0,1},{1,0},{2,3},{3,2},{4,5},{5,4},{6,7},{7,6},{8,9},{9,8},{10,11... | collective-permute-start | bytes 884744 | tf_op jit(solution)/shard_map/ppermute | solution.py:54
  30.9 1.2 collective-permute-done.8
  32.9 9.6 %all-to-all-start = ((f32[288,2,128]{2,1,0:T(2,128)}), f32[288,2,128]{2,1,0:T(2,128)S(1)}, u32[]{:S(2)}, u32[]{:S(2)}) async-start(f32[288,2,128]{2,1,0:T(2,128)} %bitcast.2), calls=%async_computation | async-start | bytes 589824 | tf_op jit(solution)/shard_map/all_to_all | solution.py:60
  42.5 1.2 copy-done.6
  43.7 1.7 %shard_map.89 = (f32[2,256,256]{2,1,0:T(8,128)S(1)}, f32[2,256,128]{2,1,0:T(8,128)}, f32[2,128,256]{2,1,0:T(8,128)}, f32[2,128,128]{2,1,0:T(8,128)}) custom-call(s32[6]{0:T(128)S(1)} %pad_add_fusion.refs_0_.marks, f32[2,256,256]{2,1,0:T(8,128)S(1)} %copy-done.1, f32[2,2,256,256]{3,2,1,0:T(8,128)S(1)} %copy-done.6), custom_call_target="tpu_custom_call" | custom-call | tf_op jit(solution)/shard_map/pallas_call | solution.py:363
  45.5 1.9 %collective-permute-start.3 = (f32[2,256,128]{2,1,0:T(8,128)}, f32[2,256,128]{2,1,0:T(8,128)S(1)}, u32[]{:S(2)}, u32[]{:S(2)}) collective-permute-start(f32[2,256,128]{2,1,0:T(8,128)} %get-tuple-element.34), channel_id=1, source_target_pairs={{0,1},{1,2},{2,3},{3,4},{4,5},{5,6},{6,7},{8,9},{9,10},{10,11},{11... | collective-permute-start | bytes 786440 | tf_op jit(solution)/shard_map/ppermute | solution.py:34
  47.4 3.4 %collective-permute-start.4 = (f32[2,128,256]{2,1,0:T(8,128)}, f32[2,128,256]{2,1,0:T(8,128)S(1)}, u32[]{:S(2)}, u32[]{:S(2)}) collective-permute-start(f32[2,128,256]{2,1,0:T(8,128)} %get-tuple-element.35), channel_id=1, source_target_pairs={{0,8},{1,9},{2,10},{3,11},{4,12},{5,13},{6,14},{7,15},{8,16},{9,17... | collective-permute-start | bytes 786440 | tf_op jit(solution)/shard_map/ppermute | solution.py:34
  52.0 4.6 %all-to-all-start.1 = ((f32[72,2,128]{2,1,0:T(2,128)}), f32[72,2,128]{2,1,0:T(2,128)S(1)}, u32[]{:S(2)}, u32[]{:S(2)}) async-start(f32[72,2,128]{2,1,0:T(2,128)} %bitcast.4), calls=%async_computation.1 | async-start | bytes 147456 | tf_op jit(solution)/shard_map/all_to_all | solution.py:60
  56.6 3.6 %collective-permute-start.5 = (f32[2,128,128]{2,1,0:T(8,128)}, f32[2,128,128]{2,1,0:T(8,128)}, u32[]{:S(2)}, u32[]{:S(2)}) collective-permute-start(f32[2,128,128]{2,1,0:T(8,128)} %get-tuple-element.36), channel_id=1, source_target_pairs={{0,9},{1,10},{2,11},{3,12},{4,13},{5,14},{6,15},{8,17},{9,18},{10,... | collective-permute-start | bytes 393224 | tf_op jit(solution)/shard_map/ppermute | solution.py:34
  60.3 5.2 %all-to-all-done.1 = f32[72,2,128]{2,1,0:T(2,128)S(1)} async-done(((f32[72,2,128]{2,1,0:T(2,128)}), f32[72,2,128]{2,1,0:T(2,128)S(1)}, u32[]{:S(2)}, u32[]{:S(2)}) %all-to-all-start.1) | async-done | bytes 73760 | tf_op jit(solution)/shard_map/all_to_all | solution.py:60
  66.2 9.5 %all-to-all-start.2 = ((f32[256,2,128]{2,1,0:T(2,128)}), f32[256,2,128]{2,1,0:T(2,128)S(1)}, u32[]{:S(2)}, u32[]{:S(2)}) async-start(f32[256,2,128]{2,1,0:T(2,128)} %bitcast.6), calls=%async_computation.2 | async-start | bytes 524288 | tf_op jit(solution)/shard_map/all_to_all | solution.py:60
  80.0 1.9 %collective-permute-start.6 = (f32[2,128,256]{2,1,0:T(8,128)S(1)}, f32[2,128,256]{2,1,0:T(8,128)S(1)}, u32[]{:S(2)}, u32[]{:S(2)}) collective-permute-start(f32[2,128,256]{2,1,0:T(8,128)S(1)} %get-tuple-element.38), channel_id=1, source_target_pairs={{8,0},{9,1},{10,2},{11,3},{12,4},{13,5},{14,6},{15,7},{16,8},{17,9... | collective-permute-start | bytes 786440 | tf_op jit(solution)/shard_map/ppermute | solution.py:34
  81.9 7.1 %collective-permute-done.6.low.refs_2_ = f32[2,128,256]{2,1,0:T(8,128)S(1)} collective-permute-done((f32[2,128,256]{2,1,0:T(8,128)S(1)}, f32[2,128,256]{2,1,0:T(8,128)S(1)}, u32[]{:S(2)}, u32[]{:S(2)}) %collective-permute-start.6) | collective-permute-done | bytes 262176 | tf_op jit(solution)/shard_map/ppermute | solution.py:34
  89.8 1.9 %collective-permute-start.7 = (f32[2,384,128]{2,1,0:T(8,128)}, f32[2,384,128]{2,1,0:T(8,128)S(1)}, u32[]{:S(2)}, u32[]{:S(2)}) collective-permute-start(f32[2,384,128]{2,1,0:T(8,128)} %shard_map.91), channel_id=1, source_target_pairs={{1,0},{2,1},{3,2},{4,3},{5,4},{6,5},{7,6},{9,8},{10,9},{11,10},{12... | collective-permute-start | bytes 1179656 | tf_op jit(solution)/shard_map/ppermute | solution.py:34
  91.7 2.4 %collective-permute-start.9 = (f32[512,128]{1,0:T(8,128)S(1)}, f32[512,128]{1,0:T(8,128)S(1)}, u32[]{:S(2)}, u32[]{:S(2)}) collective-permute-start(f32[512,128]{1,0:T(8,128)S(1)} %bitcast.17), channel_id=1, source_target_pairs={{0,1},{1,0},{2,3},{3,2},{4,5},{5,4},{6,7},{7,6},{8,9},{9,8},{10,11... | collective-permute-start | bytes 786440 | tf_op jit(solution)/shard_map/ppermute | solution.py:54
  94.1 3.2 %collective-permute-done.7.refs_3_ = f32[2,384,128]{2,1,0:T(8,128)S(1)} collective-permute-done((f32[2,384,128]{2,1,0:T(8,128)}, f32[2,384,128]{2,1,0:T(8,128)S(1)}, u32[]{:S(2)}, u32[]{:S(2)}) %collective-permute-start.7) | collective-permute-done | bytes 393248 | tf_op jit(solution)/shard_map/ppermute | solution.py:34
  97.3 4.4 %shard_map.94 = (f32[576,128]{1,0:T(8,128)S(1)}, f32[576,128]{1,0:T(8,128)S(1)}, f32[2,2,256,256]{3,2,1,0:T(8,128)S(1)}, f32[2,256,256]{2,1,0:T(8,128)S(1)}) custom-call(s32[6]{0:T(128)S(1)} %pad_add_fusion.refs_0_.marks, f32[2,256,256]{2,1,0:T(8,128)S(1)} %get-tuple-element.37.tile.refs_1_, f32[2,128,256]{2,1,0:T(8,128)S(1)} %collective-permute-done.6.low.refs_2_, ...), custom_call_target="tpu_custom_call" | custom-call | tf_op jit(solution)/shard_map/pallas_call | solution.py:363
  103.5 3.5 %collective-permute-start.12 = (f32[576,128]{1,0:T(8,128)S(1)}, f32[576,128]{1,0:T(8,128)S(1)}, u32[]{:S(2)}, u32[]{:S(2)}) collective-permute-start(f32[576,128]{1,0:T(8,128)S(1)} %get-tuple-element.49), channel_id=1, source_target_pairs={{0,1},{1,0},{2,3},{3,2},{4,5},{5,4},{6,7},{7,6},{8,9},{9,8},{10,11... | collective-permute-start | bytes 884744 | tf_op jit(solution)/shard_map/ppermute | solution.py:54
  107.1 1.2 collective-permute-done.12
  108.3 18.3 %all_to_all.30 = f32[288,2,128]{2,1,0:T(2,128)S(1)} all-to-all(f32[288,2,128]{2,1,0:T(2,128)S(1)} %bitcast.24), channel_id=1, replica_groups={{0,2,4,6,64,66,68,70,128,130,132,134,192,194,196,198,256,258,260,262,32..., dimensions={0} | all-to-all | bytes 589824 | tf_op jit(solution)/shard_map/all_to_all | solution.py:60
  126.6 11.4 %all_to_all.31 = f32[72,2,128]{2,1,0:T(2,128)S(1)} all-to-all(f32[72,2,128]{2,1,0:T(2,128)S(1)} %bitcast.23), channel_id=1, replica_groups={{0,8,16,24,32,40,48,56},{1,9,17,25,33,41,49,57},{2,10,18,26,34,42,50,58..., dimensions={0} | all-to-all | bytes 147456 | tf_op jit(solution)/shard_map/all_to_all | solution.py:60
  138.8 9.2 %all-to-all-start.5 = ((f32[256,2,128]{2,1,0:T(2,128)}), f32[256,2,128]{2,1,0:T(2,128)S(1)}, u32[]{:S(2)}, u32[]{:S(2)}) async-start(f32[256,2,128]{2,1,0:T(2,128)} %bitcast.12), calls=%async_computation.5 | async-start | bytes 524288 | tf_op jit(solution)/shard_map/all_to_all | solution.py:60
  149.0 1.9 %collective-permute-start.10 = (f32[2,384,128]{2,1,0:T(8,128)S(1)}, f32[2,384,128]{2,1,0:T(8,128)S(1)}, u32[]{:S(2)}, u32[]{:S(2)}) collective-permute-start(f32[2,384,128]{2,1,0:T(8,128)S(1)} %get-tuple-element.45), channel_id=1, source_target_pairs={{0,1},{1,2},{2,3},{3,4},{4,5},{5,6},{6,7},{8,9},{9,10},{10,11},{11... | collective-permute-start | bytes 1179656 | tf_op jit(solution)/shard_map/ppermute | solution.py:34
  150.9 7.2 %collective-permute-done.10.from_left = f32[2,384,128]{2,1,0:T(8,128)S(1)} collective-permute-done((f32[2,384,128]{2,1,0:T(8,128)S(1)}, f32[2,384,128]{2,1,0:T(8,128)S(1)}, u32[]{:S(2)}, u32[]{:S(2)}) %collective-permute-start.10) | collective-permute-done | bytes 393248 | tf_op jit(solution)/shard_map/ppermute | solution.py:34
  158.1 2.5 %collective-permute-start.11 = (f32[2,128,256]{2,1,0:T(8,128)S(1)}, f32[2,128,256]{2,1,0:T(8,128)S(1)}, u32[]{:S(2)}, u32[]{:S(2)}) collective-permute-start(f32[2,128,256]{2,1,0:T(8,128)S(1)} %shard_map.96), channel_id=1, source_target_pairs={{0,8},{1,9},{2,10},{3,11},{4,12},{5,13},{6,14},{7,15},{8,16},{9,17... | collective-permute-start | bytes 786440 | tf_op jit(solution)/shard_map/ppermute | solution.py:34
  160.6 1.9 %collective-permute-start.13 = (f32[512,128]{1,0:T(8,128)S(1)}, f32[512,128]{1,0:T(8,128)S(1)}, u32[]{:S(2)}, u32[]{:S(2)}) collective-permute-start(f32[512,128]{1,0:T(8,128)S(1)} %bitcast.19), channel_id=1, source_target_pairs={{0,1},{1,0},{2,3},{3,2},{4,5},{5,4},{6,7},{7,6},{8,9},{9,8},{10,11... | collective-permute-start | bytes 786440 | tf_op jit(solution)/shard_map/ppermute | solution.py:54
  162.5 8.1 %collective-permute-done.11.from_above = f32[2,128,256]{2,1,0:T(8,128)S(1)} collective-permute-done((f32[2,128,256]{2,1,0:T(8,128)S(1)}, f32[2,128,256]{2,1,0:T(8,128)S(1)}, u32[]{:S(2)}, u32[]{:S(2)}) %collective-permute-start.11) | collective-permute-done | bytes 262176 | tf_op jit(solution)/shard_map/ppermute | solution.py:34
  171.9 1.7 shard_map.100
  (57 shorter events, 20.3 us)
Async XLA Ops:
  0.6 1.0 copy-start
  1.7 21.0 %copy-start.2 = (bf16[8,256,256]{2,1,0:T(8,128)(2,1)S(1)}, bf16[8,256,256]{2,1,0:T(8,128)(2,1)}, u32[]{:S(2)}) copy-start(bf16[8,256,256]{2,1,0:T(8,128)(2,1)} %constant.10.clone.refs_7_.refs_9_) | copy-start | bytes 3145732
  2.5 20.2 %collective-permute-start = (f32[2,128,256]{2,1,0:T(8,128)}, f32[2,128,256]{2,1,0:T(8,128)S(1)}, u32[]{:S(2)}, u32[]{:S(2)}) collective-permute-start(f32[2,128,256]{2,1,0:T(8,128)} %get-tuple-element.27), channel_id=1, source_target_pairs={{8,0},{9,1},{10,2},{11,3},{12,4},{13,5},{14,6},{15,7},{16,8},{17,9... | collective-permute-start | bytes 786440 | tf_op jit(solution)/shard_map/ppermute | solution.py:34
  13.3 9.4 %collective-permute-start.1 = (f32[2,256,128]{2,1,0:T(8,128)S(1)}, f32[2,256,128]{2,1,0:T(8,128)S(1)}, u32[]{:S(2)}, u32[]{:S(2)}) collective-permute-start(f32[2,256,128]{2,1,0:T(8,128)S(1)} %get-tuple-element.28), channel_id=1, source_target_pairs={{1,0},{2,1},{3,2},{4,3},{5,4},{6,5},{7,6},{9,8},{10,9},{11,10},{12... | collective-permute-start | bytes 786440 | tf_op jit(solution)/shard_map/ppermute | solution.py:34
  15.2 7.5 %collective-permute-start.2 = (f32[2,128,128]{2,1,0:T(8,128)}, f32[2,128,128]{2,1,0:T(8,128)S(1)}, u32[]{:S(2)}, u32[]{:S(2)}) collective-permute-start(f32[2,128,128]{2,1,0:T(8,128)} %get-tuple-element.29), channel_id=1, source_target_pairs={{9,0},{10,1},{11,2},{12,3},{13,4},{14,5},{15,6},{17,8},{18,9},{19,... | collective-permute-start | bytes 393224 | tf_op jit(solution)/shard_map/ppermute | solution.py:34
  19.2 1.0 copy-start.7
  20.2 1.0 copy-start.8
  21.3 0.9 copy-start.15
  22.2 1.0 copy-start.1
  27.3 1.0 copy-start.5
  28.3 3.8 %collective-permute-start.8 = (f32[576,128]{1,0:T(8,128)S(1)}, f32[576,128]{1,0:T(8,128)S(1)}, u32[]{:S(2)}, u32[]{:S(2)}) collective-permute-start(f32[576,128]{1,0:T(8,128)S(1)} %get-tuple-element.40), channel_id=1, source_target_pairs={{0,1},{1,0},{2,3},{3,2},{4,5},{5,4},{6,7},{7,6},{8,9},{9,8},{10,11... | collective-permute-start | bytes 884744 | tf_op jit(solution)/shard_map/ppermute | solution.py:54
  32.9 18.5 %all-to-all-start = ((f32[288,2,128]{2,1,0:T(2,128)}), f32[288,2,128]{2,1,0:T(2,128)S(1)}, u32[]{:S(2)}, u32[]{:S(2)}) async-start(f32[288,2,128]{2,1,0:T(2,128)} %bitcast.2), calls=%async_computation | async-start | bytes 589824 | tf_op jit(solution)/shard_map/all_to_all | solution.py:60
  42.5 1.2 copy-start.6
  45.5 30.2 %collective-permute-start.3 = (f32[2,256,128]{2,1,0:T(8,128)}, f32[2,256,128]{2,1,0:T(8,128)S(1)}, u32[]{:S(2)}, u32[]{:S(2)}) collective-permute-start(f32[2,256,128]{2,1,0:T(8,128)} %get-tuple-element.34), channel_id=1, source_target_pairs={{0,1},{1,2},{2,3},{3,4},{4,5},{5,6},{6,7},{8,9},{9,10},{10,11},{11... | collective-permute-start | bytes 786440 | tf_op jit(solution)/shard_map/ppermute | solution.py:34
  47.4 29.0 %collective-permute-start.4 = (f32[2,128,256]{2,1,0:T(8,128)}, f32[2,128,256]{2,1,0:T(8,128)S(1)}, u32[]{:S(2)}, u32[]{:S(2)}) collective-permute-start(f32[2,128,256]{2,1,0:T(8,128)} %get-tuple-element.35), channel_id=1, source_target_pairs={{0,8},{1,9},{2,10},{3,11},{4,12},{5,13},{6,14},{7,15},{8,16},{9,17... | collective-permute-start | bytes 786440 | tf_op jit(solution)/shard_map/ppermute | solution.py:34
  52.0 13.4 %all-to-all-start.1 = ((f32[72,2,128]{2,1,0:T(2,128)}), f32[72,2,128]{2,1,0:T(2,128)S(1)}, u32[]{:S(2)}, u32[]{:S(2)}) async-start(f32[72,2,128]{2,1,0:T(2,128)} %bitcast.4), calls=%async_computation.1 | async-start | bytes 147456 | tf_op jit(solution)/shard_map/all_to_all | solution.py:60
  56.6 19.1 %collective-permute-start.5 = (f32[2,128,128]{2,1,0:T(8,128)}, f32[2,128,128]{2,1,0:T(8,128)}, u32[]{:S(2)}, u32[]{:S(2)}) collective-permute-start(f32[2,128,128]{2,1,0:T(8,128)} %get-tuple-element.36), channel_id=1, source_target_pairs={{0,9},{1,10},{2,11},{3,12},{4,13},{5,14},{6,15},{8,17},{9,18},{10,... | collective-permute-start | bytes 393224 | tf_op jit(solution)/shard_map/ppermute | solution.py:34
  66.2 25.5 %all-to-all-start.2 = ((f32[256,2,128]{2,1,0:T(2,128)}), f32[256,2,128]{2,1,0:T(2,128)S(1)}, u32[]{:S(2)}, u32[]{:S(2)}) async-start(f32[256,2,128]{2,1,0:T(2,128)} %bitcast.6), calls=%async_computation.2 | async-start | bytes 524288 | tf_op jit(solution)/shard_map/all_to_all | solution.py:60
  77.1 0.9 copy-start.12
  78.1 0.9 copy-start.14
  80.0 9.0 %collective-permute-start.6 = (f32[2,128,256]{2,1,0:T(8,128)S(1)}, f32[2,128,256]{2,1,0:T(8,128)S(1)}, u32[]{:S(2)}, u32[]{:S(2)}) collective-permute-start(f32[2,128,256]{2,1,0:T(8,128)S(1)} %get-tuple-element.38), channel_id=1, source_target_pairs={{8,0},{9,1},{10,2},{11,3},{12,4},{13,5},{14,6},{15,7},{16,8},{17,9... | collective-permute-start | bytes 786440 | tf_op jit(solution)/shard_map/ppermute | solution.py:34
  89.8 7.5 %collective-permute-start.7 = (f32[2,384,128]{2,1,0:T(8,128)}, f32[2,384,128]{2,1,0:T(8,128)S(1)}, u32[]{:S(2)}, u32[]{:S(2)}) collective-permute-start(f32[2,384,128]{2,1,0:T(8,128)} %shard_map.91), channel_id=1, source_target_pairs={{1,0},{2,1},{3,2},{4,3},{5,4},{6,5},{7,6},{9,8},{10,9},{11,10},{12... | collective-permute-start | bytes 1179656 | tf_op jit(solution)/shard_map/ppermute | solution.py:34
  91.7 5.6 %collective-permute-start.9 = (f32[512,128]{1,0:T(8,128)S(1)}, f32[512,128]{1,0:T(8,128)S(1)}, u32[]{:S(2)}, u32[]{:S(2)}) collective-permute-start(f32[512,128]{1,0:T(8,128)S(1)} %bitcast.17), channel_id=1, source_target_pairs={{0,1},{1,0},{2,3},{3,2},{4,5},{5,4},{6,7},{7,6},{8,9},{9,8},{10,11... | collective-permute-start | bytes 786440 | tf_op jit(solution)/shard_map/ppermute | solution.py:54
  101.7 1.0 copy-start.3
  102.8 0.8 copy-start.9
  103.5 4.7 %collective-permute-start.12 = (f32[576,128]{1,0:T(8,128)S(1)}, f32[576,128]{1,0:T(8,128)S(1)}, u32[]{:S(2)}, u32[]{:S(2)}) collective-permute-start(f32[576,128]{1,0:T(8,128)S(1)} %get-tuple-element.49), channel_id=1, source_target_pairs={{0,1},{1,0},{2,3},{3,2},{4,5},{5,4},{6,7},{7,6},{8,9},{9,8},{10,11... | collective-permute-start | bytes 884744 | tf_op jit(solution)/shard_map/ppermute | solution.py:54
  108.3 39.7 %copy-start.4 = (f32[2,2,256,256]{3,2,1,0:T(8,128)S(1)}, f32[2,2,256,256]{3,2,1,0:T(8,128)}, u32[]{:S(2)}) copy-start(f32[2,2,256,256]{3,2,1,0:T(8,128)} %copy-done.3) | copy-start | bytes 3145732
  138.8 21.8 %all-to-all-start.5 = ((f32[256,2,128]{2,1,0:T(2,128)}), f32[256,2,128]{2,1,0:T(2,128)S(1)}, u32[]{:S(2)}, u32[]{:S(2)}) async-start(f32[256,2,128]{2,1,0:T(2,128)} %bitcast.12), calls=%async_computation.5 | async-start | bytes 524288 | tf_op jit(solution)/shard_map/all_to_all | solution.py:60
  149.0 9.1 %collective-permute-start.10 = (f32[2,384,128]{2,1,0:T(8,128)S(1)}, f32[2,384,128]{2,1,0:T(8,128)S(1)}, u32[]{:S(2)}, u32[]{:S(2)}) collective-permute-start(f32[2,384,128]{2,1,0:T(8,128)S(1)} %get-tuple-element.45), channel_id=1, source_target_pairs={{0,1},{1,2},{2,3},{3,4},{4,5},{5,6},{6,7},{8,9},{9,10},{10,11},{11... | collective-permute-start | bytes 1179656 | tf_op jit(solution)/shard_map/ppermute | solution.py:34
  158.1 12.5 %collective-permute-start.11 = (f32[2,128,256]{2,1,0:T(8,128)S(1)}, f32[2,128,256]{2,1,0:T(8,128)S(1)}, u32[]{:S(2)}, u32[]{:S(2)}) collective-permute-start(f32[2,128,256]{2,1,0:T(8,128)S(1)} %shard_map.96), channel_id=1, source_target_pairs={{0,8},{1,9},{2,10},{3,11},{4,12},{5,13},{6,14},{7,15},{8,16},{9,17... | collective-permute-start | bytes 786440 | tf_op jit(solution)/shard_map/ppermute | solution.py:34
  160.6 10.9 %collective-permute-start.13 = (f32[512,128]{1,0:T(8,128)S(1)}, f32[512,128]{1,0:T(8,128)S(1)}, u32[]{:S(2)}, u32[]{:S(2)}) collective-permute-start(f32[512,128]{1,0:T(8,128)S(1)} %bitcast.19), channel_id=1, source_target_pairs={{0,1},{1,0},{2,3},{3,2},{4,5},{5,4},{6,7},{7,6},{8,9},{9,8},{10,11... | collective-permute-start | bytes 786440 | tf_op jit(solution)/shard_map/ppermute | solution.py:54
  170.6 1.2 copy-start.10
  (2 other events, 1.4 us)

commit v8 on v7

--- a/solution.py
+++ b/solution.py
@@ -90,8 +90,19 @@
     return jnp.dot(left, right, preferred_element_type=jnp.float32)
 
 
-def mul3(left, right):
-    return mul(left[0], right[0]) + (mul(left[0], right[1]) + mul(left[1], right[0]))
+def right_mul(data, tables, at):
+    high, low = split(data)
+    rows = data.shape[0]
+    both = mul(jnp.concatenate([high, low], axis=0), tables[at * 2])
+    return both[:rows] + (both[rows:] + mul(high, tables[at * 2 + 1]))
+
+
+def left_mul(tables, at, data):
+    high, low = split(data)
+    rows = data.shape[0]
+    table = tables[at * 2 : at * 2 + 2].reshape(2 * rows, rows)
+    both = mul(table, high)
+    return both[:rows] + (both[rows:] + mul(tables[at * 2], low))
 
 
 def edges_kernel(tile, low, right, corner):
@@ -198,72 +209,83 @@
     mean = jnp.sum(p_real * p_real + p_imag * p_imag) / (size * size)
     scale = object_step / (mean + tiny_value)
 
-    even, even_t, odd, odd_t = (
-        (tables[2 * n], tables[2 * n + 1]) for n in range(4)
-    )
-    pg_real = jnp.zeros((size, size), jnp.float32)
-    pg_imag = jnp.zeros((size, size), jnp.float32)
+    even, even_t, odd, odd_t = range(4)
+    z_real, z_imag, psi = [], [], []
     power_sum = jnp.zeros((), jnp.float32)
     for slot in range(slots):
         row = jnp.clip(marks[2 + 2 * slot], 0, HALO)
         col = jnp.clip(marks[3 + 2 * slot], 0, HALO)
+        z_r = take_window(ext, 0, row, col, size)
+        z_i = take_window(ext, 1, row, col, size)
+        window_power = jnp.sum(z_r * z_r + z_i * z_i)
+        power_sum = power_sum + jnp.where(slot < marks[0], window_power, 0.0)
+        psi.append((p_real * z_r - p_imag * z_i, p_real * z_i + p_imag * z_r))
+        z_real.append(z_r)
+        z_imag.append(z_i)
+
+    def both(make):
+        return jnp.concatenate([make(*psi[slot]) for slot in range(slots)], axis=0)
+
+    a_even = right_mul(
+        both(lambda r, i: jnp.concatenate([r[:, :half] + r[:, half:], i[:, :half] + i[:, half:]], axis=1)),
+        tables,
+        even,
+    )
+    a_odd = right_mul(
+        both(lambda r, i: jnp.concatenate([r[:, :half] - r[:, half:], i[:, :half] - i[:, half:]], axis=1)),
+        tables,
+        odd,
+    )
+    plus, minus = [], []
+    for slot in range(slots):
+        top = slice(slot * size, slot * size + half)
+        bottom = slice(slot * size + half, (slot + 1) * size)
+        up = jnp.concatenate([a_even[top], a_odd[top]], axis=1)
+        down = jnp.concatenate([a_even[bottom], a_odd[bottom]], axis=1)
+        total, rest = up + down, up - down
+        for out, value in ((plus, total), (minus, rest)):
+            real = jnp.concatenate([value[:, :half], value[:, size : size + half]], axis=1)
+            imag = jnp.concatenate([value[:, half:size], value[:, size + half :]], axis=1)
+            out.append(jnp.concatenate([real, imag], axis=0))
+    sums = []
+    for part, (data, table, back) in enumerate(((plus, even_t, even), (minus, odd_t, odd))):
+        hat = left_mul(tables, table, jnp.concatenate(data, axis=1))
+        h_real = hat[:half]
+        h_imag = hat[half:]
+        magnitude = h_real * h_real + h_imag * h_imag
+        measured = jnp.concatenate(
+            [amp[slot, part * half : (part + 1) * half, :] for slot in range(slots)], axis=1
+        )
+        ratio = measured * lax.rsqrt(magnitude + smooth_floor) - 1.0
+        scaled = jnp.concatenate([h_real * ratio, h_imag * ratio], axis=0)
+        sums.append(left_mul(tables, back, scaled))
+    top = sums[0] + sums[1]
+    bottom = sums[0] - sums[1]
+    stacked = []
+    for side in range(2):
+        rows = []
+        for slot in range(slots):
+            columns = slice(slot * size + side * half, slot * size + (side + 1) * half)
+            for value in (top, bottom):
+                rows.append(jnp.concatenate([value[:half, columns], value[half:, columns]], axis=1))
+        stacked.append(jnp.concatenate(rows, axis=0))
+    u = right_mul(stacked[0], tables, even_t)
+    v = right_mul(stacked[1], tables, odd_t)
+    plus = u + v
+    minus = u - v
+    pg_real = jnp.zeros((size, size), jnp.float32)
+    pg_imag = jnp.zeros((size, size), jnp.float32)
+    for slot in range(slots):
         live = slot < marks[0]
-        z_real = take_window(ext, 0, row, col, size)
-        z_imag = take_window(ext, 1, row, col, size)
-        psi_real = p_real * z_real - p_imag * z_imag
-        psi_imag = p_real * z_imag + p_imag * z_real
-        plus = jnp.concatenate(
-            [psi_real[:, :half] + psi_real[:, half:], psi_imag[:, :half] + psi_imag[:, half:]], axis=1
-        )
-        minus = jnp.concatenate(
-            [psi_real[:, :half] - psi_real[:, half:], psi_imag[:, :half] - psi_imag[:, half:]], axis=1
-        )
-        a_even = mul3(split(plus), even)
-        a_odd = mul3(split(minus), odd)
-        y_real = jnp.concatenate([a_even[:, :half], a_odd[:, :half]], axis=1)
-        y_imag = jnp.concatenate([a_even[:, half:], a_odd[:, half:]], axis=1)
-        plus = jnp.concatenate([y_real[:half] + y_real[half:], y_imag[:half] + y_imag[half:]], axis=0)
-        minus = jnp.concatenate([y_real[:half] - y_real[half:], y_imag[:half] - y_imag[half:]], axis=0)
-        sums = []
-        for part, (data, table, back) in enumerate(((plus, even_t, even), (minus, odd_t, odd))):
-            hat = mul3(table, split(data))
-            h_real = hat[:half]
-            h_imag = hat[half:]
-            magnitude = h_real * h_real + h_imag * h_imag
-            measured = amp[slot, part * half : (part + 1) * half, :]
-            ratio = measured * lax.rsqrt(magnitude + smooth_floor) - 1.0
-            scaled = jnp.concatenate([h_real * ratio, h_imag * ratio], axis=0)
-            sums.append(mul3(back, split(scaled)))
-        top = sums[0] + sums[1]
-        bottom = sums[0] - sums[1]
-        z_even = jnp.concatenate(
-            [
-                jnp.concatenate([top[:half, :half], top[half:, :half]], axis=1),
-                jnp.concatenate([bottom[:half, :half], bottom[half:, :half]], axis=1),
-            ],
-            axis=0,
-        )
-        z_odd = jnp.concatenate(
-            [
-                jnp.concatenate([top[:half, half:], top[half:, half:]], axis=1),
-                jnp.concatenate([bottom[:half, half:], bottom[half:, half:]], axis=1),
-            ],
-            axis=0,
-        )
-        u = mul3(split(z_even), even_t)
-        v = mul3(split(z_odd), odd_t)
-        plus = u + v
-        minus = u - v
-        d_real = jnp.concatenate([plus[:, :half], minus[:, :half]], axis=1)
-        d_imag = jnp.concatenate([plus[:, half:], minus[:, half:]], axis=1)
+        rows = slice(slot * size, (slot + 1) * size)
+        d_real = jnp.concatenate([plus[rows, :half], minus[rows, :half]], axis=1)
+        d_imag = jnp.concatenate([plus[rows, half:], minus[rows, half:]], axis=1)
         d_real = jnp.where(live, d_real, 0.0)
         d_imag = jnp.where(live, d_imag, 0.0)
-        pg_real = pg_real + (z_real * d_real + z_imag * d_imag)
-        pg_imag = pg_imag + (z_real * d_imag - z_imag * d_real)
+        pg_real = pg_real + (z_real[slot] * d_real + z_imag[slot] * d_imag)
+        pg_imag = pg_imag + (z_real[slot] * d_imag - z_imag[slot] * d_real)
         terms[slot, 0] = (p_real * d_real + p_imag * d_imag) * scale
         terms[slot, 1] = (p_real * d_imag - p_imag * d_real) * scale
-        window_power = jnp.sum(z_real * z_real + z_imag * z_imag)
-        power_sum = power_sum + jnp.where(live, window_power, 0.0)
 
     second = marks[1] == 1
     per = 2 * size // members
@@ -436,10 +458,10 @@
             scratch=[(2, size + margin + SUB, size + margin)],
             grant=3,
         )
+        if not last:
+            from_corner = shifted(rim_corner[0], 1, 1)
+            from_above = shifted(rim_low, 1, 0)
         from_left = shifted(rim_right, 0, 1)
-        if not last:
-            from_above = shifted(rim_low, 1, 0)
-            from_corner = shifted(rim_corner[0], 1, 1)
         if last:
             (merged,) = call(
                 merge_kernel, [edge_shapes[0]], [VMEM] * 2, rim_low, from_left
@@ -481,9 +503,7 @@
                 from_corner,
             )
             low = shifted(below, -1, 0)
-            (joined,) = call(
-                join_kernel, [(2, size + margin, margin)], [VMEM] * 2, current, low
-            )
+            (joined,) = call(join_kernel, [(2, size + margin, margin)], [VMEM] * 2, current, low)
             right = shifted(joined, 0, -1)
     (probe_now,) = call(
         probe_kernel,

time: 175 us -> 174 us (level)
  no operation moved by 1% of the time
where the time goes in v8:
time: 174 us; the launch traced here: 172 us
  starting transfers between devices  75.7 us (44%)
  waiting for transfers between devices  33.7 us (19%)
  blocking collectives  29.7 us (17%)
  Pallas kernels  17.8 us (10%)
  local copies, waits for them, and re-layouts  13 us (7%)
    all_to_all x4, starting transfers between devices, exchange(): lax.all_to_all(paired, ('row', 'col'), 0, 0, tiled=True, axis_index_group...  32.9 us
    ppermute x10, starting transfers between devices, shifted(): return lax.ppermute(value, ('row', 'col'), pairs)  32.4 us
    all_to_all x2, blocking collectives, exchange(): lax.all_to_all(paired, ('row', 'col'), 0, 0, tiled=True, axis_index_group...  29.7 us
    ppermute x10, waiting for transfers between devices, shifted(): return lax.ppermute(value, ('row', 'col'), pairs)  25.5 us
    pallas_call x15, Pallas kernels, call(): pl.pallas_call(kernel, out_shape=[jax.ShapeDtypeStruct(shape, jnp.float32...  17.8 us
    unnamed x32, local copies, waits for them, and re-layouts  12.2 us
    ppermute x4, starting transfers between devices, swap_cores(): return lax.ppermute(value, 'col', [(c, c ^ 1) for c in range(across)])  10.4 us
    all_to_all x4, waiting for transfers between devices, exchange(): lax.all_to_all(paired, ('row', 'col'), 0, 0, tiled=True, axis_index_group...  5.76 us
  transfers between devices with their start and end apart: 18, of which 8 were waited for; matrix products, arithmetic and copies ran while one was open for 0% of the time, Pallas kernels for 4%

profile of v8, /device:TPU:34, one launch (start us, length us, event | category | flops | bytes accessed | tf_op | source)
XLA Modules:
  0.0 172.4 jit_solution(7671541492315850115)
XLA Ops:
  2.5 10.8 %collective-permute-start = (f32[2,128,256]{2,1,0:T(8,128)}, f32[2,128,256]{2,1,0:T(8,128)S(1)}, u32[]{:S(2)}, u32[]{:S(2)}) collective-permute-start(f32[2,128,256]{2,1,0:T(8,128)} %get-tuple-element.27), channel_id=1, source_target_pairs={{8,0},{9,1},{10,2},{11,3},{12,4},{13,5},{14,6},{15,7},{16,8},{17,9... | collective-permute-start | bytes 786440 | tf_op jit(solution)/shard_map/ppermute | solution.py:34
  13.3 1.9 %collective-permute-start.1 = (f32[2,256,128]{2,1,0:T(8,128)S(1)}, f32[2,256,128]{2,1,0:T(8,128)S(1)}, u32[]{:S(2)}, u32[]{:S(2)}) collective-permute-start(f32[2,256,128]{2,1,0:T(8,128)S(1)} %get-tuple-element.28), channel_id=1, source_target_pairs={{1,0},{2,1},{3,2},{4,3},{5,4},{6,5},{7,6},{9,8},{10,9},{11,10},{12... | collective-permute-start | bytes 786440 | tf_op jit(solution)/shard_map/ppermute | solution.py:34
  15.2 2.5 %collective-permute-start.2 = (f32[2,128,128]{2,1,0:T(8,128)}, f32[2,128,128]{2,1,0:T(8,128)S(1)}, u32[]{:S(2)}, u32[]{:S(2)}) collective-permute-start(f32[2,128,128]{2,1,0:T(8,128)} %get-tuple-element.29), channel_id=1, source_target_pairs={{9,0},{10,1},{11,2},{12,3},{13,4},{14,5},{15,6},{17,8},{18,9},{19,... | collective-permute-start | bytes 393224 | tf_op jit(solution)/shard_map/ppermute | solution.py:34
  23.2 3.5 %shard_map.88 = (f32[576,128]{1,0:T(8,128)S(1)}, f32[576,128]{1,0:T(8,128)S(1)}, f32[2,2,256,256]{3,2,1,0:T(8,128)S(1)}) custom-call(s32[6]{0:T(128)S(1)} %pad_add_fusion.refs_0_.marks, f32[2,256,256]{2,1,0:T(8,128)S(1)} %copy-done.1, f32[2,128,256]{2,1,0:T(8,128)S(1)} %collective-permute-done.refs_2_, f32[2,256,128]{2,1,0:T(8,128)S(1)} %collective-permute-done.1.refs_3_, ...), custom_call_target="tpu_custom_call" | custom-call | tf_op jit(solution)/shard_map/pallas_call | solution.py:385
  27.8 2.6 %collective-permute-start.8 = (f32[576,128]{1,0:T(8,128)S(1)}, f32[576,128]{1,0:T(8,128)S(1)}, u32[]{:S(2)}, u32[]{:S(2)}) collective-permute-start(f32[576,128]{1,0:T(8,128)S(1)} %get-tuple-element.40), channel_id=1, source_target_pairs={{0,1},{1,0},{2,3},{3,2},{4,5},{5,4},{6,7},{7,6},{8,9},{9,8},{10,11... | collective-permute-start | bytes 884744 | tf_op jit(solution)/shard_map/ppermute | solution.py:54
  30.4 1.2 collective-permute-done.8
  32.3 9.6 %all-to-all-start = ((f32[288,2,128]{2,1,0:T(2,128)}), f32[288,2,128]{2,1,0:T(2,128)S(1)}, u32[]{:S(2)}, u32[]{:S(2)}) async-start(f32[288,2,128]{2,1,0:T(2,128)} %bitcast.2), calls=%async_computation | async-start | bytes 589824 | tf_op jit(solution)/shard_map/all_to_all | solution.py:60
  41.9 1.2 copy-done.6
  43.2 1.7 %shard_map.89 = (f32[2,256,256]{2,1,0:T(8,128)S(1)}, f32[2,256,128]{2,1,0:T(8,128)}, f32[2,128,256]{2,1,0:T(8,128)}, f32[2,128,128]{2,1,0:T(8,128)}) custom-call(s32[6]{0:T(128)S(1)} %pad_add_fusion.refs_0_.marks, f32[2,256,256]{2,1,0:T(8,128)S(1)} %copy-done.1, f32[2,2,256,256]{3,2,1,0:T(8,128)S(1)} %copy-done.6), custom_call_target="tpu_custom_call" | custom-call | tf_op jit(solution)/shard_map/pallas_call | solution.py:385
  44.9 1.9 %collective-permute-start.3 = (f32[2,256,128]{2,1,0:T(8,128)}, f32[2,256,128]{2,1,0:T(8,128)S(1)}, u32[]{:S(2)}, u32[]{:S(2)}) collective-permute-start(f32[2,256,128]{2,1,0:T(8,128)} %get-tuple-element.34), channel_id=1, source_target_pairs={{0,1},{1,2},{2,3},{3,4},{4,5},{5,6},{6,7},{8,9},{9,10},{10,11},{11... | collective-permute-start | bytes 786440 | tf_op jit(solution)/shard_map/ppermute | solution.py:34
  46.8 3.4 %collective-permute-start.4 = (f32[2,128,256]{2,1,0:T(8,128)}, f32[2,128,256]{2,1,0:T(8,128)S(1)}, u32[]{:S(2)}, u32[]{:S(2)}) collective-permute-start(f32[2,128,256]{2,1,0:T(8,128)} %get-tuple-element.35), channel_id=1, source_target_pairs={{0,8},{1,9},{2,10},{3,11},{4,12},{5,13},{6,14},{7,15},{8,16},{9,17... | collective-permute-start | bytes 786440 | tf_op jit(solution)/shard_map/ppermute | solution.py:34
  51.5 4.6 %all-to-all-start.1 = ((f32[72,2,128]{2,1,0:T(2,128)}), f32[72,2,128]{2,1,0:T(2,128)S(1)}, u32[]{:S(2)}, u32[]{:S(2)}) async-start(f32[72,2,128]{2,1,0:T(2,128)} %bitcast.4), calls=%async_computation.1 | async-start | bytes 147456 | tf_op jit(solution)/shard_map/all_to_all | solution.py:60
  56.1 3.6 %collective-permute-start.5 = (f32[2,128,128]{2,1,0:T(8,128)}, f32[2,128,128]{2,1,0:T(8,128)}, u32[]{:S(2)}, u32[]{:S(2)}) collective-permute-start(f32[2,128,128]{2,1,0:T(8,128)} %get-tuple-element.36), channel_id=1, source_target_pairs={{0,9},{1,10},{2,11},{3,12},{4,13},{5,14},{6,15},{8,17},{9,18},{10,... | collective-permute-start | bytes 393224 | tf_op jit(solution)/shard_map/ppermute | solution.py:34
  59.7 5.2 %all-to-all-done.1 = f32[72,2,128]{2,1,0:T(2,128)S(1)} async-done(((f32[72,2,128]{2,1,0:T(2,128)}), f32[72,2,128]{2,1,0:T(2,128)S(1)}, u32[]{:S(2)}, u32[]{:S(2)}) %all-to-all-start.1) | async-done | bytes 73760 | tf_op jit(solution)/shard_map/all_to_all | solution.py:60
  65.6 9.5 %all-to-all-start.2 = ((f32[256,2,128]{2,1,0:T(2,128)}), f32[256,2,128]{2,1,0:T(2,128)S(1)}, u32[]{:S(2)}, u32[]{:S(2)}) async-start(f32[256,2,128]{2,1,0:T(2,128)} %bitcast.6), calls=%async_computation.2 | async-start | bytes 524288 | tf_op jit(solution)/shard_map/all_to_all | solution.py:60
  79.4 1.9 %collective-permute-start.6 = (f32[2,128,256]{2,1,0:T(8,128)S(1)}, f32[2,128,256]{2,1,0:T(8,128)S(1)}, u32[]{:S(2)}, u32[]{:S(2)}) collective-permute-start(f32[2,128,256]{2,1,0:T(8,128)S(1)} %get-tuple-element.38), channel_id=1, source_target_pairs={{8,0},{9,1},{10,2},{11,3},{12,4},{13,5},{14,6},{15,7},{16,8},{17,9... | collective-permute-start | bytes 786440 | tf_op jit(solution)/shard_map/ppermute | solution.py:34
  81.4 7.1 %collective-permute-done.6.low.refs_2_ = f32[2,128,256]{2,1,0:T(8,128)S(1)} collective-permute-done((f32[2,128,256]{2,1,0:T(8,128)S(1)}, f32[2,128,256]{2,1,0:T(8,128)S(1)}, u32[]{:S(2)}, u32[]{:S(2)}) %collective-permute-start.6) | collective-permute-done | bytes 262176 | tf_op jit(solution)/shard_map/ppermute | solution.py:34
  89.2 1.9 %collective-permute-start.7 = (f32[2,384,128]{2,1,0:T(8,128)}, f32[2,384,128]{2,1,0:T(8,128)S(1)}, u32[]{:S(2)}, u32[]{:S(2)}) collective-permute-start(f32[2,384,128]{2,1,0:T(8,128)} %shard_map.91), channel_id=1, source_target_pairs={{1,0},{2,1},{3,2},{4,3},{5,4},{6,5},{7,6},{9,8},{10,9},{11,10},{12... | collective-permute-start | bytes 1179656 | tf_op jit(solution)/shard_map/ppermute | solution.py:34
  91.1 2.4 %collective-permute-start.9 = (f32[512,128]{1,0:T(8,128)S(1)}, f32[512,128]{1,0:T(8,128)S(1)}, u32[]{:S(2)}, u32[]{:S(2)}) collective-permute-start(f32[512,128]{1,0:T(8,128)S(1)} %bitcast.17), channel_id=1, source_target_pairs={{0,1},{1,0},{2,3},{3,2},{4,5},{5,4},{6,7},{7,6},{8,9},{9,8},{10,11... | collective-permute-start | bytes 786440 | tf_op jit(solution)/shard_map/ppermute | solution.py:54
  93.6 3.2 %collective-permute-done.7.refs_3_ = f32[2,384,128]{2,1,0:T(8,128)S(1)} collective-permute-done((f32[2,384,128]{2,1,0:T(8,128)}, f32[2,384,128]{2,1,0:T(8,128)S(1)}, u32[]{:S(2)}, u32[]{:S(2)}) %collective-permute-start.7) | collective-permute-done | bytes 393248 | tf_op jit(solution)/shard_map/ppermute | solution.py:34
  96.7 3.9 %shard_map.94 = (f32[576,128]{1,0:T(8,128)S(1)}, f32[576,128]{1,0:T(8,128)S(1)}, f32[2,2,256,256]{3,2,1,0:T(8,128)S(1)}, f32[2,256,256]{2,1,0:T(8,128)S(1)}) custom-call(s32[6]{0:T(128)S(1)} %pad_add_fusion.refs_0_.marks, f32[2,256,256]{2,1,0:T(8,128)S(1)} %get-tuple-element.37.tile.refs_1_, f32[2,128,256]{2,1,0:T(8,128)S(1)} %collective-permute-done.6.low.refs_2_, ...), custom_call_target="tpu_custom_call" | custom-call | tf_op jit(solution)/shard_map/pallas_call | solution.py:385
  102.4 3.5 %collective-permute-start.12 = (f32[576,128]{1,0:T(8,128)S(1)}, f32[576,128]{1,0:T(8,128)S(1)}, u32[]{:S(2)}, u32[]{:S(2)}) collective-permute-start(f32[576,128]{1,0:T(8,128)S(1)} %get-tuple-element.49), channel_id=1, source_target_pairs={{0,1},{1,0},{2,3},{3,2},{4,5},{5,4},{6,7},{7,6},{8,9},{9,8},{10,11... | collective-permute-start | bytes 884744 | tf_op jit(solution)/shard_map/ppermute | solution.py:54
  105.9 1.2 collective-permute-done.12
  107.1 18.3 %all_to_all.30 = f32[288,2,128]{2,1,0:T(2,128)S(1)} all-to-all(f32[288,2,128]{2,1,0:T(2,128)S(1)} %bitcast.24), channel_id=1, replica_groups={{0,2,4,6,64,66,68,70,128,130,132,134,192,194,196,198,256,258,260,262,32..., dimensions={0} | all-to-all | bytes 589824 | tf_op jit(solution)/shard_map/all_to_all | solution.py:60
  125.5 11.4 %all_to_all.31 = f32[72,2,128]{2,1,0:T(2,128)S(1)} all-to-all(f32[72,2,128]{2,1,0:T(2,128)S(1)} %bitcast.23), channel_id=1, replica_groups={{0,8,16,24,32,40,48,56},{1,9,17,25,33,41,49,57},{2,10,18,26,34,42,50,58..., dimensions={0} | all-to-all | bytes 147456 | tf_op jit(solution)/shard_map/all_to_all | solution.py:60
  137.6 9.2 %all-to-all-start.5 = ((f32[256,2,128]{2,1,0:T(2,128)}), f32[256,2,128]{2,1,0:T(2,128)S(1)}, u32[]{:S(2)}, u32[]{:S(2)}) async-start(f32[256,2,128]{2,1,0:T(2,128)} %bitcast.12), calls=%async_computation.5 | async-start | bytes 524288 | tf_op jit(solution)/shard_map/all_to_all | solution.py:60
  147.8 1.9 %collective-permute-start.10 = (f32[2,384,128]{2,1,0:T(8,128)S(1)}, f32[2,384,128]{2,1,0:T(8,128)S(1)}, u32[]{:S(2)}, u32[]{:S(2)}) collective-permute-start(f32[2,384,128]{2,1,0:T(8,128)S(1)} %get-tuple-element.45), channel_id=1, source_target_pairs={{0,1},{1,2},{2,3},{3,4},{4,5},{5,6},{6,7},{8,9},{9,10},{10,11},{11... | collective-permute-start | bytes 1179656 | tf_op jit(solution)/shard_map/ppermute | solution.py:34
  149.7 7.2 %collective-permute-done.10.from_left = f32[2,384,128]{2,1,0:T(8,128)S(1)} collective-permute-done((f32[2,384,128]{2,1,0:T(8,128)S(1)}, f32[2,384,128]{2,1,0:T(8,128)S(1)}, u32[]{:S(2)}, u32[]{:S(2)}) %collective-permute-start.10) | collective-permute-done | bytes 393248 | tf_op jit(solution)/shard_map/ppermute | solution.py:34
  156.9 2.5 %collective-permute-start.11 = (f32[2,128,256]{2,1,0:T(8,128)S(1)}, f32[2,128,256]{2,1,0:T(8,128)S(1)}, u32[]{:S(2)}, u32[]{:S(2)}) collective-permute-start(f32[2,128,256]{2,1,0:T(8,128)S(1)} %shard_map.96), channel_id=1, source_target_pairs={{0,8},{1,9},{2,10},{3,11},{4,12},{5,13},{6,14},{7,15},{8,16},{9,17... | collective-permute-start | bytes 786440 | tf_op jit(solution)/shard_map/ppermute | solution.py:34
  159.4 1.9 %collective-permute-start.13 = (f32[512,128]{1,0:T(8,128)S(1)}, f32[512,128]{1,0:T(8,128)S(1)}, u32[]{:S(2)}, u32[]{:S(2)}) collective-permute-start(f32[512,128]{1,0:T(8,128)S(1)} %bitcast.19), channel_id=1, source_target_pairs={{0,1},{1,0},{2,3},{3,2},{4,5},{5,4},{6,7},{7,6},{8,9},{9,8},{10,11... | collective-permute-start | bytes 786440 | tf_op jit(solution)/shard_map/ppermute | solution.py:54
  161.4 8.1 %collective-permute-done.11.from_above = f32[2,128,256]{2,1,0:T(8,128)S(1)} collective-permute-done((f32[2,128,256]{2,1,0:T(8,128)S(1)}, f32[2,128,256]{2,1,0:T(8,128)S(1)}, u32[]{:S(2)}, u32[]{:S(2)}) %collective-permute-start.11) | collective-permute-done | bytes 262176 | tf_op jit(solution)/shard_map/ppermute | solution.py:34
  170.7 1.7 shard_map.100
  (57 shorter events, 20.3 us)
Async XLA Ops:
  0.6 1.0 copy-start
  1.7 21.0 %copy-start.2 = (bf16[8,256,256]{2,1,0:T(8,128)(2,1)S(1)}, bf16[8,256,256]{2,1,0:T(8,128)(2,1)}, u32[]{:S(2)}) copy-start(bf16[8,256,256]{2,1,0:T(8,128)(2,1)} %constant.10.clone.refs_7_.refs_9_) | copy-start | bytes 3145732
  2.5 20.2 %collective-permute-start = (f32[2,128,256]{2,1,0:T(8,128)}, f32[2,128,256]{2,1,0:T(8,128)S(1)}, u32[]{:S(2)}, u32[]{:S(2)}) collective-permute-start(f32[2,128,256]{2,1,0:T(8,128)} %get-tuple-element.27), channel_id=1, source_target_pairs={{8,0},{9,1},{10,2},{11,3},{12,4},{13,5},{14,6},{15,7},{16,8},{17,9... | collective-permute-start | bytes 786440 | tf_op jit(solution)/shard_map/ppermute | solution.py:34
  13.3 9.4 %collective-permute-start.1 = (f32[2,256,128]{2,1,0:T(8,128)S(1)}, f32[2,256,128]{2,1,0:T(8,128)S(1)}, u32[]{:S(2)}, u32[]{:S(2)}) collective-permute-start(f32[2,256,128]{2,1,0:T(8,128)S(1)} %get-tuple-element.28), channel_id=1, source_target_pairs={{1,0},{2,1},{3,2},{4,3},{5,4},{6,5},{7,6},{9,8},{10,9},{11,10},{12... | collective-permute-start | bytes 786440 | tf_op jit(solution)/shard_map/ppermute | solution.py:34
  15.2 7.5 %collective-permute-start.2 = (f32[2,128,128]{2,1,0:T(8,128)}, f32[2,128,128]{2,1,0:T(8,128)S(1)}, u32[]{:S(2)}, u32[]{:S(2)}) collective-permute-start(f32[2,128,128]{2,1,0:T(8,128)} %get-tuple-element.29), channel_id=1, source_target_pairs={{9,0},{10,1},{11,2},{12,3},{13,4},{14,5},{15,6},{17,8},{18,9},{19,... | collective-permute-start | bytes 393224 | tf_op jit(solution)/shard_map/ppermute | solution.py:34
  19.2 1.0 copy-start.7
  20.2 1.0 copy-start.8
  21.3 0.9 copy-start.15
  22.2 1.0 copy-start.1
  26.8 1.0 copy-start.5
  27.8 3.8 %collective-permute-start.8 = (f32[576,128]{1,0:T(8,128)S(1)}, f32[576,128]{1,0:T(8,128)S(1)}, u32[]{:S(2)}, u32[]{:S(2)}) collective-permute-start(f32[576,128]{1,0:T(8,128)S(1)} %get-tuple-element.40), channel_id=1, source_target_pairs={{0,1},{1,0},{2,3},{3,2},{4,5},{5,4},{6,7},{7,6},{8,9},{9,8},{10,11... | collective-permute-start | bytes 884744 | tf_op jit(solution)/shard_map/ppermute | solution.py:54
  32.3 18.5 %all-to-all-start = ((f32[288,2,128]{2,1,0:T(2,128)}), f32[288,2,128]{2,1,0:T(2,128)S(1)}, u32[]{:S(2)}, u32[]{:S(2)}) async-start(f32[288,2,128]{2,1,0:T(2,128)} %bitcast.2), calls=%async_computation | async-start | bytes 589824 | tf_op jit(solution)/shard_map/all_to_all | solution.py:60
  41.9 1.2 copy-start.6
  44.9 30.2 %collective-permute-start.3 = (f32[2,256,128]{2,1,0:T(8,128)}, f32[2,256,128]{2,1,0:T(8,128)S(1)}, u32[]{:S(2)}, u32[]{:S(2)}) collective-permute-start(f32[2,256,128]{2,1,0:T(8,128)} %get-tuple-element.34), channel_id=1, source_target_pairs={{0,1},{1,2},{2,3},{3,4},{4,5},{5,6},{6,7},{8,9},{9,10},{10,11},{11... | collective-permute-start | bytes 786440 | tf_op jit(solution)/shard_map/ppermute | solution.py:34
  46.8 29.0 %collective-permute-start.4 = (f32[2,128,256]{2,1,0:T(8,128)}, f32[2,128,256]{2,1,0:T(8,128)S(1)}, u32[]{:S(2)}, u32[]{:S(2)}) collective-permute-start(f32[2,128,256]{2,1,0:T(8,128)} %get-tuple-element.35), channel_id=1, source_target_pairs={{0,8},{1,9},{2,10},{3,11},{4,12},{5,13},{6,14},{7,15},{8,16},{9,17... | collective-permute-start | bytes 786440 | tf_op jit(solution)/shard_map/ppermute | solution.py:34
  51.5 13.4 %all-to-all-start.1 = ((f32[72,2,128]{2,1,0:T(2,128)}), f32[72,2,128]{2,1,0:T(2,128)S(1)}, u32[]{:S(2)}, u32[]{:S(2)}) async-start(f32[72,2,128]{2,1,0:T(2,128)} %bitcast.4), calls=%async_computation.1 | async-start | bytes 147456 | tf_op jit(solution)/shard_map/all_to_all | solution.py:60
  56.1 19.1 %collective-permute-start.5 = (f32[2,128,128]{2,1,0:T(8,128)}, f32[2,128,128]{2,1,0:T(8,128)}, u32[]{:S(2)}, u32[]{:S(2)}) collective-permute-start(f32[2,128,128]{2,1,0:T(8,128)} %get-tuple-element.36), channel_id=1, source_target_pairs={{0,9},{1,10},{2,11},{3,12},{4,13},{5,14},{6,15},{8,17},{9,18},{10,... | collective-permute-start | bytes 393224 | tf_op jit(solution)/shard_map/ppermute | solution.py:34
  65.6 25.5 %all-to-all-start.2 = ((f32[256,2,128]{2,1,0:T(2,128)}), f32[256,2,128]{2,1,0:T(2,128)S(1)}, u32[]{:S(2)}, u32[]{:S(2)}) async-start(f32[256,2,128]{2,1,0:T(2,128)} %bitcast.6), calls=%async_computation.2 | async-start | bytes 524288 | tf_op jit(solution)/shard_map/all_to_all | solution.py:60
  76.6 0.9 copy-start.12
  77.5 0.9 copy-start.14
  79.4 9.0 %collective-permute-start.6 = (f32[2,128,256]{2,1,0:T(8,128)S(1)}, f32[2,128,256]{2,1,0:T(8,128)S(1)}, u32[]{:S(2)}, u32[]{:S(2)}) collective-permute-start(f32[2,128,256]{2,1,0:T(8,128)S(1)} %get-tuple-element.38), channel_id=1, source_target_pairs={{8,0},{9,1},{10,2},{11,3},{12,4},{13,5},{14,6},{15,7},{16,8},{17,9... | collective-permute-start | bytes 786440 | tf_op jit(solution)/shard_map/ppermute | solution.py:34
  89.2 7.5 %collective-permute-start.7 = (f32[2,384,128]{2,1,0:T(8,128)}, f32[2,384,128]{2,1,0:T(8,128)S(1)}, u32[]{:S(2)}, u32[]{:S(2)}) collective-permute-start(f32[2,384,128]{2,1,0:T(8,128)} %shard_map.91), channel_id=1, source_target_pairs={{1,0},{2,1},{3,2},{4,3},{5,4},{6,5},{7,6},{9,8},{10,9},{11,10},{12... | collective-permute-start | bytes 1179656 | tf_op jit(solution)/shard_map/ppermute | solution.py:34
  91.1 5.6 %collective-permute-start.9 = (f32[512,128]{1,0:T(8,128)S(1)}, f32[512,128]{1,0:T(8,128)S(1)}, u32[]{:S(2)}, u32[]{:S(2)}) collective-permute-start(f32[512,128]{1,0:T(8,128)S(1)} %bitcast.17), channel_id=1, source_target_pairs={{0,1},{1,0},{2,3},{3,2},{4,5},{5,4},{6,7},{7,6},{8,9},{9,8},{10,11... | collective-permute-start | bytes 786440 | tf_op jit(solution)/shard_map/ppermute | solution.py:54
  100.6 1.0 copy-start.3
  101.6 0.8 copy-start.9
  102.4 4.7 %collective-permute-start.12 = (f32[576,128]{1,0:T(8,128)S(1)}, f32[576,128]{1,0:T(8,128)S(1)}, u32[]{:S(2)}, u32[]{:S(2)}) collective-permute-start(f32[576,128]{1,0:T(8,128)S(1)} %get-tuple-element.49), channel_id=1, source_target_pairs={{0,1},{1,0},{2,3},{3,2},{4,5},{5,4},{6,7},{7,6},{8,9},{9,8},{10,11... | collective-permute-start | bytes 884744 | tf_op jit(solution)/shard_map/ppermute | solution.py:54
  107.1 39.7 %copy-start.4 = (f32[2,2,256,256]{3,2,1,0:T(8,128)S(1)}, f32[2,2,256,256]{3,2,1,0:T(8,128)}, u32[]{:S(2)}) copy-start(f32[2,2,256,256]{3,2,1,0:T(8,128)} %copy-done.3) | copy-start | bytes 3145732
  137.6 21.8 %all-to-all-start.5 = ((f32[256,2,128]{2,1,0:T(2,128)}), f32[256,2,128]{2,1,0:T(2,128)S(1)}, u32[]{:S(2)}, u32[]{:S(2)}) async-start(f32[256,2,128]{2,1,0:T(2,128)} %bitcast.12), calls=%async_computation.5 | async-start | bytes 524288 | tf_op jit(solution)/shard_map/all_to_all | solution.py:60
  147.8 9.1 %collective-permute-start.10 = (f32[2,384,128]{2,1,0:T(8,128)S(1)}, f32[2,384,128]{2,1,0:T(8,128)S(1)}, u32[]{:S(2)}, u32[]{:S(2)}) collective-permute-start(f32[2,384,128]{2,1,0:T(8,128)S(1)} %get-tuple-element.45), channel_id=1, source_target_pairs={{0,1},{1,2},{2,3},{3,4},{4,5},{5,6},{6,7},{8,9},{9,10},{10,11},{11... | collective-permute-start | bytes 1179656 | tf_op jit(solution)/shard_map/ppermute | solution.py:34
  156.9 12.5 %collective-permute-start.11 = (f32[2,128,256]{2,1,0:T(8,128)S(1)}, f32[2,128,256]{2,1,0:T(8,128)S(1)}, u32[]{:S(2)}, u32[]{:S(2)}) collective-permute-start(f32[2,128,256]{2,1,0:T(8,128)S(1)} %shard_map.96), channel_id=1, source_target_pairs={{0,8},{1,9},{2,10},{3,11},{4,12},{5,13},{6,14},{7,15},{8,16},{9,17... | collective-permute-start | bytes 786440 | tf_op jit(solution)/shard_map/ppermute | solution.py:34
  159.4 10.9 %collective-permute-start.13 = (f32[512,128]{1,0:T(8,128)S(1)}, f32[512,128]{1,0:T(8,128)S(1)}, u32[]{:S(2)}, u32[]{:S(2)}) collective-permute-start(f32[512,128]{1,0:T(8,128)S(1)} %bitcast.19), channel_id=1, source_target_pairs={{0,1},{1,0},{2,3},{3,2},{4,5},{5,4},{6,7},{7,6},{8,9},{9,8},{10,11... | collective-permute-start | bytes 786440 | tf_op jit(solution)/shard_map/ppermute | solution.py:54
  169.5 1.2 copy-start.10
  (2 other events, 1.4 us)
